TPU v7x, 32 devices: a whole 2x2x4 slice. The times are simulated.
32 devices in a mesh: wl: 4 (over x, core), row: 4 (over z), col: 2 (over y).
Axes of the slice: x: 2, y: 2, z: 4, core: 2. Of those that a mesh axis runs over, the one named last changes fastest.
Arguments:
- cotangent: bfloat16 [4, 2, 4096, 4096], P('wl', None, 'row', 'col'), may hold values from -6 to 6
- incident: bfloat16 [4, 4096, 4096], P('wl', 'row', 'col'), may hold values from 0.5 to 1.5
- aperture_tiles: int32 [32, 32], P('row', 'col'), may hold values 0 or 1
- charge: int32 [4], P('wl'), may hold values from 2 to 8
- wl_index: int32 [4], P('wl'), may hold values from 0 to 16
Outputs:
- gradient: bfloat16 [4096, 4096], P('row', 'col')
All inputs are finite; a program needn't handle non-finite values. No bound on the sum of `aperture_tiles` on one device may be relied on, other than what follows from the above.
Results may differ from a plain program's by a relative error of at most 0.013.
Values may be sent and summed in bfloat16 or wider, within the bound.
No kernel may reach another device: no remote copies, remote signals or barrier semaphores. Data moves between devices by JAX's collectives and lax.ppermute only.
A program may use at most 128 MiB of HBM per device.

v0:
```python
import math

import jax
import jax.numpy as jnp
from jax import lax
from jax.experimental import pallas as pl
from jax.experimental.pallas import tpu as pltpu
from jax.sharding import PartitionSpec as P


M = 512
HALF = M // 2
F32 = jnp.float32
BF16 = jnp.bfloat16


def iota(shape, axis):
    return lax.broadcasted_iota(jnp.int32, shape, axis).astype(F32)


def unit_phasor(product, period):
    turns = jnp.floor(product / period + 0.5)
    rest = product - turns * period
    quarter = jnp.floor(4.0 * rest / period + 0.5)
    theta = (4.0 * rest - quarter * period) / period * (0.5 * math.pi)
    sq = theta * theta
    sin_p = theta * (
        1.0 + sq * (-1.0 / 6.0 + sq * (1.0 / 120.0 + sq * (-1.0 / 5040.0 + sq / 362880.0)))
    )
    cos_p = 1.0 + sq * (
        -0.5 + sq * (1.0 / 24.0 + sq * (-1.0 / 720.0 + sq * (1.0 / 40320.0 - sq / 3628800.0)))
    )
    size = jnp.abs(quarter)
    odd = size == 1.0
    flip = jnp.where(size == 2.0, -1.0, 1.0)
    side = jnp.where(quarter < 0.0, -1.0, 1.0)
    cosine = jnp.where(odd, -side * sin_p, flip * cos_p)
    sine = jnp.where(odd, side * cos_p, flip * sin_p)
    return cosine, sine


def turn(first, second):
    c1, s1 = first
    c2, s2 = second
    return c1 * c2 - s1 * s2, s1 * c2 + c1 * s2


def quarter_period(index_value):
    return ((index_value + 32) * (M // 4)).astype(F32)


def table_focal_lanes(write, period, first, extent, amount, fine_ref, lanes=None, lane_count=HALF):
    block = 256
    focal = 2.0 * iota((16, lane_count), 1) + 1.0 if lanes is None else lanes
    step = iota((16, lane_count), 0)
    fine = unit_phasor(2.0 * step * focal, jnp.full((16, lane_count), period, F32))
    mid = unit_phasor(32.0 * step * focal, jnp.full((16, lane_count), period, F32))
    for b in range(16):
        re, im = turn((mid[0][b : b + 1], mid[1][b : b + 1]), fine)
        fine_ref[0, 16 * b : 16 * b + 16, :] = re
        fine_ref[1, 16 * b : 16 * b + 16, :] = im
    count = amount // block
    start = (2 * first - extent + 1).astype(F32)
    top = -(-count // 8) * 8
    focal_top = 2.0 * iota((top, lane_count), 1) + 1.0 if lanes is None else jnp.broadcast_to(lanes[:1], (top, lane_count))
    coarse = unit_phasor(
        (start + 2.0 * block * iota((top, lane_count), 0)) * focal_top,
        jnp.full((top, lane_count), period, F32),
    )
    for a in range(count):
        for part in range(0, block, 64):
            re, im = turn(
                (coarse[0][a : a + 1], coarse[1][a : a + 1]),
                (fine_ref[0, part : part + 64, :], fine_ref[1, part : part + 64, :]),
            )
            write(a * block + part, 64, re.astype(BF16), im.astype(BF16))


def table_pupil_lanes(write, period, first, extent, amount, fine_ref, focal_first, focal_count):
    count = amount // 128
    shape = (focal_count, 128)
    focal = 2.0 * (focal_first + iota(shape, 0)) + 1.0
    lane = iota(shape, 1)
    full = jnp.full(shape, period, F32)
    fine = unit_phasor(2.0 * lane * focal, full)
    fine_ref[0, :focal_count, :128] = fine[0]
    fine_ref[1, :focal_count, :128] = fine[1]
    start = (2 * first - extent + 1).astype(F32)
    coarse = unit_phasor((start + 256.0 * lane) * focal, full)
    fine_ref[0, :focal_count, 128:] = coarse[0]
    fine_ref[1, :focal_count, 128:] = coarse[1]
    for a in range(count):
        for part in range(0, focal_count, 64):
            rows = slice(part, min(part + 64, focal_count))
            re, im = turn(
                (fine_ref[0, rows, 128 + a : 129 + a], fine_ref[1, rows, 128 + a : 129 + a]),
                (fine_ref[0, rows, :128], fine_ref[1, rows, :128]),
            )
            write(part, a * 128, re.astype(BF16), im.astype(BF16))


def live_row(tiles_ref, tile_row, cells):
    tile_cols = tiles_ref.shape[1]
    width = cells // tile_cols
    parts = [
        jnp.full((1, width), jnp.where(tiles_ref[tile_row, j] == 1, 1.0, 0.0), F32)
        for j in range(tile_cols)
    ]
    return jnp.concatenate(parts, axis=1)


def forward_kernel(index_ref, charge_ref, tiles_ref, cot_ref, *refs, rows, cols, n_row, groups):
    outs, col_tab = refs[:-7], refs[-7]
    row_tab, inner, fine_ref, t_ref, held, sems = refs[-6:]
    block = min(256, rows)
    extent = rows * n_row
    row_at = lax.axis_index("row")
    col_at = lax.axis_index("col")
    tile_size = rows // tiles_ref.shape[0]
    copies = []
    for step in range(rows // block):
        span = pl.ds(step * block, block)
        copies.append(pltpu.make_async_copy(cot_ref.at[0, :, span, :], held.at[:, span, :], sems.at[step]))
        copies[-1].start()
    period = quarter_period(index_ref[0])

    def write_col(at, amount, re, im):
        col_tab[at : at + amount, :HALF] = re
        col_tab[at : at + amount, HALF:] = im

    table_focal_lanes(write_col, period, col_at * cols, extent, cols, fine_ref)

    def write_row(part, at, re, im):
        row_tab[part : part + 64, at : at + 128] = re
        row_tab[HALF + part : HALF + part + 64, at : at + 128] = im

    table_pupil_lanes(write_row, period, row_at * rows, extent, rows, fine_ref, 0.0, HALF)

    for step in range(rows // block):
        copies[step].wait()
        halves = []
        for part in range(2):
            for at in range(step * block, (step + 1) * block, tile_size):
                mask = live_row(tiles_ref, at // tile_size, cols).astype(BF16)
                halves.append(held[part, at : at + tile_size, :] * mask)
        prod = jnp.dot(jnp.concatenate(halves, axis=0), col_tab[...], preferred_element_type=F32)
        at = step * block
        inner[at : at + block, :M] = prod[:block].astype(BF16)
        inner[at : at + block, M:] = prod[block:].astype(BF16)

    charge = charge_ref[0]
    even = jnp.where(charge % 2 == 0, 1.0, 0.0).astype(F32)
    odd = 1.0 - even
    scale = 4.0 / (extent * M)
    chunk = 128
    shape = (chunk, HALF)
    for ub in range(HALF // chunk):
        both = jnp.concatenate(
            [row_tab[ub * chunk : (ub + 1) * chunk, :], row_tab[HALF + ub * chunk : HALF + (ub + 1) * chunk, :]],
            axis=0,
        )
        q = jnp.dot(both, inner[...], preferred_element_type=F32)
        q_c, q_s = q[:chunk], q[chunk:]
        u = 2.0 * (iota(shape, 0) + float(ub * chunk)) + 1.0
        v = 2.0 * iota(shape, 1) + 1.0
        inv = 1.0 / jnp.sqrt(u * u + v * v)
        power = (u * inv, v * inv)
        total = (jnp.full(shape, scale, F32), jnp.zeros(shape, F32))
        for bit in range(4):
            taken = (charge >> bit) % 2 == 1
            multiplied = turn(total, power)
            total = tuple(jnp.where(taken, new, old) for new, old in zip(multiplied, total))
            power = turn(power, power)
        c, s = total
        ce, se, co, so = c * even, s * even, c * odd, s * odd
        ca, cb, cc, cd = (q_c[:, k * HALF : (k + 1) * HALF] for k in range(4))
        sa, sb, sc, sd = (q_s[:, k * HALF : (k + 1) * HALF] for k in range(4))
        t_ee = ce * ca - se * sd + so * cb - co * sc
        t_eo = ce * cb + se * sc - so * ca - co * sd
        t_oe = ce * sa + se * cd + co * cc + so * sb
        t_oo = ce * sb - se * cc + co * cd - so * sa
        per = t_ref.shape[1]
        span = min(per, chunk)
        for j in range(chunk // span):
            rows_j = slice(j * span, (j + 1) * span)
            for first, left, right in (
                (ub * chunk + j * span, t_ee, t_eo),
                (HALF + ub * chunk + j * span, t_oe, t_oo),
            ):
                to = slice(first % per, first % per + span)
                t_ref[first // per, to, :HALF] = left[rows_j]
                t_ref[first // per, to, HALF:] = right[rows_j]
    for out, (ky, slots) in zip(outs, groups):
        for k, kz in enumerate(slots):
            source = (col_at ^ ky) * n_row + (row_at ^ kz)
            out[k] = t_ref[source].astype(BF16)


def forward(index, charge, tiles, cotangent, n_row, n_col, groups):
    rows, cols = cotangent.shape[2:]
    block = min(256, rows)
    per = M // (n_row * n_col)
    out_shape = [jax.ShapeDtypeStruct((len(slots), per, M), BF16) for _, slots in groups]
    out_shape.append(jax.ShapeDtypeStruct((cols, M), BF16))

    def kernel(*refs):
        forward_kernel(*refs, rows=rows, cols=cols, n_row=n_row, groups=groups)

    smem = pl.BlockSpec(memory_space=pltpu.SMEM)
    outs = pl.pallas_call(
        kernel,
        in_specs=[smem, smem, smem, pl.BlockSpec(memory_space=pltpu.HBM)],
        out_specs=[pl.BlockSpec(memory_space=pltpu.VMEM)] * len(out_shape),
        out_shape=out_shape,
        scratch_shapes=[
            pltpu.VMEM((M, rows), BF16),
            pltpu.VMEM((rows, 2 * M), BF16),
            pltpu.VMEM((2, HALF, HALF), F32),
            pltpu.VMEM((n_row * n_col, per, M), F32),
            pltpu.VMEM((2, rows, cols), BF16),
            pltpu.SemaphoreType.DMA((rows // block,)),
        ],
        compiler_params=pltpu.CompilerParams(vmem_limit_bytes=55 << 20),
        cost_estimate=pl.CostEstimate(
            flops=2 * rows * 2 * M * (cols + M), bytes_accessed=4 * rows * cols, transcendentals=0
        ),
        name="forward",
    )(index, charge, tiles, cotangent)
    return outs[:-1], outs[-1]


def swap(value, axis, bits):
    size = lax.axis_size(axis)
    return lax.ppermute(value, axis, [(i, i ^ bits) for i in range(size)])


def add_up(parts):
    total = parts[0].astype(F32)
    for part in parts[1:]:
        total = total + part.astype(F32)
    return total


def hop_order(n_row):
    return sorted(range(1, n_row), key=lambda k: -(k & -k))


def slot_groups(n_row, n_col):
    order = hop_order(n_row) + [0]
    if n_row <= 4:
        parts = [[kz] for kz in order]
    else:
        parts = [order[: n_row // 2], order[n_row // 2 :]]
    return [(ky, tuple(slots)) for slots in parts for ky in range(n_col)]


def reduce_blocks(parts, groups, n_row):
    reduced = {}
    for own, (ky, slots) in zip(parts, groups):
        if ky:
            continue
        terms = [own]
        for other, (step, other_slots) in zip(parts, groups):
            if step and other_slots == slots:
                terms.append(swap(other, "col", step))
        total = add_up(terms).astype(BF16)
        for k, kz in enumerate(slots):
            reduced[kz] = total[k]
    moved = [swap(reduced[kz], "row", kz) for kz in hop_order(n_row)]
    return add_up([reduced[0]] + moved).astype(BF16)


def gather_row(mine, n_row):
    found = {0: mine}
    for kz in hop_order(n_row):
        found[kz] = swap(mine, "row", kz)
    return [found[kz] for kz in range(n_row)]


def aligned(pieces):
    if any(piece.shape[0] % 16 for piece in pieces):
        return [jnp.concatenate(pieces, axis=0)]
    return pieces


def row_table_kernel(index_ref, row_tab, fine_ref, *, rows, n_row, n_col, full_rows, waves):
    extent = full_rows * n_row
    row_at = lax.axis_index("row")
    col_at = lax.axis_index("col")
    half_at = lax.rem(lax.axis_index("wl"), 2)
    per = M // (n_row * n_col)
    lane = lax.broadcasted_iota(jnp.int32, (16, M), 1)
    block = lane // per
    owner = ((block // n_row) ^ col_at) * n_row + ((block % n_row) ^ row_at)
    place = owner * per + lane % per
    is_sin = place >= HALF
    focal = 2.0 * jnp.where(is_sin, place - HALF, place).astype(F32) + 1.0
    for w in range(waves):
        period = quarter_period(index_ref[w])
        for side in range(2):
            lanes = slice(side * HALF, (side + 1) * HALF)
            sine = is_sin[:1, lanes]

            def write_row(at, amount, re, im, w=w, lanes=lanes, sine=sine):
                row_tab[w, at : at + amount, lanes] = jnp.where(
                    sine, im.astype(F32), re.astype(F32)
                ).astype(BF16)

            table_focal_lanes(
                write_row,
                period,
                row_at * full_rows + half_at * rows,
                extent,
                row_tab.shape[1],
                fine_ref,
                lanes=focal[:, lanes],
            )


def row_tables(indices, rows, n_row, n_col, full_rows):
    waves = indices.shape[0]
    own_rows = max(rows, 256)

    def kernel(*refs):
        row_table_kernel(*refs, rows=rows, n_row=n_row, n_col=n_col, full_rows=full_rows, waves=waves)

    return pl.pallas_call(
        kernel,
        in_specs=[pl.BlockSpec(memory_space=pltpu.SMEM)],
        out_specs=pl.BlockSpec(memory_space=pltpu.VMEM),
        out_shape=jax.ShapeDtypeStruct((waves, own_rows, M), BF16),
        scratch_shapes=[pltpu.VMEM((2, HALF, HALF), F32)],
        compiler_params=pltpu.CompilerParams(vmem_limit_bytes=16 << 20),
        cost_estimate=pl.CostEstimate(flops=40 * M * own_rows, bytes_accessed=4 * M * own_rows, transcendentals=0),
        name="row_tables",
    )(indices)


def col_table(index, cols, n_col):
    def kernel(index_ref, col_tab, fine_ref):
        def write_col(at, amount, re, im):
            col_tab[at : at + amount, :HALF] = re
            col_tab[at : at + amount, HALF:] = im

        table_focal_lanes(
            write_col,
            quarter_period(index_ref[0]),
            lax.axis_index("col") * cols,
            cols * n_col,
            cols,
            fine_ref,
        )

    return pl.pallas_call(
        kernel,
        in_specs=[pl.BlockSpec(memory_space=pltpu.SMEM)],
        out_specs=pl.BlockSpec(memory_space=pltpu.VMEM),
        out_shape=jax.ShapeDtypeStruct((cols, M), BF16),
        scratch_shapes=[pltpu.VMEM((2, HALF, HALF), F32)],
        compiler_params=pltpu.CompilerParams(vmem_limit_bytes=16 << 20),
        cost_estimate=pl.CostEstimate(flops=20 * M * cols, bytes_accessed=4 * M * cols, transcendentals=0),
        name="col_table",
    )(index)


def backward_kernel(tiles_ref, *refs, counts, wave_ids, part_first, chunks, tile_size, rows):
    waves = len(counts)
    total_pieces = sum(counts)
    sources, refs = refs[:total_pieces], refs[total_pieces:]
    row_tab, refs = refs[0], refs[1:]
    col_tabs, refs = refs[:waves], refs[waves:]
    incidents, refs = refs[:waves], refs[waves:]
    outs, refs = refs[: len(chunks)], refs[len(chunks) :]
    matrices, (held, sems) = list(refs[:-2]), refs[-2:]
    half_at = lax.rem(lax.axis_index("wl"), 2)
    first = chunks[0][0]
    copies = []
    for k, (at, amount) in enumerate(chunks):
        for w in range(waves):
            if part_first[w] is None:
                span = pl.ds(pl.multiple_of(half_at * rows + at, amount), amount)
                source = incidents[w].at[0, span, :]
            else:
                source = incidents[w].at[pl.ds(at - part_first[w], amount), :]
            copies.append(
                pltpu.make_async_copy(source, held.at[w, pl.ds(at - first, amount), :], sems.at[k, w])
            )
            copies[-1].start()
    ready = []
    for w in range(waves):
        pieces, sources = sources[: counts[w]], sources[counts[w] :]
        if counts[w] == 1:
            ready.append(pieces[0])
            continue
        target = matrices.pop(0)
        at = 0
        for piece in pieces:
            target[at : at + piece.shape[0], :] = piece[...]
            at += piece.shape[0]
        ready.append(target)
    cols = outs[0].shape[1]
    wide = min(512, cols)
    for k, (at, amount) in enumerate(chunks):
        back_y = [
            jnp.dot(row_tab[wave_ids[w], at : at + amount, :], ready[w][...], preferred_element_type=F32).astype(BF16)
            for w in range(waves)
        ]
        masks = [live_row(tiles_ref, (half_at * rows + at + h) // tile_size, cols) for h in range(0, amount, tile_size)]
        for w in range(waves):
            copies[k * waves + w].wait()
        for part in range(0, cols, wide):
            span = slice(part, part + wide)
            total = None
            for w in range(waves):
                back = lax.dot_general(
                    back_y[w], col_tabs[w][span, :], (((1,), (1,)), ((), ())), preferred_element_type=F32
                )
                term = back * held[w, at - first : at - first + amount, span].astype(F32)
                total = term if total is None else total + term
            for h, mask in enumerate(masks):
                some = slice(h * tile_size, min((h + 1) * tile_size, amount))
                outs[k][some, span] = (total[some] * mask[:, span]).astype(BF16)


def backward(tiles, waves, row_tab, chunks, tile_size, rows):
    cols = tiles.shape[1] * tile_size
    flat = [piece for wave in waves for piece in wave[0]]
    amount = sum(n for _, n in chunks)
    counts = [len(wave[0]) for wave in waves]
    emit = sum(count > 1 for count in counts)

    def kernel(*refs):
        backward_kernel(
            *refs,
            counts=counts,
            wave_ids=[wave[1] for wave in waves],
            part_first=[wave[4] for wave in waves],
            chunks=chunks,
            tile_size=tile_size,
            rows=rows,
        )

    vmem = pl.BlockSpec(memory_space=pltpu.VMEM)
    hbm = pl.BlockSpec(memory_space=pl.ANY)
    out_shape = [jax.ShapeDtypeStruct((n, cols), BF16) for _, n in chunks]
    out_shape += [jax.ShapeDtypeStruct((M, M), BF16)] * emit
    outs = pl.pallas_call(
        kernel,
        in_specs=[pl.BlockSpec(memory_space=pltpu.SMEM)]
        + [vmem] * (len(flat) + 1 + len(waves))
        + [hbm] * len(waves),
        out_specs=[vmem] * len(out_shape),
        out_shape=out_shape,
        scratch_shapes=[
            pltpu.VMEM((len(waves), amount, cols), BF16),
            pltpu.SemaphoreType.DMA((len(chunks), len(waves))),
        ],
        compiler_params=pltpu.CompilerParams(vmem_limit_bytes=24 << 20),
        cost_estimate=pl.CostEstimate(
            flops=2 * len(waves) * amount * M * (cols + M), bytes_accessed=6 * amount * cols, transcendentals=0
        ),
    )(tiles, *flat, row_tab, *[wave[2] for wave in waves], *[wave[3] for wave in waves])
    return outs[: len(chunks)], outs[len(chunks) :]


def place_kernel(*refs, chunks, rows):
    sources = refs[: 2 * len(chunks)]
    out, sems = refs[-2:]
    half_at = lax.rem(lax.axis_index("wl"), 2)
    copies = []
    for k, (at, amount) in enumerate(chunks):
        for side in range(2):
            where = half_at if side == 0 else 1 - half_at
            target = out.at[pl.ds(pl.multiple_of(where * rows + at, amount), amount), :]
            copies.append(pltpu.make_async_copy(sources[2 * k + side], target, sems.at[k, side]))
    for copy in copies:
        copy.start()
    for copy in copies:
        copy.wait()


def place(done, chunks, rows, into=None):
    flat = [part for pair in done for part in pair]
    cols = flat[0].shape[1]
    operands = flat + ([into] if into is not None else [])

    def kernel(*refs):
        place_kernel(*refs, chunks=chunks, rows=rows)

    hbm = pl.BlockSpec(memory_space=pl.ANY)
    return pl.pallas_call(
        kernel,
        in_specs=[hbm] * len(operands),
        out_specs=hbm,
        out_shape=jax.ShapeDtypeStruct((2 * rows, cols), BF16),
        scratch_shapes=[pltpu.SemaphoreType.DMA((len(chunks), 2))],
        input_output_aliases={len(flat): 0} if into is not None else {},
        compiler_params=pltpu.CompilerParams(vmem_limit_bytes=1 << 20),
        cost_estimate=pl.CostEstimate(flops=0, bytes_accessed=4 * cols * sum(n for _, n in chunks), transcendentals=0),
    )(*operands)


EXCHANGED = (2, 1, 1)
REPEATED = (2, 2)


def all_steps(cotangent, incident, tiles, charge, wl_index):
    rows, cols = cotangent.shape[2:]
    n_row = lax.axis_size("row")
    n_col = lax.axis_size("col")
    tile_size = rows // tiles.shape[0]
    half = rows // 2
    core = lax.axis_index("wl") % 2
    unit = half // 8
    chunks = []
    at = 0
    for size in EXCHANGED + REPEATED:
        chunks.append((at, size * unit))
        at += size * unit
    n_first = len(EXCHANGED)
    split = chunks[n_first][0]

    def rows_for(which):
        return lax.dynamic_slice_in_dim(incident[0], which * half + split, half - split, 0)

    inc_straight = swap(rows_for(core), "wl", 2)
    inc_core = swap(incident, "wl", 1)
    groups = slot_groups(n_row, n_col)
    parts, col_own = forward(wl_index, charge, tiles, cotangent, n_row, n_col, groups)
    mine = reduce_blocks(parts, groups, n_row)
    inc_cross = swap(rows_for(1 - core), "wl", 3)
    col_core = swap(col_own, "wl", 1)
    indices = jnp.concatenate([wl_index, swap(wl_index, "wl", 2)])
    indices = jnp.concatenate([indices, swap(indices, "wl", 1)])
    row_tab = row_tables(indices, half, n_row, n_col, rows)
    col_straight = col_table(indices[1:2], cols, n_col)
    col_cross = swap(col_straight, "wl", 1)

    here = gather_row(mine, n_row)
    if n_row > 4:
        here = [jnp.concatenate(here, axis=0)]
    joined = jnp.concatenate(here, axis=0)
    pieces, pieces_core = [joined], [swap(joined, "wl", 1)]
    for ky in range(1, n_col):
        for piece in here:
            pieces.append(swap(piece, "col", ky))
            pieces_core.append(swap(pieces[-1], "wl", 1))

    far = swap(mine, "wl", 2)
    far = jnp.concatenate(gather_row(far, n_row), axis=0)
    far = jnp.concatenate([far] + [swap(far, "col", ky) for ky in range(1, n_col)], axis=0)
    far_core = swap(far, "wl", 1)

    own = (aligned(pieces), 0, col_own, incident, None)
    mate = (aligned(pieces_core), 2, col_core, inc_core, None)
    first, matrices = backward(tiles, [own, mate], row_tab, chunks[:1], tile_size, half)
    if len(matrices) == 2:
        own = ([matrices[0]],) + own[1:]
        mate = ([matrices[1]],) + mate[1:]
    second, _ = backward(tiles, [own, mate], row_tab, chunks[1:n_first], tile_size, half)
    straight = ([far], 1, col_straight, inc_straight, split)
    cross = ([far_core], 3, col_cross, inc_cross, split)
    both, _ = backward(tiles, [own, mate, straight, cross], row_tab, chunks[n_first:], tile_size, half)
    done = []
    for pair in list(first) + list(second):
        total = add_up([pair, swap(pair, "wl", 2)]).astype(BF16)
        done.append((total, swap(total, "wl", 1)))
    ready = [(part, swap(part, "wl", 1)) for part in both]
    result = place(ready, chunks[n_first:], half)
    result = place(done[:-1], chunks[: n_first - 1], half, result)
    return place(done[-1:], chunks[n_first - 1 : n_first], half, result)


def solution(mesh):
    return jax.shard_map(
        all_steps,
        mesh=mesh,
        in_specs=(
            P("wl", None, "row", "col"),
            P("wl", "row", "col"),
            P("row", "col"),
            P("wl"),
            P("wl"),
        ),
        out_specs=P("row", "col"),
        check_vma=False,
    )
```

profile of v0, /device:TPU:0, one launch (start us, length us, event | category | flops | bytes accessed | tf_op | source)
XLA Modules:
  0.0 147.1 jit_solution(12568822451791576305)
XLA Ops:
  1.8 10.2 %forward.1 = (bf16[1,64,512]{2,1,0:T(8,128)(2,1)}, bf16[1,64,512]{2,1,0:T(8,128)(2,1)}, bf16[1,64,512]{2,1,0:T(8,128)(2,1)}, bf16[1,64,512]{2,1,0:T(8,128)(2,1)}...) custom-call(s32[1]{0:T(128)S(6)} %copy.15.refs_0_, ...), custom_call_target="tpu_custom_call" | custom-call | flops 5368709120 | bytes 8388608 | tf_op jit(solution)/shard_map/forward/pallas_call | solution.py:210
  12.0 2.6 %collective-permute-start.1 = (bf16[1,64,512]{2,1,0:T(8,128)(2,1)}, bf16[1,64,512]{2,1,0:T(8,128)(2,1)S(1)}, u32[]{:S(2)}, u32[]{:S(2)}) collective-permute-start(bf16[1,64,512]{2,1,0:T(8,128)(2,1)} %get-tuple-element.24), channel_id=1, source_target_pairs={{0,1},{1,0},{2,3},{3,2},{4,5},{5,4},{6,7},{7,6},{8,9},{9,8},{10,11... | collective-permute-start | bytes 196616 | tf_op jit(solution)/shard_map/ppermute | solution.py:234
  14.6 1.5 %collective-permute-start.19 = (s32[1]{0:T(128)}, s32[1]{0:T(128)}, u32[]{:S(2)}, u32[]{:S(2)}) collective-permute-start(s32[1]{0:T(128)} %param.9), channel_id=1, source_target_pairs={{0,16},{8,24},{16,0},{24,8},{1,17},{9,25},{17,1},{25,9},{2,18},{10... | collective-permute-start | bytes 20 | tf_op jit(solution)/shard_map/ppermute | solution.py:234
  16.6 1.5 %collective-permute-start.3 = (bf16[1,64,512]{2,1,0:T(8,128)(2,1)}, bf16[1,64,512]{2,1,0:T(8,128)(2,1)S(1)}, u32[]{:S(2)}, u32[]{:S(2)}) collective-permute-start(bf16[1,64,512]{2,1,0:T(8,128)(2,1)} %get-tuple-element.26), channel_id=1, source_target_pairs={{0,1},{1,0},{2,3},{3,2},{4,5},{5,4},{6,7},{7,6},{8,9},{9,8},{10,11... | collective-permute-start | bytes 196616 | tf_op jit(solution)/shard_map/ppermute | solution.py:234
  20.2 2.2 %collective-permute-done.3 = bf16[1,64,512]{2,1,0:T(8,128)(2,1)S(1)} collective-permute-done((bf16[1,64,512]{2,1,0:T(8,128)(2,1)}, bf16[1,64,512]{2,1,0:T(8,128)(2,1)S(1)}, u32[]{:S(2)}, u32[]{:S(2)}) %collective-permute-start.3) | collective-permute-done | bytes 65568 | tf_op jit(solution)/shard_map/ppermute | solution.py:234
  23.2 2.7 %collective-permute-start.2 = (bf16[64,512]{1,0:T(8,128)(2,1)S(1)}, bf16[64,512]{1,0:T(8,128)(2,1)S(1)}, u32[]{:S(2)}, u32[]{:S(2)}) collective-permute-start(bf16[64,512]{1,0:T(8,128)(2,1)S(1)} %fusion.4), channel_id=1, source_target_pairs={{0,4},{2,6},{4,0},{6,2},{1,5},{3,7},{5,1},{7,3},{8,12},{10,14},{12... | collective-permute-start | bytes 196616 | tf_op jit(solution)/shard_map/ppermute | solution.py:234
  26.8 1.6 %collective-permute-start.4 = (bf16[64,512]{1,0:T(8,128)(2,1)S(1)}, bf16[64,512]{1,0:T(8,128)(2,1)S(1)}, u32[]{:S(2)}, u32[]{:S(2)}) collective-permute-start(bf16[64,512]{1,0:T(8,128)(2,1)S(1)} %fusion.5), channel_id=1, source_target_pairs={{0,2},{2,0},{4,6},{6,4},{1,3},{3,1},{5,7},{7,5},{8,10},{10,8},{12,... | collective-permute-start | bytes 196616 | tf_op jit(solution)/shard_map/ppermute | solution.py:234
  28.6 2.6 %col_table.1.refs_8_ = bf16[2048,512]{1,0:T(8,128)(2,1)} custom-call(s32[1]{0:T(128)} %collective-permute-done.19.index_ref), custom_call_target="tpu_custom_call" | custom-call | flops 20971520 | bytes 4194304 | tf_op jit(solution)/shard_map/col_table/pallas_call | solution.py:354
  31.3 3.2 %collective-permute-done.6 = bf16[64,512]{1,0:T(8,128)(2,1)S(1)} collective-permute-done((bf16[64,512]{1,0:T(8,128)(2,1)S(1)}, bf16[64,512]{1,0:T(8,128)(2,1)S(1)}, u32[]{:S(2)}, u32[]{:S(2)}) %collective-permute-start.6) | collective-permute-done | bytes 65568 | tf_op jit(solution)/shard_map/ppermute | solution.py:234
  37.7 2.0 %collective-permute-start.10 = (bf16[64,512]{1,0:T(8,128)(2,1)S(1)}, bf16[64,512]{1,0:T(8,128)(2,1)S(1)}, u32[]{:S(2)}, u32[]{:S(2)}) collective-permute-start(bf16[64,512]{1,0:T(8,128)(2,1)S(1)} %fusion.2), channel_id=1, source_target_pairs={{0,1},{1,0},{2,3},{3,2},{4,5},{5,4},{6,7},{7,6},{8,9},{9,8},{10,11... | collective-permute-start | bytes 196616 | tf_op jit(solution)/shard_map/ppermute | solution.py:234
  39.7 1.4 collective-permute-start.9
  42.8 3.3 %collective-permute-done.9 = bf16[64,512]{1,0:T(8,128)(2,1)S(1)} collective-permute-done((bf16[64,512]{1,0:T(8,128)(2,1)S(1)}, bf16[64,512]{1,0:T(8,128)(2,1)S(1)}, u32[]{:S(2)}, u32[]{:S(2)}) %collective-permute-start.9) | collective-permute-done | bytes 65568 | tf_op jit(solution)/shard_map/ppermute | solution.py:234
  46.2 2.1 %collective-permute-done.8 = bf16[64,512]{1,0:T(8,128)(2,1)S(1)} collective-permute-done((bf16[64,512]{1,0:T(8,128)(2,1)S(1)}, bf16[64,512]{1,0:T(8,128)(2,1)S(1)}, u32[]{:S(2)}, u32[]{:S(2)}) %collective-permute-start.8) | collective-permute-done | bytes 65568 | tf_op jit(solution)/shard_map/ppermute | solution.py:234
  48.3 1.6 %collective-permute-start.32 = (bf16[64,512]{1,0:T(8,128)(2,1)S(1)}, bf16[64,512]{1,0:T(8,128)(2,1)S(1)}, u32[]{:S(2)}, u32[]{:S(2)}) collective-permute-start(bf16[64,512]{1,0:T(8,128)(2,1)S(1)} %collective-permute-done.29), channel_id=1, source_target_pairs={{0,6},{2,4},{4,2},{6,0},{1,7},{3,5},{5,3},{7,1},{8,14},{10,12},{12... | collective-permute-start | bytes 196616 | tf_op jit(solution)/shard_map/ppermute | solution.py:234
  50.6 4.1 %collective-permute-done.32 = bf16[64,512]{1,0:T(8,128)(2,1)S(1)} collective-permute-done((bf16[64,512]{1,0:T(8,128)(2,1)S(1)}, bf16[64,512]{1,0:T(8,128)(2,1)S(1)}, u32[]{:S(2)}, u32[]{:S(2)}) %collective-permute-start.32) | collective-permute-done | bytes 65568 | tf_op jit(solution)/shard_map/ppermute | solution.py:234
  54.8 2.1 %collective-permute-done.31 = bf16[64,512]{1,0:T(8,128)(2,1)S(1)} collective-permute-done((bf16[64,512]{1,0:T(8,128)(2,1)S(1)}, bf16[64,512]{1,0:T(8,128)(2,1)S(1)}, u32[]{:S(2)}, u32[]{:S(2)}) %collective-permute-start.31) | collective-permute-done | bytes 65568 | tf_op jit(solution)/shard_map/ppermute | solution.py:234
  56.9 2.2 %collective-permute-done.30 = bf16[64,512]{1,0:T(8,128)(2,1)S(1)} collective-permute-done((bf16[64,512]{1,0:T(8,128)(2,1)S(1)}, bf16[64,512]{1,0:T(8,128)(2,1)S(1)}, u32[]{:S(2)}, u32[]{:S(2)}) %collective-permute-start.30) | collective-permute-done | bytes 65568 | tf_op jit(solution)/shard_map/ppermute | solution.py:234
  61.1 2.4 %collective-permute-done.13.refs_5_ = bf16[64,512]{1,0:T(8,128)(2,1)S(1)} collective-permute-done((bf16[64,512]{1,0:T(8,128)(2,1)S(1)}, bf16[64,512]{1,0:T(8,128)(2,1)S(1)}, u32[]{:S(2)}, u32[]{:S(2)}) %collective-permute-start.13) | collective-permute-done | bytes 65568 | tf_op jit(solution)/shard_map/ppermute | solution.py:234
  63.5 1.3 collective-permute-start.11
  64.8 2.9 %collective-permute-done.11.refs_3_ = bf16[64,512]{1,0:T(8,128)(2,1)S(1)} collective-permute-done((bf16[64,512]{1,0:T(8,128)(2,1)S(1)}, bf16[64,512]{1,0:T(8,128)(2,1)S(1)}, u32[]{:S(2)}, u32[]{:S(2)}) %collective-permute-start.11) | collective-permute-done | bytes 65568 | tf_op jit(solution)/shard_map/ppermute | solution.py:234
  69.2 1.3 collective-permute-start.33
  70.5 1.8 %dynamic-slice_bitcast_fusion = (bf16[256,2048]{1,0:T(8,128)(2,1)S(1)}, bf16[256,2048]{1,0:T(8,128)(2,1)S(1)}) fusion(bf16[1,1024,2048]{2,1,0:T(8,128)(2,1)} %refs_10_.1, s32[]{:T(128)S(6)} %select_n.15, s32[]{:T(128)S(6)} %select_n.14), kind=kLoop, calls=%fused_computation | loop fusion | bytes 4194312 | tf_op jit(solution)/shard_map/dynamic_slice | solution.py:524
  72.3 5.4 %collective-permute-done.33 = bf16[256,512]{1,0:T(8,128)(2,1)S(1)} collective-permute-done((bf16[256,512]{1,0:T(8,128)(2,1)S(1)}, bf16[256,512]{1,0:T(8,128)(2,1)S(1)}, u32[]{:S(2)}, u32[]{:S(2)}) %collective-permute-start.33) | collective-permute-done | bytes 262176 | tf_op jit(solution)/shard_map/ppermute | solution.py:234
  78.8 2.6 %row_tables.1.refs_11_.refs_3_.refs_5_ = bf16[4,512,512]{2,1,0:T(8,128)(2,1)S(1)} custom-call(s32[4]{0:T(128)S(1)} %pad_add_fusion.1.refs_0_), custom_call_target="tpu_custom_call" | custom-call | flops 10485760 | bytes 1048576 | tf_op jit(solution)/shard_map/row_tables/pallas_call | solution.py:327
  81.5 3.5 %shard_map.55 = (bf16[128,2048]{1,0:T(8,128)(2,1)S(1)}, bf16[512,512]{1,0:T(8,128)(2,1)S(1)}, bf16[512,512]{1,0:T(8,128)(2,1)S(1)}) custom-call(s32[8,16]{1,0:T(8,128)S(1)} %copy-done.2, bf16[256,512]{1,0:T(8,128)(2,1)S(1)} %pad_maximum_fusion.refs_1_, bf16[64,512]{1,0:T(8,128)(2,1)S(1)} %collective-permute-done.10.refs_2_, ...), custom_call_target="tpu_custom_call" | custom-call | flops 671088640 | bytes 1572864 | tf_op jit(solution)/shard_map/pallas_call | solution.py:447
  85.0 4.6 %shard_map.56 = (bf16[64,2048]{1,0:T(8,128)(2,1)S(1)}, bf16[64,2048]{1,0:T(8,128)(2,1)S(1)}) custom-call(s32[8,16]{1,0:T(8,128)S(1)} %copy-done.2, bf16[512,512]{1,0:T(8,128)(2,1)S(1)} %get-tuple-element.30.refs_1_, bf16[512,512]{1,0:T(8,128)(2,1)S(1)} %get-tuple-element.31.refs_2_, bf16[4,512,512]{2,1,0:T(8,128)(2,1)S(1)} %row_tables.1.refs_11_.refs_3_.refs_5_, ...), custom_call_target="tpu_custom_call" | custom-call | flops 671088640 | bytes 1572864 | tf_op jit(solution)/shard_map/pallas_call | solution.py:447
  89.5 1.8 %collective-permute-start.27 = (bf16[64,2048]{1,0:T(8,128)(2,1)S(1)}, bf16[64,2048]{1,0:T(8,128)(2,1)S(1)}, u32[]{:S(2)}, u32[]{:S(2)}) collective-permute-start(bf16[64,2048]{1,0:T(8,128)(2,1)S(1)} %get-tuple-element.34), channel_id=1, source_target_pairs={{0,16},{8,24},{16,0},{24,8},{1,17},{9,25},{17,1},{25,9},{2,18},{10... | collective-permute-start | bytes 786440 | tf_op jit(solution)/shard_map/ppermute | solution.py:234
  91.4 6.2 %collective-permute-done.37.refs_13_ = bf16[256,2048]{1,0:T(8,128)(2,1)S(1)} collective-permute-done((bf16[256,2048]{1,0:T(8,128)(2,1)S(1)}, bf16[256,2048]{1,0:T(8,128)(2,1)S(1)}, u32[]{:S(2)}, u32[]{:S(2)}) %collective-permute-start.37) | collective-permute-done | bytes 1048608 | tf_op jit(solution)/shard_map/ppermute | solution.py:234
  97.6 22.9 %collective-permute-done.36.refs_12_ = bf16[256,2048]{1,0:T(8,128)(2,1)S(1)} collective-permute-done((bf16[256,2048]{1,0:T(8,128)(2,1)S(1)}, bf16[256,2048]{1,0:T(8,128)(2,1)S(1)}, u32[]{:S(2)}, u32[]{:S(2)}) %collective-permute-start.36) | collective-permute-done | bytes 1048608 | tf_op jit(solution)/shard_map/ppermute | solution.py:234
  120.8 9.3 %shard_map.57 = (bf16[128,2048]{1,0:T(8,128)(2,1)S(1)}, bf16[128,2048]{1,0:T(8,128)(2,1)S(1)}) custom-call(s32[8,16]{1,0:T(8,128)S(1)} %copy-done.2, bf16[512,512]{1,0:T(8,128)(2,1)S(1)} %get-tuple-element.30.refs_1_, bf16[512,512]{1,0:T(8,128)(2,1)S(1)} %get-tuple-element.31.refs_2_, bf16[512,512]{1,0:T(8,128)(2,1)S(1)} %constant_dynamic-update-slice_fusion.refs_3_, ...), custom_call_target="tpu_custom_call" | custom-call | flops 2684354560 | bytes 3145728 | tf_op jit(solution)/shard_map/pallas_call | solution.py:447
  131.0 11.8 %collective-permute-done.25 = bf16[128,2048]{1,0:T(8,128)(2,1)S(1)} collective-permute-done((bf16[128,2048]{1,0:T(8,128)(2,1)S(1)}, bf16[128,2048]{1,0:T(8,128)(2,1)S(1)}, u32[]{:S(2)}, u32[]{:S(2)}) %collective-permute-start.25) | collective-permute-done | bytes 524320 | tf_op jit(solution)/shard_map/ppermute | solution.py:234
  143.6 1.3 shard_map.58.refs_4_
  (80 shorter events, 19.5 us)
Async XLA Ops:
  0.0 81.4 %collective-permute-start.22 = (bf16[1,1024,2048]{2,1,0:T(8,128)(2,1)}, bf16[1,1024,2048]{2,1,0:T(8,128)(2,1)}, u32[]{:S(2)}, u32[]{:S(2)}) collective-permute-start(bf16[1,1024,2048]{2,1,0:T(8,128)(2,1)} %refs_10_.1), channel_id=1, source_target_pairs={{0,8},{8,0},{16,24},{24,16},{1,9},{9,1},{17,25},{25,17},{2,10},{10... | collective-permute-start | bytes 12582920 | tf_op jit(solution)/shard_map/ppermute | solution.py:234
  12.0 6.1 %collective-permute-start.1 = (bf16[1,64,512]{2,1,0:T(8,128)(2,1)}, bf16[1,64,512]{2,1,0:T(8,128)(2,1)S(1)}, u32[]{:S(2)}, u32[]{:S(2)}) collective-permute-start(bf16[1,64,512]{2,1,0:T(8,128)(2,1)} %get-tuple-element.24), channel_id=1, source_target_pairs={{0,1},{1,0},{2,3},{3,2},{4,5},{5,4},{6,7},{7,6},{8,9},{9,8},{10,11... | collective-permute-start | bytes 196616 | tf_op jit(solution)/shard_map/ppermute | solution.py:234
  14.6 12.1 %collective-permute-start.19 = (s32[1]{0:T(128)}, s32[1]{0:T(128)}, u32[]{:S(2)}, u32[]{:S(2)}) collective-permute-start(s32[1]{0:T(128)} %param.9), channel_id=1, source_target_pairs={{0,16},{8,24},{16,0},{24,8},{1,17},{9,25},{17,1},{25,9},{2,18},{10... | collective-permute-start | bytes 20 | tf_op jit(solution)/shard_map/ppermute | solution.py:234
  16.1 12.3 %collective-permute-start = (bf16[1,64,512]{2,1,0:T(8,128)(2,1)}, bf16[1,64,512]{2,1,0:T(8,128)(2,1)S(1)}, u32[]{:S(2)}, u32[]{:S(2)}) collective-permute-start(bf16[1,64,512]{2,1,0:T(8,128)(2,1)} %get-tuple-element.22), channel_id=1, source_target_pairs={{0,1},{1,0},{2,3},{3,2},{4,5},{5,4},{6,7},{7,6},{8,9},{9,8},{10,11... | collective-permute-start | bytes 196616 | tf_op jit(solution)/shard_map/ppermute | solution.py:234
  16.6 5.8 %collective-permute-start.3 = (bf16[1,64,512]{2,1,0:T(8,128)(2,1)}, bf16[1,64,512]{2,1,0:T(8,128)(2,1)S(1)}, u32[]{:S(2)}, u32[]{:S(2)}) collective-permute-start(bf16[1,64,512]{2,1,0:T(8,128)(2,1)} %get-tuple-element.26), channel_id=1, source_target_pairs={{0,1},{1,0},{2,3},{3,2},{4,5},{5,4},{6,7},{7,6},{8,9},{9,8},{10,11... | collective-permute-start | bytes 196616 | tf_op jit(solution)/shard_map/ppermute | solution.py:234
  18.1 5.1 %collective-permute-start.5 = (bf16[1,64,512]{2,1,0:T(8,128)(2,1)}, bf16[1,64,512]{2,1,0:T(8,128)(2,1)S(1)}, u32[]{:S(2)}, u32[]{:S(2)}) collective-permute-start(bf16[1,64,512]{2,1,0:T(8,128)(2,1)} %get-tuple-element.28), channel_id=1, source_target_pairs={{0,1},{1,0},{2,3},{3,2},{4,5},{5,4},{6,7},{7,6},{8,9},{9,8},{10,11... | collective-permute-start | bytes 196616 | tf_op jit(solution)/shard_map/ppermute | solution.py:234
  22.3 55.7 %collective-permute-start.21 = (bf16[2048,512]{1,0:T(8,128)(2,1)}, bf16[2048,512]{1,0:T(8,128)(2,1)S(1)}, u32[]{:S(2)}, u32[]{:S(2)}) collective-permute-start(bf16[2048,512]{1,0:T(8,128)(2,1)} %get-tuple-element.29.refs_12_.refs_4_.refs_6_), channel_id=1, source_target_pairs={{0,8},{8,0},{16,24},{24,16},{1,9},{9,1},{17,25},{25,17},{2,10},{10... | collective-permute-start | bytes 6291464 | tf_op jit(solution)/shard_map/ppermute | solution.py:234
  23.2 8.0 %collective-permute-start.2 = (bf16[64,512]{1,0:T(8,128)(2,1)S(1)}, bf16[64,512]{1,0:T(8,128)(2,1)S(1)}, u32[]{:S(2)}, u32[]{:S(2)}) collective-permute-start(bf16[64,512]{1,0:T(8,128)(2,1)S(1)} %fusion.4), channel_id=1, source_target_pairs={{0,4},{2,6},{4,0},{6,2},{1,5},{3,7},{5,1},{7,3},{8,12},{10,14},{12... | collective-permute-start | bytes 196616 | tf_op jit(solution)/shard_map/ppermute | solution.py:234
  26.8 4.5 %collective-permute-start.4 = (bf16[64,512]{1,0:T(8,128)(2,1)S(1)}, bf16[64,512]{1,0:T(8,128)(2,1)S(1)}, u32[]{:S(2)}, u32[]{:S(2)}) collective-permute-start(bf16[64,512]{1,0:T(8,128)(2,1)S(1)} %fusion.5), channel_id=1, source_target_pairs={{0,2},{2,0},{4,6},{6,4},{1,3},{3,1},{5,7},{7,5},{8,10},{10,8},{12,... | collective-permute-start | bytes 196616 | tf_op jit(solution)/shard_map/ppermute | solution.py:234
  28.4 6.1 %collective-permute-start.6 = (bf16[64,512]{1,0:T(8,128)(2,1)S(1)}, bf16[64,512]{1,0:T(8,128)(2,1)S(1)}, u32[]{:S(2)}, u32[]{:S(2)}) collective-permute-start(bf16[64,512]{1,0:T(8,128)(2,1)S(1)} %fusion.6), channel_id=1, source_target_pairs={{0,6},{2,4},{4,2},{6,0},{1,7},{3,5},{5,3},{7,1},{8,14},{10,12},{12... | collective-permute-start | bytes 196616 | tf_op jit(solution)/shard_map/ppermute | solution.py:234
  31.2 89.7 %collective-permute-start.35 = (bf16[2048,512]{1,0:T(8,128)(2,1)}, bf16[2048,512]{1,0:T(8,128)(2,1)}, u32[]{:S(2)}, u32[]{:S(2)}) collective-permute-start(bf16[2048,512]{1,0:T(8,128)(2,1)} %col_table.1.refs_8_), channel_id=1, source_target_pairs={{0,8},{8,0},{16,24},{24,16},{1,9},{9,1},{17,25},{25,17},{2,10},{10... | collective-permute-start | bytes 6291464 | tf_op jit(solution)/shard_map/ppermute | solution.py:234
  35.3 4.3 %collective-permute-start.29 = (bf16[64,512]{1,0:T(8,128)(2,1)S(1)}, bf16[64,512]{1,0:T(8,128)(2,1)S(1)}, u32[]{:S(2)}, u32[]{:S(2)}) collective-permute-start(bf16[64,512]{1,0:T(8,128)(2,1)S(1)} %fusion.2), channel_id=1, source_target_pairs={{0,16},{8,24},{16,0},{24,8},{1,17},{9,25},{17,1},{25,9},{2,18},{10... | collective-permute-start | bytes 196616 | tf_op jit(solution)/shard_map/ppermute | solution.py:234
  37.7 4.4 %collective-permute-start.10 = (bf16[64,512]{1,0:T(8,128)(2,1)S(1)}, bf16[64,512]{1,0:T(8,128)(2,1)S(1)}, u32[]{:S(2)}, u32[]{:S(2)}) collective-permute-start(bf16[64,512]{1,0:T(8,128)(2,1)S(1)} %fusion.2), channel_id=1, source_target_pairs={{0,1},{1,0},{2,3},{3,2},{4,5},{5,4},{6,7},{7,6},{8,9},{9,8},{10,11... | collective-permute-start | bytes 196616 | tf_op jit(solution)/shard_map/ppermute | solution.py:234
  39.7 6.5 %collective-permute-start.9 = (bf16[64,512]{1,0:T(8,128)(2,1)S(1)}, bf16[64,512]{1,0:T(8,128)(2,1)S(1)}, u32[]{:S(2)}, u32[]{:S(2)}) collective-permute-start(bf16[64,512]{1,0:T(8,128)(2,1)S(1)} %fusion.2), channel_id=1, source_target_pairs={{0,6},{2,4},{4,2},{6,0},{1,7},{3,5},{5,3},{7,1},{8,14},{10,12},{12... | collective-permute-start | bytes 196616 | tf_op jit(solution)/shard_map/ppermute | solution.py:234
  42.1 6.2 %collective-permute-start.8 = (bf16[64,512]{1,0:T(8,128)(2,1)S(1)}, bf16[64,512]{1,0:T(8,128)(2,1)S(1)}, u32[]{:S(2)}, u32[]{:S(2)}) collective-permute-start(bf16[64,512]{1,0:T(8,128)(2,1)S(1)} %fusion.2), channel_id=1, source_target_pairs={{0,4},{2,6},{4,0},{6,2},{1,5},{3,7},{5,1},{7,3},{8,12},{10,14},{12... | collective-permute-start | bytes 196616 | tf_op jit(solution)/shard_map/ppermute | solution.py:234
  46.2 4.3 %collective-permute-start.7 = (bf16[64,512]{1,0:T(8,128)(2,1)S(1)}, bf16[64,512]{1,0:T(8,128)(2,1)S(1)}, u32[]{:S(2)}, u32[]{:S(2)}) collective-permute-start(bf16[64,512]{1,0:T(8,128)(2,1)S(1)} %fusion.2), channel_id=1, source_target_pairs={{0,2},{2,0},{4,6},{6,4},{1,3},{3,1},{5,7},{7,5},{8,10},{10,8},{12,... | collective-permute-start | bytes 196616 | tf_op jit(solution)/shard_map/ppermute | solution.py:234
  48.3 6.5 %collective-permute-start.32 = (bf16[64,512]{1,0:T(8,128)(2,1)S(1)}, bf16[64,512]{1,0:T(8,128)(2,1)S(1)}, u32[]{:S(2)}, u32[]{:S(2)}) collective-permute-start(bf16[64,512]{1,0:T(8,128)(2,1)S(1)} %collective-permute-done.29), channel_id=1, source_target_pairs={{0,6},{2,4},{4,2},{6,0},{1,7},{3,5},{5,3},{7,1},{8,14},{10,12},{12... | collective-permute-start | bytes 196616 | tf_op jit(solution)/shard_map/ppermute | solution.py:234
  50.4 6.4 %collective-permute-start.31 = (bf16[64,512]{1,0:T(8,128)(2,1)S(1)}, bf16[64,512]{1,0:T(8,128)(2,1)S(1)}, u32[]{:S(2)}, u32[]{:S(2)}) collective-permute-start(bf16[64,512]{1,0:T(8,128)(2,1)S(1)} %collective-permute-done.29), channel_id=1, source_target_pairs={{0,4},{2,6},{4,0},{6,2},{1,5},{3,7},{5,1},{7,3},{8,12},{10,14},{12... | collective-permute-start | bytes 196616 | tf_op jit(solution)/shard_map/ppermute | solution.py:234
  54.8 4.3 %collective-permute-start.30 = (bf16[64,512]{1,0:T(8,128)(2,1)S(1)}, bf16[64,512]{1,0:T(8,128)(2,1)S(1)}, u32[]{:S(2)}, u32[]{:S(2)}) collective-permute-start(bf16[64,512]{1,0:T(8,128)(2,1)S(1)} %collective-permute-done.29), channel_id=1, source_target_pairs={{0,2},{2,0},{4,6},{6,4},{1,3},{3,1},{5,7},{7,5},{8,10},{10,8},{12,... | collective-permute-start | bytes 196616 | tf_op jit(solution)/shard_map/ppermute | solution.py:234
  59.0 4.5 %collective-permute-start.13 = (bf16[64,512]{1,0:T(8,128)(2,1)S(1)}, bf16[64,512]{1,0:T(8,128)(2,1)S(1)}, u32[]{:S(2)}, u32[]{:S(2)}) collective-permute-start(bf16[64,512]{1,0:T(8,128)(2,1)S(1)} %collective-permute-done.9), channel_id=1, source_target_pairs={{0,1},{1,0},{2,3},{3,2},{4,5},{5,4},{6,7},{7,6},{8,9},{9,8},{10,11... | collective-permute-start | bytes 196616 | tf_op jit(solution)/shard_map/ppermute | solution.py:234
  60.0 4.8 %collective-permute-start.12 = (bf16[64,512]{1,0:T(8,128)(2,1)S(1)}, bf16[64,512]{1,0:T(8,128)(2,1)S(1)}, u32[]{:S(2)}, u32[]{:S(2)}) collective-permute-start(bf16[64,512]{1,0:T(8,128)(2,1)S(1)} %collective-permute-done.8), channel_id=1, source_target_pairs={{0,1},{1,0},{2,3},{3,2},{4,5},{5,4},{6,7},{7,6},{8,9},{9,8},{10,11... | collective-permute-start | bytes 196616 | tf_op jit(solution)/shard_map/ppermute | solution.py:234
  63.5 4.3 %collective-permute-start.11 = (bf16[64,512]{1,0:T(8,128)(2,1)S(1)}, bf16[64,512]{1,0:T(8,128)(2,1)S(1)}, u32[]{:S(2)}, u32[]{:S(2)}) collective-permute-start(bf16[64,512]{1,0:T(8,128)(2,1)S(1)} %collective-permute-done.7), channel_id=1, source_target_pairs={{0,1},{1,0},{2,3},{3,2},{4,5},{5,4},{6,7},{7,6},{8,9},{9,8},{10,11... | collective-permute-start | bytes 196616 | tf_op jit(solution)/shard_map/ppermute | solution.py:234
  69.2 8.6 %collective-permute-start.33 = (bf16[256,512]{1,0:T(8,128)(2,1)S(1)}, bf16[256,512]{1,0:T(8,128)(2,1)S(1)}, u32[]{:S(2)}, u32[]{:S(2)}) collective-permute-start(bf16[256,512]{1,0:T(8,128)(2,1)S(1)} %pad_maximum_fusion.1), channel_id=1, source_target_pairs={{0,1},{1,0},{2,3},{3,2},{4,5},{5,4},{6,7},{7,6},{8,9},{9,8},{10,11... | collective-permute-start | bytes 786440 | tf_op jit(solution)/shard_map/ppermute | solution.py:234
  72.3 25.3 %collective-permute-start.37 = (bf16[256,2048]{1,0:T(8,128)(2,1)S(1)}, bf16[256,2048]{1,0:T(8,128)(2,1)S(1)}, u32[]{:S(2)}, u32[]{:S(2)}) collective-permute-start(bf16[256,2048]{1,0:T(8,128)(2,1)S(1)} %get-tuple-element.37), channel_id=1, source_target_pairs={{0,24},{8,16},{16,8},{24,0},{1,25},{9,17},{17,9},{25,1},{2,26},{10... | collective-permute-start | bytes 3145736 | tf_op jit(solution)/shard_map/ppermute | solution.py:234
  77.7 42.8 %collective-permute-start.36 = (bf16[256,2048]{1,0:T(8,128)(2,1)S(1)}, bf16[256,2048]{1,0:T(8,128)(2,1)S(1)}, u32[]{:S(2)}, u32[]{:S(2)}) collective-permute-start(bf16[256,2048]{1,0:T(8,128)(2,1)S(1)} %get-tuple-element.38), channel_id=1, source_target_pairs={{0,16},{8,24},{16,0},{24,8},{1,17},{9,25},{17,1},{25,9},{2,18},{10... | collective-permute-start | bytes 3145736 | tf_op jit(solution)/shard_map/ppermute | solution.py:234
  78.1 42.8 %collective-permute-start.34 = (bf16[512,512]{1,0:T(8,128)(2,1)S(1)}, bf16[512,512]{1,0:T(8,128)(2,1)S(1)}, u32[]{:S(2)}, u32[]{:S(2)}) collective-permute-start(bf16[512,512]{1,0:T(8,128)(2,1)S(1)} %constant_dynamic-update-slice_fusion.refs_3_), channel_id=1, source_target_pairs={{0,8},{8,0},{16,24},{24,16},{1,9},{9,1},{17,25},{25,17},{2,10},{10... | collective-permute-start | bytes 1572872 | tf_op jit(solution)/shard_map/ppermute | solution.py:234
  89.5 41.2 %collective-permute-start.27 = (bf16[64,2048]{1,0:T(8,128)(2,1)S(1)}, bf16[64,2048]{1,0:T(8,128)(2,1)S(1)}, u32[]{:S(2)}, u32[]{:S(2)}) collective-permute-start(bf16[64,2048]{1,0:T(8,128)(2,1)S(1)} %get-tuple-element.34), channel_id=1, source_target_pairs={{0,16},{8,24},{16,0},{24,8},{1,17},{9,25},{17,1},{25,9},{2,18},{10... | collective-permute-start | bytes 786440 | tf_op jit(solution)/shard_map/ppermute | solution.py:234
  97.5 45.4 %collective-permute-start.23 = (bf16[64,2048]{1,0:T(8,128)(2,1)S(1)}, bf16[64,2048]{1,0:T(8,128)(2,1)S(1)}, u32[]{:S(2)}, u32[]{:S(2)}) collective-permute-start(bf16[64,2048]{1,0:T(8,128)(2,1)S(1)} %get-tuple-element.32), channel_id=1, source_target_pairs={{0,16},{8,24},{16,0},{24,8},{1,17},{9,25},{17,1},{25,9},{2,18},{10... | collective-permute-start | bytes 786440 | tf_op jit(solution)/shard_map/ppermute | solution.py:234
  120.5 22.2 %collective-permute-start.25 = (bf16[128,2048]{1,0:T(8,128)(2,1)S(1)}, bf16[128,2048]{1,0:T(8,128)(2,1)S(1)}, u32[]{:S(2)}, u32[]{:S(2)}) collective-permute-start(bf16[128,2048]{1,0:T(8,128)(2,1)S(1)} %get-tuple-element.33), channel_id=1, source_target_pairs={{0,16},{8,24},{16,0},{24,8},{1,17},{9,25},{17,1},{25,9},{2,18},{10... | collective-permute-start | bytes 1572872 | tf_op jit(solution)/shard_map/ppermute | solution.py:234
  130.2 13.4 %collective-permute-start.38 = (bf16[128,2048]{1,0:T(8,128)(2,1)S(1)}, bf16[128,2048]{1,0:T(8,128)(2,1)S(1)}, u32[]{:S(2)}, u32[]{:S(2)}) collective-permute-start(bf16[128,2048]{1,0:T(8,128)(2,1)S(1)} %get-tuple-element.35.refs_0_), channel_id=1, source_target_pairs={{0,8},{8,0},{16,24},{24,16},{1,9},{9,1},{17,25},{25,17},{2,10},{10... | collective-permute-start | bytes 1572872 | tf_op jit(solution)/shard_map/ppermute | solution.py:234
  130.2 13.3 %collective-permute-start.39 = (bf16[128,2048]{1,0:T(8,128)(2,1)S(1)}, bf16[128,2048]{1,0:T(8,128)(2,1)S(1)}, u32[]{:S(2)}, u32[]{:S(2)}) collective-permute-start(bf16[128,2048]{1,0:T(8,128)(2,1)S(1)} %get-tuple-element.36.refs_2_), channel_id=1, source_target_pairs={{0,8},{8,0},{16,24},{24,16},{1,9},{9,1},{17,25},{25,17},{2,10},{10... | collective-permute-start | bytes 1572872 | tf_op jit(solution)/shard_map/ppermute | solution.py:234
  130.8 14.1 %collective-permute-start.28 = (bf16[64,2048]{1,0:T(8,128)(2,1)S(1)}, bf16[64,2048]{1,0:T(8,128)(2,1)S(1)}, u32[]{:S(2)}, u32[]{:S(2)}) collective-permute-start(bf16[64,2048]{1,0:T(8,128)(2,1)S(1)} %add_convert_fusion.1.refs_2_), channel_id=1, source_target_pairs={{0,8},{8,0},{16,24},{24,16},{1,9},{9,1},{17,25},{25,17},{2,10},{10... | collective-permute-start | bytes 786440 | tf_op jit(solution)/shard_map/ppermute | solution.py:234
  (11 other events, 79.5 us)
where the time goes:
time: 148 us; the launch traced here: 147 us
  waiting for transfers between devices  74.5 us (50%)
  Pallas kernels  36.1 us (24%)
  starting transfers between devices  27.9 us (19%)
  other arithmetic  5.03 us (3%)
  local copies, waits for them, and re-layouts  1.83 us (1%)
  between operations  1.76 us (1%)
    ppermute x40, waiting for transfers between devices, swap(): return lax.ppermute(value, axis, [(i, i ^ bits) for i in range(size)])  74.5 us
    ppermute x40, starting transfers between devices, swap(): return lax.ppermute(value, axis, [(i, i ^ bits) for i in range(size)])  27.9 us
    pallas_call x3, Pallas kernels, backward(): pl.pallas_call(kernel, in_specs=[pl.BlockSpec(memory_space=pltpu.SMEM)] +...  17.4 us
    pallas_call x1, Pallas kernels, forward(): pl.pallas_call(kernel, in_specs=[smem, smem, smem, pl.BlockSpec(memory_sp...  10.2 us
    pallas_call x3, Pallas kernels, place(): pl.pallas_call(kernel, in_specs=[hbm] * len(operands), out_specs=hbm, out...  3.35 us
  transfers between devices with their start and end apart: 40, of which 18 were waited for; matrix products, arithmetic and copies ran while one was open for 5% of the time, Pallas kernels for 24%

commit v1 on v0

--- a/solution.py
+++ b/solution.py
@@ -367,7 +367,8 @@
     waves = len(counts)
     total_pieces = sum(counts)
     sources, refs = refs[:total_pieces], refs[total_pieces:]
-    row_tab, refs = refs[0], refs[1:]
+    n_tables = 1 + max(table for table, _ in wave_ids)
+    row_tabs, refs = refs[:n_tables], refs[n_tables:]
     col_tabs, refs = refs[:waves], refs[waves:]
     incidents, refs = refs[:waves], refs[waves:]
     outs, refs = refs[: len(chunks)], refs[len(chunks) :]
@@ -400,41 +401,49 @@
         ready.append(target)
     cols = outs[0].shape[1]
     wide = min(512, cols)
-    for k, (at, amount) in enumerate(chunks):
-        back_y = [
-            jnp.dot(row_tab[wave_ids[w], at : at + amount, :], ready[w][...], preferred_element_type=F32).astype(BF16)
-            for w in range(waves)
-        ]
-        masks = [live_row(tiles_ref, (half_at * rows + at + h) // tile_size, cols) for h in range(0, amount, tile_size)]
+    amount = sum(n for _, n in chunks)
+    back_y = [
+        jnp.dot(
+            row_tabs[table][which, first : first + amount, :], ready[w][...], preferred_element_type=F32
+        ).astype(BF16)
+        for w, (table, which) in enumerate(wave_ids)
+    ]
+    for copy in copies:
+        copy.wait()
+    for part in range(0, cols, wide):
+        span = slice(part, part + wide)
+        total = None
         for w in range(waves):
-            copies[k * waves + w].wait()
-        for part in range(0, cols, wide):
-            span = slice(part, part + wide)
-            total = None
-            for w in range(waves):
-                back = lax.dot_general(
-                    back_y[w], col_tabs[w][span, :], (((1,), (1,)), ((), ())), preferred_element_type=F32
-                )
-                term = back * held[w, at - first : at - first + amount, span].astype(F32)
-                total = term if total is None else total + term
-            for h, mask in enumerate(masks):
-                some = slice(h * tile_size, min((h + 1) * tile_size, amount))
-                outs[k][some, span] = (total[some] * mask[:, span]).astype(BF16)
-
-
-def backward(tiles, waves, row_tab, chunks, tile_size, rows):
+            back = lax.dot_general(
+                back_y[w], col_tabs[w][span, :], (((1,), (1,)), ((), ())), preferred_element_type=F32
+            )
+            term = back * held[w, :, span].astype(F32)
+            total = term if total is None else total + term
+        for out, (at, size) in zip(outs, chunks):
+            for h in range(0, size, tile_size):
+                high = min(h + tile_size, size)
+                mask = live_row(tiles_ref, (half_at * rows + at + h) // tile_size, cols)[:, span]
+                out[h:high, span] = (total[at - first + h : at - first + high] * mask).astype(BF16)
+
+
+def backward(tiles, waves, chunks, tile_size, rows):
     cols = tiles.shape[1] * tile_size
     flat = [piece for wave in waves for piece in wave[0]]
     amount = sum(n for _, n in chunks)
     counts = [len(wave[0]) for wave in waves]
     emit = sum(count > 1 for count in counts)
+    tables = []
+    for wave in waves:
+        if not any(wave[1] is table for table in tables):
+            tables.append(wave[1])
+    wave_ids = [([wave[1] is table for table in tables].index(True), wave[2]) for wave in waves]
 
     def kernel(*refs):
         backward_kernel(
             *refs,
             counts=counts,
-            wave_ids=[wave[1] for wave in waves],
-            part_first=[wave[4] for wave in waves],
+            wave_ids=wave_ids,
+            part_first=[wave[5] for wave in waves],
             chunks=chunks,
             tile_size=tile_size,
             rows=rows,
@@ -447,7 +456,7 @@
     outs = pl.pallas_call(
         kernel,
         in_specs=[pl.BlockSpec(memory_space=pltpu.SMEM)]
-        + [vmem] * (len(flat) + 1 + len(waves))
+        + [vmem] * (len(flat) + len(tables) + len(waves))
         + [hbm] * len(waves),
         out_specs=[vmem] * len(out_shape),
         out_shape=out_shape,
@@ -459,7 +468,7 @@
         cost_estimate=pl.CostEstimate(
             flops=2 * len(waves) * amount * M * (cols + M), bytes_accessed=6 * amount * cols, transcendentals=0
         ),
-    )(tiles, *flat, row_tab, *[wave[2] for wave in waves], *[wave[3] for wave in waves])
+    )(tiles, *flat, *tables, *[wave[3] for wave in waves], *[wave[4] for wave in waves])
     return outs[: len(chunks)], outs[len(chunks) :]
 
 
@@ -500,6 +509,31 @@
     )(*operands)
 
 
+def slices(incident, rows, begin):
+    amount, cols = rows - begin, incident.shape[2]
+
+    def kernel(source, own, other, sems):
+        half_at = lax.rem(lax.axis_index("wl"), 2)
+        copies = []
+        for k, (out, where) in enumerate(((own, half_at), (other, 1 - half_at))):
+            span = pl.ds(pl.multiple_of(where * rows + begin, amount), amount)
+            copies.append(pltpu.make_async_copy(source.at[0, span, :], out, sems.at[k]))
+            copies[-1].start()
+        for copy in copies:
+            copy.wait()
+
+    return pl.pallas_call(
+        kernel,
+        in_specs=[pl.BlockSpec(memory_space=pl.ANY)],
+        out_specs=[pl.BlockSpec(memory_space=pltpu.VMEM)] * 2,
+        out_shape=[jax.ShapeDtypeStruct((amount, cols), BF16)] * 2,
+        scratch_shapes=[pltpu.SemaphoreType.DMA((2,))],
+        compiler_params=pltpu.CompilerParams(vmem_limit_bytes=58 << 20),
+        cost_estimate=pl.CostEstimate(flops=0, bytes_accessed=8 * amount * cols, transcendentals=0),
+        name="slices",
+    )(incident)
+
+
 EXCHANGED = (2, 1, 1)
 REPEATED = (2, 2)
 
@@ -510,7 +544,6 @@
     n_col = lax.axis_size("col")
     tile_size = rows // tiles.shape[0]
     half = rows // 2
-    core = lax.axis_index("wl") % 2
     unit = half // 8
     chunks = []
     at = 0
@@ -520,20 +553,20 @@
     n_first = len(EXCHANGED)
     split = chunks[n_first][0]
 
-    def rows_for(which):
-        return lax.dynamic_slice_in_dim(incident[0], which * half + split, half - split, 0)
-
-    inc_straight = swap(rows_for(core), "wl", 2)
-    inc_core = swap(incident, "wl", 1)
+    slice_own, slice_other = slices(incident, half, split)
+    inc_straight = swap(slice_own, "wl", 2)
     groups = slot_groups(n_row, n_col)
     parts, col_own = forward(wl_index, charge, tiles, cotangent, n_row, n_col, groups)
     mine = reduce_blocks(parts, groups, n_row)
-    inc_cross = swap(rows_for(1 - core), "wl", 3)
+    inc_core = swap(incident, "wl", 1)
+    inc_cross = swap(slice_other, "wl", 3)
     col_core = swap(col_own, "wl", 1)
-    indices = jnp.concatenate([wl_index, swap(wl_index, "wl", 2)])
-    indices = jnp.concatenate([indices, swap(indices, "wl", 1)])
-    row_tab = row_tables(indices, half, n_row, n_col, rows)
-    col_straight = col_table(indices[1:2], cols, n_col)
+    near = jnp.concatenate([wl_index, swap(wl_index, "wl", 1)])
+    far = swap(wl_index, "wl", 2)
+    far_core = swap(far, "wl", 1)
+    row_near = row_tables(near, half, n_row, n_col, rows)
+    row_far = row_tables(jnp.concatenate([far, far_core]), half, n_row, n_col, rows)
+    col_straight = col_table(far, cols, n_col)
     col_cross = swap(col_straight, "wl", 1)
 
     here = gather_row(mine, n_row)
@@ -546,21 +579,20 @@
             pieces.append(swap(piece, "col", ky))
             pieces_core.append(swap(pieces[-1], "wl", 1))
 
-    far = swap(mine, "wl", 2)
-    far = jnp.concatenate(gather_row(far, n_row), axis=0)
-    far = jnp.concatenate([far] + [swap(far, "col", ky) for ky in range(1, n_col)], axis=0)
-    far_core = swap(far, "wl", 1)
-
-    own = (aligned(pieces), 0, col_own, incident, None)
-    mate = (aligned(pieces_core), 2, col_core, inc_core, None)
-    first, matrices = backward(tiles, [own, mate], row_tab, chunks[:1], tile_size, half)
+    straight = [swap(joined, "wl", 2)]
+    straight += [swap(straight[0], "col", ky) for ky in range(1, n_col)]
+    cross = [swap(piece, "wl", 1) for piece in straight]
+
+    own = (aligned(pieces), row_near, 0, col_own, incident, None)
+    mate = (aligned(pieces_core), row_near, 1, col_core, inc_core, None)
+    first, matrices = backward(tiles, [own, mate], chunks[:1], tile_size, half)
     if len(matrices) == 2:
         own = ([matrices[0]],) + own[1:]
         mate = ([matrices[1]],) + mate[1:]
-    second, _ = backward(tiles, [own, mate], row_tab, chunks[1:n_first], tile_size, half)
-    straight = ([far], 1, col_straight, inc_straight, split)
-    cross = ([far_core], 3, col_cross, inc_cross, split)
-    both, _ = backward(tiles, [own, mate, straight, cross], row_tab, chunks[n_first:], tile_size, half)
+    second, _ = backward(tiles, [own, mate], chunks[1:n_first], tile_size, half)
+    straight = (aligned(straight), row_far, 0, col_straight, inc_straight, split)
+    cross = (aligned(cross), row_far, 1, col_cross, inc_cross, split)
+    both, _ = backward(tiles, [own, mate, straight, cross], chunks[n_first:], tile_size, half)
     done = []
     for pair in list(first) + list(second):
         total = add_up([pair, swap(pair, "wl", 2)]).astype(BF16)

time: 148 us -> 139 us (0.939)
  waiting for transfers between devices: 74.5 us -> 57.3 us
  starting transfers between devices: 27.9 us -> 34 us
  Pallas kernels: 36.1 us -> 38.3 us
    ppermute x40 -> x39, waiting for transfers between devices: 74.5 us -> 57.3 us  [swap(): return lax.ppermute(value, axis, [(i, i ^ bits) for i in range(size)])]
    ppermute x40 -> x39, starting transfers between devices: 27.9 us -> 34 us  [swap(): return lax.ppermute(value, axis, [(i, i ^ bits) for i in range(size)])]
    pallas_call x0 -> x1, Pallas kernels: none -> 2.96 us  [slices(): pl.pallas_call(kernel, in_specs=[pl.BlockSpec(memory_space=pl.ANY)], out_...]
    dynamic_slice x1 -> x0, local copies, waits for them, and re-layouts: 1.78 us -> none  [rows_for(): lax.dynamic_slice_in_dim(incident[0], which * half + split, half - split, 0)]
    unnamed x10 -> x6, local copies, waits for them, and re-layouts: 0.04 us -> 1.59 us
    pallas_call x3, Pallas kernels: 17.4 us -> 15.9 us  [backward(): pl.pallas_call(kernel, in_specs=[pl.BlockSpec(memory_space=pltpu.SMEM)] +...]
    pallas_call x1 -> x2, Pallas kernels: 2.61 us -> 3.2 us  [row_tables(): pl.pallas_call(kernel, in_specs=[pl.BlockSpec(memory_space=pltpu.SMEM)],...]
  transfers between devices with their start and end apart: 40 -> 39, of which waited for: 18 -> 16; matrix products, arithmetic and copies ran while one was open for 5% -> 4% of each run, Pallas kernels for 24% -> 27%
where the time goes in v1:
time: 139 us
  waiting for transfers between devices  57.3 us (41%)
  Pallas kernels  38.3 us (28%)
  starting transfers between devices  34 us (24%)
  other arithmetic  5.96 us (4%)
  between operations  1.71 us (1%)
  local copies, waits for them, and re-layouts  1.59 us (1%)
    ppermute x39, waiting for transfers between devices, swap(): return lax.ppermute(value, axis, [(i, i ^ bits) for i in range(size)])  57.3 us
    ppermute x39, starting transfers between devices, swap(): return lax.ppermute(value, axis, [(i, i ^ bits) for i in range(size)])  34 us
    pallas_call x3, Pallas kernels, backward(): pl.pallas_call(kernel, in_specs=[pl.BlockSpec(memory_space=pltpu.SMEM)] +...  15.9 us
    pallas_call x1, Pallas kernels, forward(): pl.pallas_call(kernel, in_specs=[smem, smem, smem, pl.BlockSpec(memory_sp...  10.2 us
    pallas_call x3, Pallas kernels, place(): pl.pallas_call(kernel, in_specs=[hbm] * len(operands), out_specs=hbm, out...  3.35 us
    pallas_call x2, Pallas kernels, row_tables(): pl.pallas_call(kernel, in_specs=[pl.BlockSpec(memory_space=pltpu.SMEM)],...  3.2 us
    pallas_call x1, Pallas kernels, slices(): pl.pallas_call(kernel, in_specs=[pl.BlockSpec(memory_space=pl.ANY)], out_...  2.96 us
  transfers between devices with their start and end apart: 39, of which 16 were waited for; matrix products, arithmetic and copies ran while one was open for 4% of the time, Pallas kernels for 27%

profile of v1, /device:TPU:0, one launch (start us, length us, event | category | flops | bytes accessed | tf_op | source)
XLA Modules:
  0.0 138.9 jit_solution(7345620700446712322)
XLA Ops:
  1.8 10.2 %forward.1 = (bf16[1,64,512]{2,1,0:T(8,128)(2,1)}, bf16[1,64,512]{2,1,0:T(8,128)(2,1)}, bf16[1,64,512]{2,1,0:T(8,128)(2,1)}, bf16[1,64,512]{2,1,0:T(8,128)(2,1)}...) custom-call(s32[1]{0:T(128)S(6)} %copy.11.refs_0_, ...), custom_call_target="tpu_custom_call" | custom-call | flops 5368709120 | bytes 8388608 | tf_op jit(solution)/shard_map/forward/pallas_call | solution.py:210
  12.0 2.6 %collective-permute-start.1 = (bf16[1,64,512]{2,1,0:T(8,128)(2,1)}, bf16[1,64,512]{2,1,0:T(8,128)(2,1)S(1)}, u32[]{:S(2)}, u32[]{:S(2)}) collective-permute-start(bf16[1,64,512]{2,1,0:T(8,128)(2,1)} %get-tuple-element.26), channel_id=1, source_target_pairs={{0,1},{1,0},{2,3},{3,2},{4,5},{5,4},{6,7},{7,6},{8,9},{9,8},{10,11... | collective-permute-start | bytes 196616 | tf_op jit(solution)/shard_map/ppermute | solution.py:234
  14.6 1.5 %collective-permute-start.32 = (s32[1]{0:T(128)}, s32[1]{0:T(128)}, u32[]{:S(2)}, u32[]{:S(2)}) collective-permute-start(s32[1]{0:T(128)} %param.9), channel_id=1, source_target_pairs={{0,16},{8,24},{16,0},{24,8},{1,17},{9,25},{17,1},{25,9},{2,18},{10... | collective-permute-start | bytes 20 | tf_op jit(solution)/shard_map/ppermute | solution.py:234
  16.6 1.5 %collective-permute-start.3 = (bf16[1,64,512]{2,1,0:T(8,128)(2,1)}, bf16[1,64,512]{2,1,0:T(8,128)(2,1)S(1)}, u32[]{:S(2)}, u32[]{:S(2)}) collective-permute-start(bf16[1,64,512]{2,1,0:T(8,128)(2,1)} %get-tuple-element.28), channel_id=1, source_target_pairs={{0,1},{1,0},{2,3},{3,2},{4,5},{5,4},{6,7},{7,6},{8,9},{9,8},{10,11... | collective-permute-start | bytes 196616 | tf_op jit(solution)/shard_map/ppermute | solution.py:234
  18.1 1.2 collective-permute-start.5
  20.2 2.2 %collective-permute-done.3 = bf16[1,64,512]{2,1,0:T(8,128)(2,1)S(1)} collective-permute-done((bf16[1,64,512]{2,1,0:T(8,128)(2,1)}, bf16[1,64,512]{2,1,0:T(8,128)(2,1)S(1)}, u32[]{:S(2)}, u32[]{:S(2)}) %collective-permute-start.3) | collective-permute-done | bytes 65568 | tf_op jit(solution)/shard_map/ppermute | solution.py:234
  23.2 2.7 %collective-permute-start.2 = (bf16[64,512]{1,0:T(8,128)(2,1)S(1)}, bf16[64,512]{1,0:T(8,128)(2,1)S(1)}, u32[]{:S(2)}, u32[]{:S(2)}) collective-permute-start(bf16[64,512]{1,0:T(8,128)(2,1)S(1)} %fusion.4), channel_id=1, source_target_pairs={{0,4},{2,6},{4,0},{6,2},{1,5},{3,7},{5,1},{7,3},{8,12},{10,14},{12... | collective-permute-start | bytes 196616 | tf_op jit(solution)/shard_map/ppermute | solution.py:234
  26.9 1.6 %collective-permute-start.4 = (bf16[64,512]{1,0:T(8,128)(2,1)S(1)}, bf16[64,512]{1,0:T(8,128)(2,1)S(1)}, u32[]{:S(2)}, u32[]{:S(2)}) collective-permute-start(bf16[64,512]{1,0:T(8,128)(2,1)S(1)} %fusion.5), channel_id=1, source_target_pairs={{0,2},{2,0},{4,6},{6,4},{1,3},{3,1},{5,7},{7,5},{8,10},{10,8},{12,... | collective-permute-start | bytes 196616 | tf_op jit(solution)/shard_map/ppermute | solution.py:234
  28.8 2.7 %col_table.1.refs_11_ = bf16[2048,512]{1,0:T(8,128)(2,1)} custom-call(s32[1]{0:T(128)} %collective-permute-done.32.index_ref), custom_call_target="tpu_custom_call" | custom-call | flops 20971520 | bytes 4194304 | tf_op jit(solution)/shard_map/col_table/pallas_call | solution.py:354
  32.0 2.6 %collective-permute-done.6 = bf16[64,512]{1,0:T(8,128)(2,1)S(1)} collective-permute-done((bf16[64,512]{1,0:T(8,128)(2,1)S(1)}, bf16[64,512]{1,0:T(8,128)(2,1)S(1)}, u32[]{:S(2)}, u32[]{:S(2)}) %collective-permute-start.6) | collective-permute-done | bytes 65568 | tf_op jit(solution)/shard_map/ppermute | solution.py:234
  36.4 3.3 %collective-permute-start.9 = (bf16[64,512]{1,0:T(8,128)(2,1)S(1)}, bf16[64,512]{1,0:T(8,128)(2,1)S(1)}, u32[]{:S(2)}, u32[]{:S(2)}) collective-permute-start(bf16[64,512]{1,0:T(8,128)(2,1)S(1)} %fusion.2), channel_id=1, source_target_pairs={{0,6},{2,4},{4,2},{6,0},{1,7},{3,5},{5,3},{7,1},{8,14},{10,12},{12... | collective-permute-start | bytes 196616 | tf_op jit(solution)/shard_map/ppermute | solution.py:234
  41.0 2.1 %collective-permute-done.9 = bf16[64,512]{1,0:T(8,128)(2,1)S(1)} collective-permute-done((bf16[64,512]{1,0:T(8,128)(2,1)S(1)}, bf16[64,512]{1,0:T(8,128)(2,1)S(1)}, u32[]{:S(2)}, u32[]{:S(2)}) %collective-permute-start.9) | collective-permute-done | bytes 65568 | tf_op jit(solution)/shard_map/ppermute | solution.py:234
  43.1 2.5 %collective-permute-start.7 = (bf16[64,512]{1,0:T(8,128)(2,1)S(1)}, bf16[64,512]{1,0:T(8,128)(2,1)S(1)}, u32[]{:S(2)}, u32[]{:S(2)}) collective-permute-start(bf16[64,512]{1,0:T(8,128)(2,1)S(1)} %fusion.2), channel_id=1, source_target_pairs={{0,2},{2,0},{4,6},{6,4},{1,3},{3,1},{5,7},{7,5},{8,10},{10,8},{12,... | collective-permute-start | bytes 196616 | tf_op jit(solution)/shard_map/ppermute | solution.py:234
  46.0 1.8 %collective-permute-done.7 = bf16[64,512]{1,0:T(8,128)(2,1)S(1)} collective-permute-done((bf16[64,512]{1,0:T(8,128)(2,1)S(1)}, bf16[64,512]{1,0:T(8,128)(2,1)S(1)}, u32[]{:S(2)}, u32[]{:S(2)}) %collective-permute-start.7) | collective-permute-done | bytes 65568 | tf_op jit(solution)/shard_map/ppermute | solution.py:234
  49.9 2.2 %collective-permute-done.13.refs_5_ = bf16[64,512]{1,0:T(8,128)(2,1)S(1)} collective-permute-done((bf16[64,512]{1,0:T(8,128)(2,1)S(1)}, bf16[64,512]{1,0:T(8,128)(2,1)S(1)}, u32[]{:S(2)}, u32[]{:S(2)}) %collective-permute-start.13) | collective-permute-done | bytes 65568 | tf_op jit(solution)/shard_map/ppermute | solution.py:234
  54.8 1.6 %collective-permute-done.11.refs_3_ = bf16[64,512]{1,0:T(8,128)(2,1)S(1)} collective-permute-done((bf16[64,512]{1,0:T(8,128)(2,1)S(1)}, bf16[64,512]{1,0:T(8,128)(2,1)S(1)}, u32[]{:S(2)}, u32[]{:S(2)}) %collective-permute-start.11) | collective-permute-done | bytes 65568 | tf_op jit(solution)/shard_map/ppermute | solution.py:234
  56.4 1.3 collective-permute-done.18.refs_10_
  61.2 3.0 %slices.1 = (bf16[256,2048]{1,0:T(8,128)(2,1)}, bf16[256,2048]{1,0:T(8,128)(2,1)}) custom-call(bf16[1,1024,2048]{2,1,0:T(8,128)(2,1)} %refs_13_.1), custom_call_target="tpu_custom_call" | custom-call | bytes 4194304 | tf_op jit(solution)/shard_map/slices/pallas_call | solution.py:525
  65.1 3.8 %collective-permute-done.29.refs_4_ = bf16[256,512]{1,0:T(8,128)(2,1)S(1)} collective-permute-done((bf16[256,512]{1,0:T(8,128)(2,1)S(1)}, bf16[256,512]{1,0:T(8,128)(2,1)S(1)}, u32[]{:S(2)}, u32[]{:S(2)}) %collective-permute-start.29) | collective-permute-done | bytes 262176 | tf_op jit(solution)/shard_map/ppermute | solution.py:234
  71.2 1.6 %row_tables.2.refs_11_.refs_3_.refs_7_ = bf16[2,512,512]{2,1,0:T(8,128)(2,1)S(1)} custom-call(s32[2]{0:T(128)S(1)} %pad_add_fusion.refs_0_), custom_call_target="tpu_custom_call" | custom-call | flops 10485760 | bytes 1048576 | tf_op jit(solution)/shard_map/row_tables/pallas_call | solution.py:327
  72.9 1.6 %copy-done.1 = bf16[2048,512]{1,0:T(8,128)(2,1)S(1)} copy-done((bf16[2048,512]{1,0:T(8,128)(2,1)S(1)}, bf16[2048,512]{1,0:T(8,128)(2,1)}, u32[]{:S(2)}) %copy-start.1) | copy-done | bytes 2097176
  74.4 4.6 %shard_map.55 = (bf16[128,2048]{1,0:T(8,128)(2,1)S(1)}, bf16[512,512]{1,0:T(8,128)(2,1)S(1)}, bf16[512,512]{1,0:T(8,128)(2,1)S(1)}) custom-call(s32[8,16]{1,0:T(8,128)S(1)} %copy-done.2, bf16[256,512]{1,0:T(8,128)(2,1)S(1)} %pad_maximum_fusion.refs_1_, bf16[64,512]{1,0:T(8,128)(2,1)S(1)} %collective-permute-done.10.refs_2_, ...), custom_call_target="tpu_custom_call" | custom-call | flops 671088640 | bytes 1572864 | tf_op jit(solution)/shard_map/pallas_call | solution.py:456
  79.1 4.3 %shard_map.56 = (bf16[64,2048]{1,0:T(8,128)(2,1)S(1)}, bf16[64,2048]{1,0:T(8,128)(2,1)S(1)}) custom-call(s32[8,16]{1,0:T(8,128)S(1)} %copy-done.2, bf16[512,512]{1,0:T(8,128)(2,1)S(1)} %get-tuple-element.32.refs_1_, bf16[512,512]{1,0:T(8,128)(2,1)S(1)} %get-tuple-element.33.refs_2_, bf16[2,512,512]{2,1,0:T(8,128)(2,1)S(1)} %row_tables.2.refs_11_.refs_3_.refs_7_, ...), custom_call_target="tpu_custom_call" | custom-call | flops 671088640 | bytes 1572864 | tf_op jit(solution)/shard_map/pallas_call | solution.py:456
  84.1 1.3 pad_add_fusion.1.refs_0_
  85.4 1.6 %row_tables.3.refs_8_ = bf16[2,512,512]{2,1,0:T(8,128)(2,1)S(1)} custom-call(s32[2]{0:T(128)S(1)} %pad_add_fusion.1.refs_0_), custom_call_target="tpu_custom_call" | custom-call | flops 10485760 | bytes 1048576 | tf_op jit(solution)/shard_map/row_tables/pallas_call | solution.py:327
  87.0 1.5 %collective-permute-start.22 = (bf16[64,2048]{1,0:T(8,128)(2,1)S(1)}, bf16[64,2048]{1,0:T(8,128)(2,1)S(1)}, u32[]{:S(2)}, u32[]{:S(2)}) collective-permute-start(bf16[64,2048]{1,0:T(8,128)(2,1)S(1)} %get-tuple-element.34), channel_id=1, source_target_pairs={{0,16},{8,24},{16,0},{24,8},{1,17},{9,25},{17,1},{25,9},{2,18},{10... | collective-permute-start | bytes 786440 | tf_op jit(solution)/shard_map/ppermute | solution.py:234
  88.5 1.9 %collective-permute-done.35.refs_15_ = bf16[256,2048]{1,0:T(8,128)(2,1)S(1)} collective-permute-done((bf16[256,2048]{1,0:T(8,128)(2,1)}, bf16[256,2048]{1,0:T(8,128)(2,1)S(1)}, u32[]{:S(2)}, u32[]{:S(2)}) %collective-permute-start.35) | collective-permute-done | bytes 1048608 | tf_op jit(solution)/shard_map/ppermute | solution.py:234
  91.3 20.1 %collective-permute-done.36.refs_16_ = bf16[256,2048]{1,0:T(8,128)(2,1)S(1)} collective-permute-done((bf16[256,2048]{1,0:T(8,128)(2,1)}, bf16[256,2048]{1,0:T(8,128)(2,1)S(1)}, u32[]{:S(2)}, u32[]{:S(2)}) %collective-permute-start.36) | collective-permute-done | bytes 1048608 | tf_op jit(solution)/shard_map/ppermute | solution.py:234
  111.4 6.9 %shard_map.57 = (bf16[128,2048]{1,0:T(8,128)(2,1)S(1)}, bf16[128,2048]{1,0:T(8,128)(2,1)S(1)}, bf16[512,512]{1,0:T(8,128)(2,1)}, bf16[512,512]{1,0:T(8,128)(2,1)}) custom-call(s32[8,16]{1,0:T(8,128)S(1)} %copy-done.2, bf16[512,512]{1,0:T(8,128)(2,1)S(1)} %get-tuple-element.32.refs_1_, bf16[512,512]{1,0:T(8,128)(2,1)S(1)} %get-tuple-element.33.refs_2_, ...), custom_call_target="tpu_custom_call" | custom-call | flops 2684354560 | bytes 3145728 | tf_op jit(solution)/shard_map/pallas_call | solution.py:456
  118.3 1.4 %collective-permute-start.37 = (bf16[128,2048]{1,0:T(8,128)(2,1)S(1)}, bf16[128,2048]{1,0:T(8,128)(2,1)S(1)}, u32[]{:S(2)}, u32[]{:S(2)}) collective-permute-start(bf16[128,2048]{1,0:T(8,128)(2,1)S(1)} %get-tuple-element.39.refs_0_), channel_id=1, source_target_pairs={{0,8},{8,0},{16,24},{24,16},{1,9},{9,1},{17,25},{25,17},{2,10},{10... | collective-permute-start | bytes 1572872 | tf_op jit(solution)/shard_map/ppermute | solution.py:234
  120.4 14.1 %collective-permute-done.24 = bf16[128,2048]{1,0:T(8,128)(2,1)S(1)} collective-permute-done((bf16[128,2048]{1,0:T(8,128)(2,1)S(1)}, bf16[128,2048]{1,0:T(8,128)(2,1)S(1)}, u32[]{:S(2)}, u32[]{:S(2)}) %collective-permute-start.24) | collective-permute-done | bytes 524320 | tf_op jit(solution)/shard_map/ppermute | solution.py:234
  135.4 1.3 shard_map.58.refs_4_
  (73 shorter events, 24.5 us)
Async XLA Ops:
  0.0 70.4 %collective-permute-start.21 = (bf16[1,1024,2048]{2,1,0:T(8,128)(2,1)}, bf16[1,1024,2048]{2,1,0:T(8,128)(2,1)}, u32[]{:S(2)}, u32[]{:S(2)}) collective-permute-start(bf16[1,1024,2048]{2,1,0:T(8,128)(2,1)} %refs_13_.1), channel_id=1, source_target_pairs={{0,8},{8,0},{16,24},{24,16},{1,9},{9,1},{17,25},{25,17},{2,10},{10... | collective-permute-start | bytes 12582920 | tf_op jit(solution)/shard_map/ppermute | solution.py:234
  12.0 6.1 %collective-permute-start.1 = (bf16[1,64,512]{2,1,0:T(8,128)(2,1)}, bf16[1,64,512]{2,1,0:T(8,128)(2,1)S(1)}, u32[]{:S(2)}, u32[]{:S(2)}) collective-permute-start(bf16[1,64,512]{2,1,0:T(8,128)(2,1)} %get-tuple-element.26), channel_id=1, source_target_pairs={{0,1},{1,0},{2,3},{3,2},{4,5},{5,4},{6,7},{7,6},{8,9},{9,8},{10,11... | collective-permute-start | bytes 196616 | tf_op jit(solution)/shard_map/ppermute | solution.py:234
  14.6 12.3 %collective-permute-start.32 = (s32[1]{0:T(128)}, s32[1]{0:T(128)}, u32[]{:S(2)}, u32[]{:S(2)}) collective-permute-start(s32[1]{0:T(128)} %param.9), channel_id=1, source_target_pairs={{0,16},{8,24},{16,0},{24,8},{1,17},{9,25},{17,1},{25,9},{2,18},{10... | collective-permute-start | bytes 20 | tf_op jit(solution)/shard_map/ppermute | solution.py:234
  16.1 12.5 %collective-permute-start = (bf16[1,64,512]{2,1,0:T(8,128)(2,1)}, bf16[1,64,512]{2,1,0:T(8,128)(2,1)S(1)}, u32[]{:S(2)}, u32[]{:S(2)}) collective-permute-start(bf16[1,64,512]{2,1,0:T(8,128)(2,1)} %get-tuple-element.24), channel_id=1, source_target_pairs={{0,1},{1,0},{2,3},{3,2},{4,5},{5,4},{6,7},{7,6},{8,9},{9,8},{10,11... | collective-permute-start | bytes 196616 | tf_op jit(solution)/shard_map/ppermute | solution.py:234
  16.6 5.8 %collective-permute-start.3 = (bf16[1,64,512]{2,1,0:T(8,128)(2,1)}, bf16[1,64,512]{2,1,0:T(8,128)(2,1)S(1)}, u32[]{:S(2)}, u32[]{:S(2)}) collective-permute-start(bf16[1,64,512]{2,1,0:T(8,128)(2,1)} %get-tuple-element.28), channel_id=1, source_target_pairs={{0,1},{1,0},{2,3},{3,2},{4,5},{5,4},{6,7},{7,6},{8,9},{9,8},{10,11... | collective-permute-start | bytes 196616 | tf_op jit(solution)/shard_map/ppermute | solution.py:234
  18.1 5.1 %collective-permute-start.5 = (bf16[1,64,512]{2,1,0:T(8,128)(2,1)}, bf16[1,64,512]{2,1,0:T(8,128)(2,1)S(1)}, u32[]{:S(2)}, u32[]{:S(2)}) collective-permute-start(bf16[1,64,512]{2,1,0:T(8,128)(2,1)} %get-tuple-element.30), channel_id=1, source_target_pairs={{0,1},{1,0},{2,3},{3,2},{4,5},{5,4},{6,7},{7,6},{8,9},{9,8},{10,11... | collective-permute-start | bytes 196616 | tf_op jit(solution)/shard_map/ppermute | solution.py:234
  22.3 47.0 %collective-permute-start.20 = (bf16[2048,512]{1,0:T(8,128)(2,1)}, bf16[2048,512]{1,0:T(8,128)(2,1)}, u32[]{:S(2)}, u32[]{:S(2)}) collective-permute-start(bf16[2048,512]{1,0:T(8,128)(2,1)} %get-tuple-element.31.refs_12_.refs_4_.refs_9_), channel_id=1, source_target_pairs={{0,8},{8,0},{16,24},{24,16},{1,9},{9,1},{17,25},{25,17},{2,10},{10... | collective-permute-start | bytes 6291464 | tf_op jit(solution)/shard_map/ppermute | solution.py:234
  23.2 8.3 %collective-permute-start.2 = (bf16[64,512]{1,0:T(8,128)(2,1)S(1)}, bf16[64,512]{1,0:T(8,128)(2,1)S(1)}, u32[]{:S(2)}, u32[]{:S(2)}) collective-permute-start(bf16[64,512]{1,0:T(8,128)(2,1)S(1)} %fusion.4), channel_id=1, source_target_pairs={{0,4},{2,6},{4,0},{6,2},{1,5},{3,7},{5,1},{7,3},{8,12},{10,14},{12... | collective-permute-start | bytes 196616 | tf_op jit(solution)/shard_map/ppermute | solution.py:234
  26.9 4.6 %collective-permute-start.4 = (bf16[64,512]{1,0:T(8,128)(2,1)S(1)}, bf16[64,512]{1,0:T(8,128)(2,1)S(1)}, u32[]{:S(2)}, u32[]{:S(2)}) collective-permute-start(bf16[64,512]{1,0:T(8,128)(2,1)S(1)} %fusion.5), channel_id=1, source_target_pairs={{0,2},{2,0},{4,6},{6,4},{1,3},{3,1},{5,7},{7,5},{8,10},{10,8},{12,... | collective-permute-start | bytes 196616 | tf_op jit(solution)/shard_map/ppermute | solution.py:234
  28.6 6.1 %collective-permute-start.6 = (bf16[64,512]{1,0:T(8,128)(2,1)S(1)}, bf16[64,512]{1,0:T(8,128)(2,1)S(1)}, u32[]{:S(2)}, u32[]{:S(2)}) collective-permute-start(bf16[64,512]{1,0:T(8,128)(2,1)S(1)} %fusion.6), channel_id=1, source_target_pairs={{0,6},{2,4},{4,2},{6,0},{1,7},{3,5},{5,3},{7,1},{8,14},{10,12},{12... | collective-permute-start | bytes 196616 | tf_op jit(solution)/shard_map/ppermute | solution.py:234
  31.5 4.0 %collective-permute-start.19 = (s32[1]{0:T(128)}, s32[1]{0:T(128)}, u32[]{:S(2)}, u32[]{:S(2)}) collective-permute-start(s32[1]{0:T(128)} %param.9), channel_id=1, source_target_pairs={{0,8},{8,0},{16,24},{24,16},{1,9},{9,1},{17,25},{25,17},{2,10},{10... | collective-permute-start | bytes 20 | tf_op jit(solution)/shard_map/ppermute | solution.py:234
  31.5 79.9 %collective-permute-start.34 = (bf16[2048,512]{1,0:T(8,128)(2,1)}, bf16[2048,512]{1,0:T(8,128)(2,1)}, u32[]{:S(2)}, u32[]{:S(2)}) collective-permute-start(bf16[2048,512]{1,0:T(8,128)(2,1)} %col_table.1.refs_11_), channel_id=1, source_target_pairs={{0,8},{8,0},{16,24},{24,16},{1,9},{9,1},{17,25},{25,17},{2,10},{10... | collective-permute-start | bytes 6291464 | tf_op jit(solution)/shard_map/ppermute | solution.py:234
  35.5 4.6 %collective-permute-start.10 = (bf16[64,512]{1,0:T(8,128)(2,1)S(1)}, bf16[64,512]{1,0:T(8,128)(2,1)S(1)}, u32[]{:S(2)}, u32[]{:S(2)}) collective-permute-start(bf16[64,512]{1,0:T(8,128)(2,1)S(1)} %fusion.2), channel_id=1, source_target_pairs={{0,1},{1,0},{2,3},{3,2},{4,5},{5,4},{6,7},{7,6},{8,9},{9,8},{10,11... | collective-permute-start | bytes 196616 | tf_op jit(solution)/shard_map/ppermute | solution.py:234
  36.4 6.7 %collective-permute-start.9 = (bf16[64,512]{1,0:T(8,128)(2,1)S(1)}, bf16[64,512]{1,0:T(8,128)(2,1)S(1)}, u32[]{:S(2)}, u32[]{:S(2)}) collective-permute-start(bf16[64,512]{1,0:T(8,128)(2,1)S(1)} %fusion.2), channel_id=1, source_target_pairs={{0,6},{2,4},{4,2},{6,0},{1,7},{3,5},{5,3},{7,1},{8,14},{10,12},{12... | collective-permute-start | bytes 196616 | tf_op jit(solution)/shard_map/ppermute | solution.py:234
  40.1 5.9 %collective-permute-start.8 = (bf16[64,512]{1,0:T(8,128)(2,1)S(1)}, bf16[64,512]{1,0:T(8,128)(2,1)S(1)}, u32[]{:S(2)}, u32[]{:S(2)}) collective-permute-start(bf16[64,512]{1,0:T(8,128)(2,1)S(1)} %fusion.2), channel_id=1, source_target_pairs={{0,4},{2,6},{4,0},{6,2},{1,5},{3,7},{5,1},{7,3},{8,12},{10,14},{12... | collective-permute-start | bytes 196616 | tf_op jit(solution)/shard_map/ppermute | solution.py:234
  43.1 4.8 %collective-permute-start.7 = (bf16[64,512]{1,0:T(8,128)(2,1)S(1)}, bf16[64,512]{1,0:T(8,128)(2,1)S(1)}, u32[]{:S(2)}, u32[]{:S(2)}) collective-permute-start(bf16[64,512]{1,0:T(8,128)(2,1)S(1)} %fusion.2), channel_id=1, source_target_pairs={{0,2},{2,0},{4,6},{6,4},{1,3},{3,1},{5,7},{7,5},{8,10},{10,8},{12,... | collective-permute-start | bytes 196616 | tf_op jit(solution)/shard_map/ppermute | solution.py:234
  47.8 4.3 %collective-permute-start.13 = (bf16[64,512]{1,0:T(8,128)(2,1)S(1)}, bf16[64,512]{1,0:T(8,128)(2,1)S(1)}, u32[]{:S(2)}, u32[]{:S(2)}) collective-permute-start(bf16[64,512]{1,0:T(8,128)(2,1)S(1)} %collective-permute-done.9), channel_id=1, source_target_pairs={{0,1},{1,0},{2,3},{3,2},{4,5},{5,4},{6,7},{7,6},{8,9},{9,8},{10,11... | collective-permute-start | bytes 196616 | tf_op jit(solution)/shard_map/ppermute | solution.py:234
  48.7 4.9 %collective-permute-start.12 = (bf16[64,512]{1,0:T(8,128)(2,1)S(1)}, bf16[64,512]{1,0:T(8,128)(2,1)S(1)}, u32[]{:S(2)}, u32[]{:S(2)}) collective-permute-start(bf16[64,512]{1,0:T(8,128)(2,1)S(1)} %collective-permute-done.8), channel_id=1, source_target_pairs={{0,1},{1,0},{2,3},{3,2},{4,5},{5,4},{6,7},{7,6},{8,9},{9,8},{10,11... | collective-permute-start | bytes 196616 | tf_op jit(solution)/shard_map/ppermute | solution.py:234
  52.1 4.3 %collective-permute-start.11 = (bf16[64,512]{1,0:T(8,128)(2,1)S(1)}, bf16[64,512]{1,0:T(8,128)(2,1)S(1)}, u32[]{:S(2)}, u32[]{:S(2)}) collective-permute-start(bf16[64,512]{1,0:T(8,128)(2,1)S(1)} %collective-permute-done.7), channel_id=1, source_target_pairs={{0,1},{1,0},{2,3},{3,2},{4,5},{5,4},{6,7},{7,6},{8,9},{9,8},{10,11... | collective-permute-start | bytes 196616 | tf_op jit(solution)/shard_map/ppermute | solution.py:234
  53.6 6.7 %collective-permute-start.28 = (bf16[256,512]{1,0:T(8,128)(2,1)S(1)}, bf16[256,512]{1,0:T(8,128)(2,1)S(1)}, u32[]{:S(2)}, u32[]{:S(2)}) collective-permute-start(bf16[256,512]{1,0:T(8,128)(2,1)S(1)} %pad_maximum_fusion.refs_1_), channel_id=1, source_target_pairs={{0,16},{8,24},{16,0},{24,8},{1,17},{9,25},{17,1},{25,9},{2,18},{10... | collective-permute-start | bytes 786440 | tf_op jit(solution)/shard_map/ppermute | solution.py:234
  60.1 4.0 %collective-permute-start.14 = (bf16[256,512]{1,0:T(8,128)(2,1)S(1)}, bf16[256,512]{1,0:T(8,128)(2,1)S(1)}, u32[]{:S(2)}, u32[]{:S(2)}) collective-permute-start(bf16[256,512]{1,0:T(8,128)(2,1)S(1)} %pad_maximum_fusion.refs_1_), channel_id=1, source_target_pairs={{0,8},{8,0},{16,24},{24,16},{1,9},{9,1},{17,25},{25,17},{2,10},{10... | collective-permute-start | bytes 786440 | tf_op jit(solution)/shard_map/ppermute | solution.py:234
  60.3 8.6 %collective-permute-start.29 = (bf16[256,512]{1,0:T(8,128)(2,1)S(1)}, bf16[256,512]{1,0:T(8,128)(2,1)S(1)}, u32[]{:S(2)}, u32[]{:S(2)}) collective-permute-start(bf16[256,512]{1,0:T(8,128)(2,1)S(1)} %collective-permute-done.28.refs_3_), channel_id=1, source_target_pairs={{0,1},{1,0},{2,3},{3,2},{4,5},{5,4},{6,7},{7,6},{8,9},{9,8},{10,11... | collective-permute-start | bytes 786440 | tf_op jit(solution)/shard_map/ppermute | solution.py:234
  64.2 26.3 %collective-permute-start.35 = (bf16[256,2048]{1,0:T(8,128)(2,1)}, bf16[256,2048]{1,0:T(8,128)(2,1)S(1)}, u32[]{:S(2)}, u32[]{:S(2)}) collective-permute-start(bf16[256,2048]{1,0:T(8,128)(2,1)} %get-tuple-element.37), channel_id=1, source_target_pairs={{0,16},{8,24},{16,0},{24,8},{1,17},{9,25},{17,1},{25,9},{2,18},{10... | collective-permute-start | bytes 3145736 | tf_op jit(solution)/shard_map/ppermute | solution.py:234
  68.9 42.5 %collective-permute-start.36 = (bf16[256,2048]{1,0:T(8,128)(2,1)}, bf16[256,2048]{1,0:T(8,128)(2,1)S(1)}, u32[]{:S(2)}, u32[]{:S(2)}) collective-permute-start(bf16[256,2048]{1,0:T(8,128)(2,1)} %get-tuple-element.38), channel_id=1, source_target_pairs={{0,24},{8,16},{16,8},{24,0},{1,25},{9,17},{17,9},{25,1},{2,26},{10... | collective-permute-start | bytes 3145736 | tf_op jit(solution)/shard_map/ppermute | solution.py:234
  69.4 14.0 %collective-permute-start.30 = (bf16[256,512]{1,0:T(8,128)(2,1)S(1)}, bf16[256,512]{1,0:T(8,128)(2,1)S(1)}, u32[]{:S(2)}, u32[]{:S(2)}) collective-permute-start(bf16[256,512]{1,0:T(8,128)(2,1)S(1)} %collective-permute-done.28.refs_3_), channel_id=1, source_target_pairs={{0,8},{8,0},{16,24},{24,16},{1,9},{9,1},{17,25},{25,17},{2,10},{10... | collective-permute-start | bytes 786440 | tf_op jit(solution)/shard_map/ppermute | solution.py:234
  70.4 16.6 %collective-permute-start.31 = (bf16[256,512]{1,0:T(8,128)(2,1)S(1)}, bf16[256,512]{1,0:T(8,128)(2,1)S(1)}, u32[]{:S(2)}, u32[]{:S(2)}) collective-permute-start(bf16[256,512]{1,0:T(8,128)(2,1)S(1)} %collective-permute-done.29.refs_4_), channel_id=1, source_target_pairs={{0,8},{8,0},{16,24},{24,16},{1,9},{9,1},{17,25},{25,17},{2,10},{10... | collective-permute-start | bytes 786440 | tf_op jit(solution)/shard_map/ppermute | solution.py:234
  83.4 36.4 %collective-permute-start.26 = (bf16[64,2048]{1,0:T(8,128)(2,1)S(1)}, bf16[64,2048]{1,0:T(8,128)(2,1)S(1)}, u32[]{:S(2)}, u32[]{:S(2)}) collective-permute-start(bf16[64,2048]{1,0:T(8,128)(2,1)S(1)} %get-tuple-element.36), channel_id=1, source_target_pairs={{0,16},{8,24},{16,0},{24,8},{1,17},{9,25},{17,1},{25,9},{2,18},{10... | collective-permute-start | bytes 786440 | tf_op jit(solution)/shard_map/ppermute | solution.py:234
  87.0 47.7 %collective-permute-start.22 = (bf16[64,2048]{1,0:T(8,128)(2,1)S(1)}, bf16[64,2048]{1,0:T(8,128)(2,1)S(1)}, u32[]{:S(2)}, u32[]{:S(2)}) collective-permute-start(bf16[64,2048]{1,0:T(8,128)(2,1)S(1)} %get-tuple-element.34), channel_id=1, source_target_pairs={{0,16},{8,24},{16,0},{24,8},{1,17},{9,25},{17,1},{25,9},{2,18},{10... | collective-permute-start | bytes 786440 | tf_op jit(solution)/shard_map/ppermute | solution.py:234
  90.5 44.0 %collective-permute-start.24 = (bf16[128,2048]{1,0:T(8,128)(2,1)S(1)}, bf16[128,2048]{1,0:T(8,128)(2,1)S(1)}, u32[]{:S(2)}, u32[]{:S(2)}) collective-permute-start(bf16[128,2048]{1,0:T(8,128)(2,1)S(1)} %get-tuple-element.35), channel_id=1, source_target_pairs={{0,16},{8,24},{16,0},{24,8},{1,17},{9,25},{17,1},{25,9},{2,18},{10... | collective-permute-start | bytes 1572872 | tf_op jit(solution)/shard_map/ppermute | solution.py:234
  118.3 17.0 %collective-permute-start.37 = (bf16[128,2048]{1,0:T(8,128)(2,1)S(1)}, bf16[128,2048]{1,0:T(8,128)(2,1)S(1)}, u32[]{:S(2)}, u32[]{:S(2)}) collective-permute-start(bf16[128,2048]{1,0:T(8,128)(2,1)S(1)} %get-tuple-element.39.refs_0_), channel_id=1, source_target_pairs={{0,8},{8,0},{16,24},{24,16},{1,9},{9,1},{17,25},{25,17},{2,10},{10... | collective-permute-start | bytes 1572872 | tf_op jit(solution)/shard_map/ppermute | solution.py:234
  119.8 15.6 %collective-permute-start.38 = (bf16[128,2048]{1,0:T(8,128)(2,1)S(1)}, bf16[128,2048]{1,0:T(8,128)(2,1)S(1)}, u32[]{:S(2)}, u32[]{:S(2)}) collective-permute-start(bf16[128,2048]{1,0:T(8,128)(2,1)S(1)} %get-tuple-element.40.refs_2_), channel_id=1, source_target_pairs={{0,8},{8,0},{16,24},{24,16},{1,9},{9,1},{17,25},{25,17},{2,10},{10... | collective-permute-start | bytes 1572872 | tf_op jit(solution)/shard_map/ppermute | solution.py:234
  119.9 16.8 %collective-permute-start.27 = (bf16[64,2048]{1,0:T(8,128)(2,1)S(1)}, bf16[64,2048]{1,0:T(8,128)(2,1)S(1)}, u32[]{:S(2)}, u32[]{:S(2)}) collective-permute-start(bf16[64,2048]{1,0:T(8,128)(2,1)S(1)} %add_convert_fusion.1.refs_2_), channel_id=1, source_target_pairs={{0,8},{8,0},{16,24},{24,16},{1,9},{9,1},{17,25},{25,17},{2,10},{10... | collective-permute-start | bytes 786440 | tf_op jit(solution)/shard_map/ppermute | solution.py:234
  (10 other events, 109.0 us)

commit v2 on v1

--- a/solution.py
+++ b/solution.py
@@ -109,8 +109,13 @@
     return jnp.concatenate(parts, axis=1)
 
 
-def forward_kernel(index_ref, charge_ref, tiles_ref, cot_ref, *refs, rows, cols, n_row, groups):
-    outs, col_tab = refs[:-7], refs[-7]
+def slice_rows(source, target, sem, which, begin):
+    span = pl.ds(pl.multiple_of(which * (source.shape[1] // 2) + begin, target.shape[0]), target.shape[0])
+    return pltpu.make_async_copy(source.at[0, span, :], target, sem)
+
+
+def forward_kernel(index_ref, charge_ref, tiles_ref, cot_ref, inc_ref, *refs, rows, cols, n_row, groups, begin):
+    outs, (col_tab, slice_ref) = refs[:-8], refs[-8:-6]
     row_tab, inner, fine_ref, t_ref, held, sems = refs[-6:]
     block = min(256, rows)
     extent = rows * n_row
@@ -122,6 +127,9 @@
         span = pl.ds(step * block, block)
         copies.append(pltpu.make_async_copy(cot_ref.at[0, :, span, :], held.at[:, span, :], sems.at[step]))
         copies[-1].start()
+    half_at = lax.rem(lax.axis_index("wl"), 2)
+    slice_copy = slice_rows(inc_ref, slice_ref, sems.at[rows // block], 1 - half_at, begin)
+    slice_copy.start()
     period = quarter_period(index_ref[0])
 
     def write_col(at, amount, re, im):
@@ -194,22 +202,28 @@
         for k, kz in enumerate(slots):
             source = (col_at ^ ky) * n_row + (row_at ^ kz)
             out[k] = t_ref[source].astype(BF16)
-
-
-def forward(index, charge, tiles, cotangent, n_row, n_col, groups):
+    slice_copy.wait()
+
+
+def in_hbm(value):
+    return pltpu.with_memory_space_constraint(value, pltpu.HBM)
+
+
+def forward(index, charge, tiles, cotangent, incident, begin, n_row, n_col, groups):
     rows, cols = cotangent.shape[2:]
     block = min(256, rows)
     per = M // (n_row * n_col)
     out_shape = [jax.ShapeDtypeStruct((len(slots), per, M), BF16) for _, slots in groups]
     out_shape.append(jax.ShapeDtypeStruct((cols, M), BF16))
+    out_shape.append(jax.ShapeDtypeStruct((rows // 2 - begin, cols), BF16))
 
     def kernel(*refs):
-        forward_kernel(*refs, rows=rows, cols=cols, n_row=n_row, groups=groups)
+        forward_kernel(*refs, rows=rows, cols=cols, n_row=n_row, groups=groups, begin=begin)
 
     smem = pl.BlockSpec(memory_space=pltpu.SMEM)
     outs = pl.pallas_call(
         kernel,
-        in_specs=[smem, smem, smem, pl.BlockSpec(memory_space=pltpu.HBM)],
+        in_specs=[smem, smem, smem] + [pl.BlockSpec(memory_space=pltpu.HBM)] * 2,
         out_specs=[pl.BlockSpec(memory_space=pltpu.VMEM)] * len(out_shape),
         out_shape=out_shape,
         scratch_shapes=[
@@ -218,15 +232,15 @@
             pltpu.VMEM((2, HALF, HALF), F32),
             pltpu.VMEM((n_row * n_col, per, M), F32),
             pltpu.VMEM((2, rows, cols), BF16),
-            pltpu.SemaphoreType.DMA((rows // block,)),
+            pltpu.SemaphoreType.DMA((rows // block + 1,)),
         ],
-        compiler_params=pltpu.CompilerParams(vmem_limit_bytes=55 << 20),
+        compiler_params=pltpu.CompilerParams(vmem_limit_bytes=36 << 20),
         cost_estimate=pl.CostEstimate(
             flops=2 * rows * 2 * M * (cols + M), bytes_accessed=4 * rows * cols, transcendentals=0
         ),
         name="forward",
-    )(index, charge, tiles, cotangent)
-    return outs[:-1], outs[-1]
+    )(index, charge, tiles, in_hbm(cotangent), in_hbm(incident))
+    return outs[:-2], outs[-2], outs[-1]
 
 
 def swap(value, axis, bits):
@@ -509,29 +523,24 @@
     )(*operands)
 
 
-def slices(incident, rows, begin):
-    amount, cols = rows - begin, incident.shape[2]
-
-    def kernel(source, own, other, sems):
-        half_at = lax.rem(lax.axis_index("wl"), 2)
-        copies = []
-        for k, (out, where) in enumerate(((own, half_at), (other, 1 - half_at))):
-            span = pl.ds(pl.multiple_of(where * rows + begin, amount), amount)
-            copies.append(pltpu.make_async_copy(source.at[0, span, :], out, sems.at[k]))
-            copies[-1].start()
-        for copy in copies:
-            copy.wait()
+def own_slice(incident, begin):
+    amount, cols = incident.shape[1] // 2 - begin, incident.shape[2]
+
+    def kernel(source, out, sem):
+        copy = slice_rows(source, out, sem, lax.rem(lax.axis_index("wl"), 2), begin)
+        copy.start()
+        copy.wait()
 
     return pl.pallas_call(
         kernel,
-        in_specs=[pl.BlockSpec(memory_space=pl.ANY)],
-        out_specs=[pl.BlockSpec(memory_space=pltpu.VMEM)] * 2,
-        out_shape=[jax.ShapeDtypeStruct((amount, cols), BF16)] * 2,
-        scratch_shapes=[pltpu.SemaphoreType.DMA((2,))],
-        compiler_params=pltpu.CompilerParams(vmem_limit_bytes=58 << 20),
-        cost_estimate=pl.CostEstimate(flops=0, bytes_accessed=8 * amount * cols, transcendentals=0),
-        name="slices",
-    )(incident)
+        in_specs=[pl.BlockSpec(memory_space=pltpu.HBM)],
+        out_specs=pl.BlockSpec(memory_space=pltpu.VMEM),
+        out_shape=jax.ShapeDtypeStruct((amount, cols), BF16),
+        scratch_shapes=[pltpu.SemaphoreType.DMA],
+        compiler_params=pltpu.CompilerParams(vmem_limit_bytes=4 << 20),
+        cost_estimate=pl.CostEstimate(flops=0, bytes_accessed=4 * amount * cols, transcendentals=0),
+        name="own_slice",
+    )(in_hbm(incident))
 
 
 EXCHANGED = (2, 1, 1)
@@ -553,10 +562,11 @@
     n_first = len(EXCHANGED)
     split = chunks[n_first][0]
 
-    slice_own, slice_other = slices(incident, half, split)
-    inc_straight = swap(slice_own, "wl", 2)
+    inc_straight = swap(own_slice(incident, split), "wl", 2)
     groups = slot_groups(n_row, n_col)
-    parts, col_own = forward(wl_index, charge, tiles, cotangent, n_row, n_col, groups)
+    parts, col_own, slice_other = forward(
+        wl_index, charge, tiles, cotangent, incident, split, n_row, n_col, groups
+    )
     mine = reduce_blocks(parts, groups, n_row)
     inc_core = swap(incident, "wl", 1)
     inc_cross = swap(slice_other, "wl", 3)

time: 139 us -> 134 us (0.964)
  waiting for transfers between devices: 57.3 us -> 68 us
  Pallas kernels: 38.3 us -> 28.4 us
  other arithmetic: 5.96 us -> 2.37 us
    ppermute x39, waiting for transfers between devices: 57.3 us -> 68 us  [swap(): return lax.ppermute(value, axis, [(i, i ^ bits) for i in range(size)])]
    pallas_call x3, Pallas kernels: 15.9 us -> 10.6 us  [backward(): pl.pallas_call(kernel, in_specs=[pl.BlockSpec(memory_space=pltpu.SMEM)] +...]
    pallas_call x2, Pallas kernels: 13.2 us -> 9.96 us  [the longest x1 8.72 us: forward(): pl.pallas_call(kernel, in_specs=[smem, smem, smem] + [pl.BlockSpec(memory...]
    squeeze x3, other arithmetic: 2.73 us -> 0.06 us  [reduce_blocks(): reduced[kz] = total[k]]
    pallas_call x1, Pallas kernels: 2.7 us -> 1.29 us  [col_table(): pl.pallas_call(kernel, in_specs=[pl.BlockSpec(memory_space=pltpu.SMEM)],...]
  transfers between devices with their start and end apart: 39 -> 39, of which waited for: 16 -> 20; matrix products, arithmetic and copies ran while one was open for 4% -> 2% of each run, Pallas kernels for 27% -> 21%
where the time goes in v2:
time: 134 us
  waiting for transfers between devices  68 us (51%)
  starting transfers between devices  32.9 us (25%)
  Pallas kernels  28.4 us (21%)
  other arithmetic  2.37 us (2%)
  between operations  1.73 us (1%)
    ppermute x39, waiting for transfers between devices, swap(): return lax.ppermute(value, axis, [(i, i ^ bits) for i in range(size)])  68 us
    ppermute x39, starting transfers between devices, swap(): return lax.ppermute(value, axis, [(i, i ^ bits) for i in range(size)])  32.9 us
    pallas_call x3, Pallas kernels, backward(): pl.pallas_call(kernel, in_specs=[pl.BlockSpec(memory_space=pltpu.SMEM)] +...  10.6 us
    pallas_call x1, Pallas kernels, forward(): pl.pallas_call(kernel, in_specs=[smem, smem, smem] + [pl.BlockSpec(memory...  8.72 us
    pallas_call x3, Pallas kernels, place(): pl.pallas_call(kernel, in_specs=[hbm] * len(operands), out_specs=hbm, out...  3.35 us
    pallas_call x2, Pallas kernels, row_tables(): pl.pallas_call(kernel, in_specs=[pl.BlockSpec(memory_space=pltpu.SMEM)],...  3.2 us
  transfers between devices with their start and end apart: 39, of which 20 were waited for; matrix products, arithmetic and copies ran while one was open for 2% of the time, Pallas kernels for 21%

profile of v2, /device:TPU:0, one launch (start us, length us, event | category | flops | bytes accessed | tf_op | source)
XLA Modules:
  0.0 134.1 jit_solution(15147643309477680459)
XLA Ops:
  2.5 8.7 %forward.1 = (bf16[1,64,512]{2,1,0:T(8,128)(2,1)S(1)}, bf16[1,64,512]{2,1,0:T(8,128)(2,1)S(1)}, bf16[1,64,512]{2,1,0:T(8,128)(2,1)S(1)}, bf16[1,64,512]{2,1,0:T(...) custom-call(s32[1]{0:T(128)S(6)} %copy.11.refs_0_, ...), custom_call_target="tpu_custom_call" | custom-call | flops 5368709120 | bytes 8388608 | tf_op jit(solution)/shard_map/forward/pallas_call | solution.py:224
  11.2 2.6 %collective-permute-start.1 = (bf16[1,64,512]{2,1,0:T(8,128)(2,1)S(1)}, bf16[1,64,512]{2,1,0:T(8,128)(2,1)S(1)}, u32[]{:S(2)}, u32[]{:S(2)}) collective-permute-start(bf16[1,64,512]{2,1,0:T(8,128)(2,1)S(1)} %get-tuple-element.25), channel_id=1, source_target_pairs={{0,1},{1,0},{2,3},{3,2},{4,5},{5,4},{6,7},{7,6},{8,9},{9,8},{10,11... | collective-permute-start | bytes 196616 | tf_op jit(solution)/shard_map/ppermute | solution.py:248
  13.8 1.5 %collective-permute-start.32 = (s32[1]{0:T(128)}, s32[1]{0:T(128)}, u32[]{:S(2)}, u32[]{:S(2)}) collective-permute-start(s32[1]{0:T(128)} %param.9), channel_id=1, source_target_pairs={{0,16},{8,24},{16,0},{24,8},{1,17},{9,25},{17,1},{25,9},{2,18},{10... | collective-permute-start | bytes 20 | tf_op jit(solution)/shard_map/ppermute | solution.py:248
  15.8 1.5 %collective-permute-start.3 = (bf16[1,64,512]{2,1,0:T(8,128)(2,1)S(1)}, bf16[1,64,512]{2,1,0:T(8,128)(2,1)S(1)}, u32[]{:S(2)}, u32[]{:S(2)}) collective-permute-start(bf16[1,64,512]{2,1,0:T(8,128)(2,1)S(1)} %get-tuple-element.27), channel_id=1, source_target_pairs={{0,1},{1,0},{2,3},{3,2},{4,5},{5,4},{6,7},{7,6},{8,9},{9,8},{10,11... | collective-permute-start | bytes 196616 | tf_op jit(solution)/shard_map/ppermute | solution.py:248
  18.3 3.0 %collective-permute-done.3 = bf16[1,64,512]{2,1,0:T(8,128)(2,1)S(1)} collective-permute-done((bf16[1,64,512]{2,1,0:T(8,128)(2,1)S(1)}, bf16[1,64,512]{2,1,0:T(8,128)(2,1)S(1)}, u32[]{:S(2)}, u32[]{:S(2)}) %collective-permute-start.3) | collective-permute-done | bytes 65568 | tf_op jit(solution)/shard_map/ppermute | solution.py:248
  22.0 2.6 %collective-permute-start.2 = (bf16[64,512]{1,0:T(8,128)(2,1)S(1)}, bf16[64,512]{1,0:T(8,128)(2,1)S(1)}, u32[]{:S(2)}, u32[]{:S(2)}) collective-permute-start(bf16[64,512]{1,0:T(8,128)(2,1)S(1)} %fusion.4), channel_id=1, source_target_pairs={{0,4},{2,6},{4,0},{6,2},{1,5},{3,7},{5,1},{7,3},{8,12},{10,14},{12... | collective-permute-start | bytes 196616 | tf_op jit(solution)/shard_map/ppermute | solution.py:248
  24.7 1.6 %collective-permute-start.4 = (bf16[64,512]{1,0:T(8,128)(2,1)S(1)}, bf16[64,512]{1,0:T(8,128)(2,1)S(1)}, u32[]{:S(2)}, u32[]{:S(2)}) collective-permute-start(bf16[64,512]{1,0:T(8,128)(2,1)S(1)} %fusion.5), channel_id=1, source_target_pairs={{0,2},{2,0},{4,6},{6,4},{1,3},{3,1},{5,7},{7,5},{8,10},{10,8},{12,... | collective-permute-start | bytes 196616 | tf_op jit(solution)/shard_map/ppermute | solution.py:248
  26.5 1.3 col_table.1.refs_11_
  29.1 3.3 %collective-permute-done.6 = bf16[64,512]{1,0:T(8,128)(2,1)S(1)} collective-permute-done((bf16[64,512]{1,0:T(8,128)(2,1)S(1)}, bf16[64,512]{1,0:T(8,128)(2,1)S(1)}, u32[]{:S(2)}, u32[]{:S(2)}) %collective-permute-start.6) | collective-permute-done | bytes 65568 | tf_op jit(solution)/shard_map/ppermute | solution.py:248
  33.7 3.5 %collective-permute-start.9 = (bf16[64,512]{1,0:T(8,128)(2,1)S(1)}, bf16[64,512]{1,0:T(8,128)(2,1)S(1)}, u32[]{:S(2)}, u32[]{:S(2)}) collective-permute-start(bf16[64,512]{1,0:T(8,128)(2,1)S(1)} %fusion.2), channel_id=1, source_target_pairs={{0,6},{2,4},{4,2},{6,0},{1,7},{3,5},{5,3},{7,1},{8,14},{10,12},{12... | collective-permute-start | bytes 196616 | tf_op jit(solution)/shard_map/ppermute | solution.py:248
  38.3 2.3 %collective-permute-done.9 = bf16[64,512]{1,0:T(8,128)(2,1)S(1)} collective-permute-done((bf16[64,512]{1,0:T(8,128)(2,1)S(1)}, bf16[64,512]{1,0:T(8,128)(2,1)S(1)}, u32[]{:S(2)}, u32[]{:S(2)}) %collective-permute-start.9) | collective-permute-done | bytes 65568 | tf_op jit(solution)/shard_map/ppermute | solution.py:248
  40.6 2.2 %collective-permute-start.7 = (bf16[64,512]{1,0:T(8,128)(2,1)S(1)}, bf16[64,512]{1,0:T(8,128)(2,1)S(1)}, u32[]{:S(2)}, u32[]{:S(2)}) collective-permute-start(bf16[64,512]{1,0:T(8,128)(2,1)S(1)} %fusion.2), channel_id=1, source_target_pairs={{0,2},{2,0},{4,6},{6,4},{1,3},{3,1},{5,7},{7,5},{8,10},{10,8},{12,... | collective-permute-start | bytes 196616 | tf_op jit(solution)/shard_map/ppermute | solution.py:248
  43.3 1.7 %collective-permute-done.7 = bf16[64,512]{1,0:T(8,128)(2,1)S(1)} collective-permute-done((bf16[64,512]{1,0:T(8,128)(2,1)S(1)}, bf16[64,512]{1,0:T(8,128)(2,1)S(1)}, u32[]{:S(2)}, u32[]{:S(2)}) %collective-permute-start.7) | collective-permute-done | bytes 65568 | tf_op jit(solution)/shard_map/ppermute | solution.py:248
  45.9 1.2 collective-permute-start.12
  47.1 2.2 %collective-permute-done.13.refs_5_ = bf16[64,512]{1,0:T(8,128)(2,1)S(1)} collective-permute-done((bf16[64,512]{1,0:T(8,128)(2,1)S(1)}, bf16[64,512]{1,0:T(8,128)(2,1)S(1)}, u32[]{:S(2)}, u32[]{:S(2)}) %collective-permute-start.13) | collective-permute-done | bytes 65568 | tf_op jit(solution)/shard_map/ppermute | solution.py:248
  51.7 1.9 %collective-permute-done.11.refs_3_ = bf16[64,512]{1,0:T(8,128)(2,1)S(1)} collective-permute-done((bf16[64,512]{1,0:T(8,128)(2,1)S(1)}, bf16[64,512]{1,0:T(8,128)(2,1)S(1)}, u32[]{:S(2)}, u32[]{:S(2)}) %collective-permute-start.11) | collective-permute-done | bytes 65568 | tf_op jit(solution)/shard_map/ppermute | solution.py:248
  53.6 1.3 collective-permute-done.18.refs_10_
  58.3 1.2 own_slice.1
  59.6 1.4 %collective-permute-start.35 = (bf16[256,2048]{1,0:T(8,128)(2,1)S(1)}, bf16[256,2048]{1,0:T(8,128)(2,1)S(1)}, u32[]{:S(2)}, u32[]{:S(2)}) collective-permute-start(bf16[256,2048]{1,0:T(8,128)(2,1)S(1)} %own_slice.1), channel_id=1, source_target_pairs={{0,16},{8,24},{16,0},{24,8},{1,17},{9,25},{17,1},{25,9},{2,18},{10... | collective-permute-start | bytes 3145736 | tf_op jit(solution)/shard_map/ppermute | solution.py:248
  61.0 5.0 %collective-permute-done.29.refs_4_ = bf16[256,512]{1,0:T(8,128)(2,1)S(1)} collective-permute-done((bf16[256,512]{1,0:T(8,128)(2,1)S(1)}, bf16[256,512]{1,0:T(8,128)(2,1)S(1)}, u32[]{:S(2)}, u32[]{:S(2)}) %collective-permute-start.29) | collective-permute-done | bytes 262176 | tf_op jit(solution)/shard_map/ppermute | solution.py:248
  68.1 1.6 %row_tables.2.refs_11_.refs_3_.refs_7_ = bf16[2,512,512]{2,1,0:T(8,128)(2,1)S(1)} custom-call(s32[2]{0:T(128)S(1)} %pad_add_fusion.refs_0_), custom_call_target="tpu_custom_call" | custom-call | flops 10485760 | bytes 1048576 | tf_op jit(solution)/shard_map/row_tables/pallas_call | solution.py:341
  69.7 2.8 %shard_map.55 = (bf16[128,2048]{1,0:T(8,128)(2,1)S(1)}, bf16[512,512]{1,0:T(8,128)(2,1)S(1)}, bf16[512,512]{1,0:T(8,128)(2,1)S(1)}) custom-call(s32[8,16]{1,0:T(8,128)S(1)} %copy-done.2, bf16[256,512]{1,0:T(8,128)(2,1)S(1)} %pad_maximum_fusion.refs_1_, bf16[64,512]{1,0:T(8,128)(2,1)S(1)} %collective-permute-done.10.refs_2_, ...), custom_call_target="tpu_custom_call" | custom-call | flops 671088640 | bytes 1572864 | tf_op jit(solution)/shard_map/pallas_call | solution.py:470
  72.5 2.6 %shard_map.56 = (bf16[64,2048]{1,0:T(8,128)(2,1)S(1)}, bf16[64,2048]{1,0:T(8,128)(2,1)S(1)}) custom-call(s32[8,16]{1,0:T(8,128)S(1)} %copy-done.2, bf16[512,512]{1,0:T(8,128)(2,1)S(1)} %get-tuple-element.31.refs_1_, bf16[512,512]{1,0:T(8,128)(2,1)S(1)} %get-tuple-element.32.refs_2_, bf16[2,512,512]{2,1,0:T(8,128)(2,1)S(1)} %row_tables.2.refs_11_.refs_3_.refs_7_, ...), custom_call_target="tpu_custom_call" | custom-call | flops 671088640 | bytes 1572864 | tf_op jit(solution)/shard_map/pallas_call | solution.py:470
  76.1 1.3 pad_add_fusion.1.refs_0_
  77.4 1.6 %row_tables.3.refs_8_ = bf16[2,512,512]{2,1,0:T(8,128)(2,1)S(1)} custom-call(s32[2]{0:T(128)S(1)} %pad_add_fusion.1.refs_0_), custom_call_target="tpu_custom_call" | custom-call | flops 10485760 | bytes 1048576 | tf_op jit(solution)/shard_map/row_tables/pallas_call | solution.py:341
  80.2 5.5 %collective-permute-done.35.refs_15_ = bf16[256,2048]{1,0:T(8,128)(2,1)S(1)} collective-permute-done((bf16[256,2048]{1,0:T(8,128)(2,1)S(1)}, bf16[256,2048]{1,0:T(8,128)(2,1)S(1)}, u32[]{:S(2)}, u32[]{:S(2)}) %collective-permute-start.35) | collective-permute-done | bytes 1048608 | tf_op jit(solution)/shard_map/ppermute | solution.py:248
  85.7 1.4 %collective-permute-start.24 = (bf16[128,2048]{1,0:T(8,128)(2,1)S(1)}, bf16[128,2048]{1,0:T(8,128)(2,1)S(1)}, u32[]{:S(2)}, u32[]{:S(2)}) collective-permute-start(bf16[128,2048]{1,0:T(8,128)(2,1)S(1)} %get-tuple-element.34), channel_id=1, source_target_pairs={{0,16},{8,24},{16,0},{24,8},{1,17},{9,25},{17,1},{25,9},{2,18},{10... | collective-permute-start | bytes 1572872 | tf_op jit(solution)/shard_map/ppermute | solution.py:248
  87.1 20.0 %collective-permute-done.36.refs_16_ = bf16[256,2048]{1,0:T(8,128)(2,1)S(1)} collective-permute-done((bf16[256,2048]{1,0:T(8,128)(2,1)S(1)}, bf16[256,2048]{1,0:T(8,128)(2,1)S(1)}, u32[]{:S(2)}, u32[]{:S(2)}) %collective-permute-start.36) | collective-permute-done | bytes 1048608 | tf_op jit(solution)/shard_map/ppermute | solution.py:248
  107.0 5.2 %shard_map.57 = (bf16[128,2048]{1,0:T(8,128)(2,1)S(1)}, bf16[128,2048]{1,0:T(8,128)(2,1)S(1)}, bf16[512,512]{1,0:T(8,128)(2,1)}, bf16[512,512]{1,0:T(8,128)(2,1)}) custom-call(s32[8,16]{1,0:T(8,128)S(1)} %copy-done.2, bf16[512,512]{1,0:T(8,128)(2,1)S(1)} %get-tuple-element.31.refs_1_, bf16[512,512]{1,0:T(8,128)(2,1)S(1)} %get-tuple-element.32.refs_2_, ...), custom_call_target="tpu_custom_call" | custom-call | flops 2684354560 | bytes 3145728 | tf_op jit(solution)/shard_map/pallas_call | solution.py:470
  113.9 15.8 %collective-permute-done.24 = bf16[128,2048]{1,0:T(8,128)(2,1)S(1)} collective-permute-done((bf16[128,2048]{1,0:T(8,128)(2,1)S(1)}, bf16[128,2048]{1,0:T(8,128)(2,1)S(1)}, u32[]{:S(2)}, u32[]{:S(2)}) %collective-permute-start.24) | collective-permute-done | bytes 524320 | tf_op jit(solution)/shard_map/ppermute | solution.py:248
  130.6 1.3 %shard_map.58.refs_4_ = bf16[1024,2048]{1,0:T(8,128)(2,1)} custom-call(bf16[128,2048]{1,0:T(8,128)(2,1)S(1)} %get-tuple-element.37.refs_0_, bf16[128,2048]{1,0:T(8,128)(2,1)S(1)} %collective-permute-done.37.refs_1_, bf16[128,2048]{1,0:T(8,128)(2,1)S(1)} %get-tuple-element.38.refs_2_, bf16[128,2048]{1,0:T(8,128)(2,1)S(1)} %collective-permute-done.38.refs_3_), custom_call_target="tpu_custom_call" | custom-call | bytes 2097152 | tf_op jit(solution)/shard_map/pallas_call | solution.py:514
  131.9 1.2 shard_map.59.refs_2_
  (73 shorter events, 21.9 us)
Async XLA Ops:
  0.0 67.3 %collective-permute-start.21 = (bf16[1,1024,2048]{2,1,0:T(8,128)(2,1)}, bf16[1,1024,2048]{2,1,0:T(8,128)(2,1)S(1)}, u32[]{:S(2)}, u32[]{:S(2)}) collective-permute-start(bf16[1,1024,2048]{2,1,0:T(8,128)(2,1)} %refs_13_.1), channel_id=1, source_target_pairs={{0,8},{8,0},{16,24},{24,16},{1,9},{9,1},{17,25},{25,17},{2,10},{10... | collective-permute-start | bytes 12582920 | tf_op jit(solution)/shard_map/ppermute | solution.py:248
  11.2 6.1 %collective-permute-start.1 = (bf16[1,64,512]{2,1,0:T(8,128)(2,1)S(1)}, bf16[1,64,512]{2,1,0:T(8,128)(2,1)S(1)}, u32[]{:S(2)}, u32[]{:S(2)}) collective-permute-start(bf16[1,64,512]{2,1,0:T(8,128)(2,1)S(1)} %get-tuple-element.25), channel_id=1, source_target_pairs={{0,1},{1,0},{2,3},{3,2},{4,5},{5,4},{6,7},{7,6},{8,9},{9,8},{10,11... | collective-permute-start | bytes 196616 | tf_op jit(solution)/shard_map/ppermute | solution.py:248
  13.8 10.9 %collective-permute-start.32 = (s32[1]{0:T(128)}, s32[1]{0:T(128)}, u32[]{:S(2)}, u32[]{:S(2)}) collective-permute-start(s32[1]{0:T(128)} %param.9), channel_id=1, source_target_pairs={{0,16},{8,24},{16,0},{24,8},{1,17},{9,25},{17,1},{25,9},{2,18},{10... | collective-permute-start | bytes 20 | tf_op jit(solution)/shard_map/ppermute | solution.py:248
  15.3 11.0 %collective-permute-start = (bf16[1,64,512]{2,1,0:T(8,128)(2,1)S(1)}, bf16[1,64,512]{2,1,0:T(8,128)(2,1)S(1)}, u32[]{:S(2)}, u32[]{:S(2)}) collective-permute-start(bf16[1,64,512]{2,1,0:T(8,128)(2,1)S(1)} %get-tuple-element.23), channel_id=1, source_target_pairs={{0,1},{1,0},{2,3},{3,2},{4,5},{5,4},{6,7},{7,6},{8,9},{9,8},{10,11... | collective-permute-start | bytes 196616 | tf_op jit(solution)/shard_map/ppermute | solution.py:248
  15.8 5.5 %collective-permute-start.3 = (bf16[1,64,512]{2,1,0:T(8,128)(2,1)S(1)}, bf16[1,64,512]{2,1,0:T(8,128)(2,1)S(1)}, u32[]{:S(2)}, u32[]{:S(2)}) collective-permute-start(bf16[1,64,512]{2,1,0:T(8,128)(2,1)S(1)} %get-tuple-element.27), channel_id=1, source_target_pairs={{0,1},{1,0},{2,3},{3,2},{4,5},{5,4},{6,7},{7,6},{8,9},{9,8},{10,11... | collective-permute-start | bytes 196616 | tf_op jit(solution)/shard_map/ppermute | solution.py:248
  17.3 4.7 %collective-permute-start.5 = (bf16[1,64,512]{2,1,0:T(8,128)(2,1)S(1)}, bf16[1,64,512]{2,1,0:T(8,128)(2,1)S(1)}, u32[]{:S(2)}, u32[]{:S(2)}) collective-permute-start(bf16[1,64,512]{2,1,0:T(8,128)(2,1)S(1)} %get-tuple-element.29), channel_id=1, source_target_pairs={{0,1},{1,0},{2,3},{3,2},{4,5},{5,4},{6,7},{7,6},{8,9},{9,8},{10,11... | collective-permute-start | bytes 196616 | tf_op jit(solution)/shard_map/ppermute | solution.py:248
  21.3 45.0 %collective-permute-start.20 = (bf16[2048,512]{1,0:T(8,128)(2,1)S(1)}, bf16[2048,512]{1,0:T(8,128)(2,1)S(1)}, u32[]{:S(2)}, u32[]{:S(2)}) collective-permute-start(bf16[2048,512]{1,0:T(8,128)(2,1)S(1)} %get-tuple-element.30.refs_12_.refs_4_.refs_9_), channel_id=1, source_target_pairs={{0,8},{8,0},{16,24},{24,16},{1,9},{9,1},{17,25},{25,17},{2,10},{10... | collective-permute-start | bytes 6291464 | tf_op jit(solution)/shard_map/ppermute | solution.py:248
  22.0 6.5 %collective-permute-start.2 = (bf16[64,512]{1,0:T(8,128)(2,1)S(1)}, bf16[64,512]{1,0:T(8,128)(2,1)S(1)}, u32[]{:S(2)}, u32[]{:S(2)}) collective-permute-start(bf16[64,512]{1,0:T(8,128)(2,1)S(1)} %fusion.4), channel_id=1, source_target_pairs={{0,4},{2,6},{4,0},{6,2},{1,5},{3,7},{5,1},{7,3},{8,12},{10,14},{12... | collective-permute-start | bytes 196616 | tf_op jit(solution)/shard_map/ppermute | solution.py:248
  24.7 4.3 %collective-permute-start.4 = (bf16[64,512]{1,0:T(8,128)(2,1)S(1)}, bf16[64,512]{1,0:T(8,128)(2,1)S(1)}, u32[]{:S(2)}, u32[]{:S(2)}) collective-permute-start(bf16[64,512]{1,0:T(8,128)(2,1)S(1)} %fusion.5), channel_id=1, source_target_pairs={{0,2},{2,0},{4,6},{6,4},{1,3},{3,1},{5,7},{7,5},{8,10},{10,8},{12,... | collective-permute-start | bytes 196616 | tf_op jit(solution)/shard_map/ppermute | solution.py:248
  26.3 6.1 %collective-permute-start.6 = (bf16[64,512]{1,0:T(8,128)(2,1)S(1)}, bf16[64,512]{1,0:T(8,128)(2,1)S(1)}, u32[]{:S(2)}, u32[]{:S(2)}) collective-permute-start(bf16[64,512]{1,0:T(8,128)(2,1)S(1)} %fusion.6), channel_id=1, source_target_pairs={{0,6},{2,4},{4,2},{6,0},{1,7},{3,5},{5,3},{7,1},{8,14},{10,12},{12... | collective-permute-start | bytes 196616 | tf_op jit(solution)/shard_map/ppermute | solution.py:248
  28.6 3.9 %collective-permute-start.19 = (s32[1]{0:T(128)}, s32[1]{0:T(128)}, u32[]{:S(2)}, u32[]{:S(2)}) collective-permute-start(s32[1]{0:T(128)} %param.9), channel_id=1, source_target_pairs={{0,8},{8,0},{16,24},{24,16},{1,9},{9,1},{17,25},{25,17},{2,10},{10... | collective-permute-start | bytes 20 | tf_op jit(solution)/shard_map/ppermute | solution.py:248
  29.0 78.0 %collective-permute-start.34 = (bf16[2048,512]{1,0:T(8,128)(2,1)S(1)}, bf16[2048,512]{1,0:T(8,128)(2,1)S(1)}, u32[]{:S(2)}, u32[]{:S(2)}) collective-permute-start(bf16[2048,512]{1,0:T(8,128)(2,1)S(1)} %col_table.1.refs_11_), channel_id=1, source_target_pairs={{0,8},{8,0},{16,24},{24,16},{1,9},{9,1},{17,25},{25,17},{2,10},{10... | collective-permute-start | bytes 6291464 | tf_op jit(solution)/shard_map/ppermute | solution.py:248
  32.4 4.8 %collective-permute-start.10 = (bf16[64,512]{1,0:T(8,128)(2,1)S(1)}, bf16[64,512]{1,0:T(8,128)(2,1)S(1)}, u32[]{:S(2)}, u32[]{:S(2)}) collective-permute-start(bf16[64,512]{1,0:T(8,128)(2,1)S(1)} %fusion.2), channel_id=1, source_target_pairs={{0,1},{1,0},{2,3},{3,2},{4,5},{5,4},{6,7},{7,6},{8,9},{9,8},{10,11... | collective-permute-start | bytes 196616 | tf_op jit(solution)/shard_map/ppermute | solution.py:248
  33.7 6.9 %collective-permute-start.9 = (bf16[64,512]{1,0:T(8,128)(2,1)S(1)}, bf16[64,512]{1,0:T(8,128)(2,1)S(1)}, u32[]{:S(2)}, u32[]{:S(2)}) collective-permute-start(bf16[64,512]{1,0:T(8,128)(2,1)S(1)} %fusion.2), channel_id=1, source_target_pairs={{0,6},{2,4},{4,2},{6,0},{1,7},{3,5},{5,3},{7,1},{8,14},{10,12},{12... | collective-permute-start | bytes 196616 | tf_op jit(solution)/shard_map/ppermute | solution.py:248
  37.2 6.1 %collective-permute-start.8 = (bf16[64,512]{1,0:T(8,128)(2,1)S(1)}, bf16[64,512]{1,0:T(8,128)(2,1)S(1)}, u32[]{:S(2)}, u32[]{:S(2)}) collective-permute-start(bf16[64,512]{1,0:T(8,128)(2,1)S(1)} %fusion.2), channel_id=1, source_target_pairs={{0,4},{2,6},{4,0},{6,2},{1,5},{3,7},{5,1},{7,3},{8,12},{10,14},{12... | collective-permute-start | bytes 196616 | tf_op jit(solution)/shard_map/ppermute | solution.py:248
  40.6 4.4 %collective-permute-start.7 = (bf16[64,512]{1,0:T(8,128)(2,1)S(1)}, bf16[64,512]{1,0:T(8,128)(2,1)S(1)}, u32[]{:S(2)}, u32[]{:S(2)}) collective-permute-start(bf16[64,512]{1,0:T(8,128)(2,1)S(1)} %fusion.2), channel_id=1, source_target_pairs={{0,2},{2,0},{4,6},{6,4},{1,3},{3,1},{5,7},{7,5},{8,10},{10,8},{12,... | collective-permute-start | bytes 196616 | tf_op jit(solution)/shard_map/ppermute | solution.py:248
  45.0 4.3 %collective-permute-start.13 = (bf16[64,512]{1,0:T(8,128)(2,1)S(1)}, bf16[64,512]{1,0:T(8,128)(2,1)S(1)}, u32[]{:S(2)}, u32[]{:S(2)}) collective-permute-start(bf16[64,512]{1,0:T(8,128)(2,1)S(1)} %collective-permute-done.9), channel_id=1, source_target_pairs={{0,1},{1,0},{2,3},{3,2},{4,5},{5,4},{6,7},{7,6},{8,9},{9,8},{10,11... | collective-permute-start | bytes 196616 | tf_op jit(solution)/shard_map/ppermute | solution.py:248
  45.9 4.9 %collective-permute-start.12 = (bf16[64,512]{1,0:T(8,128)(2,1)S(1)}, bf16[64,512]{1,0:T(8,128)(2,1)S(1)}, u32[]{:S(2)}, u32[]{:S(2)}) collective-permute-start(bf16[64,512]{1,0:T(8,128)(2,1)S(1)} %collective-permute-done.8), channel_id=1, source_target_pairs={{0,1},{1,0},{2,3},{3,2},{4,5},{5,4},{6,7},{7,6},{8,9},{9,8},{10,11... | collective-permute-start | bytes 196616 | tf_op jit(solution)/shard_map/ppermute | solution.py:248
  49.3 4.3 %collective-permute-start.11 = (bf16[64,512]{1,0:T(8,128)(2,1)S(1)}, bf16[64,512]{1,0:T(8,128)(2,1)S(1)}, u32[]{:S(2)}, u32[]{:S(2)}) collective-permute-start(bf16[64,512]{1,0:T(8,128)(2,1)S(1)} %collective-permute-done.7), channel_id=1, source_target_pairs={{0,1},{1,0},{2,3},{3,2},{4,5},{5,4},{6,7},{7,6},{8,9},{9,8},{10,11... | collective-permute-start | bytes 196616 | tf_op jit(solution)/shard_map/ppermute | solution.py:248
  50.8 6.7 %collective-permute-start.28 = (bf16[256,512]{1,0:T(8,128)(2,1)S(1)}, bf16[256,512]{1,0:T(8,128)(2,1)S(1)}, u32[]{:S(2)}, u32[]{:S(2)}) collective-permute-start(bf16[256,512]{1,0:T(8,128)(2,1)S(1)} %pad_maximum_fusion.refs_1_), channel_id=1, source_target_pairs={{0,16},{8,24},{16,0},{24,8},{1,17},{9,25},{17,1},{25,9},{2,18},{10... | collective-permute-start | bytes 786440 | tf_op jit(solution)/shard_map/ppermute | solution.py:248
  57.5 8.6 %collective-permute-start.29 = (bf16[256,512]{1,0:T(8,128)(2,1)S(1)}, bf16[256,512]{1,0:T(8,128)(2,1)S(1)}, u32[]{:S(2)}, u32[]{:S(2)}) collective-permute-start(bf16[256,512]{1,0:T(8,128)(2,1)S(1)} %collective-permute-done.28.refs_3_), channel_id=1, source_target_pairs={{0,1},{1,0},{2,3},{3,2},{4,5},{5,4},{6,7},{7,6},{8,9},{9,8},{10,11... | collective-permute-start | bytes 786440 | tf_op jit(solution)/shard_map/ppermute | solution.py:248
  59.6 26.1 %collective-permute-start.35 = (bf16[256,2048]{1,0:T(8,128)(2,1)S(1)}, bf16[256,2048]{1,0:T(8,128)(2,1)S(1)}, u32[]{:S(2)}, u32[]{:S(2)}) collective-permute-start(bf16[256,2048]{1,0:T(8,128)(2,1)S(1)} %own_slice.1), channel_id=1, source_target_pairs={{0,16},{8,24},{16,0},{24,8},{1,17},{9,25},{17,1},{25,9},{2,18},{10... | collective-permute-start | bytes 3145736 | tf_op jit(solution)/shard_map/ppermute | solution.py:248
  66.1 41.0 %collective-permute-start.36 = (bf16[256,2048]{1,0:T(8,128)(2,1)S(1)}, bf16[256,2048]{1,0:T(8,128)(2,1)S(1)}, u32[]{:S(2)}, u32[]{:S(2)}) collective-permute-start(bf16[256,2048]{1,0:T(8,128)(2,1)S(1)} %get-tuple-element.36), channel_id=1, source_target_pairs={{0,24},{8,16},{16,8},{24,0},{1,25},{9,17},{17,9},{25,1},{2,26},{10... | collective-permute-start | bytes 3145736 | tf_op jit(solution)/shard_map/ppermute | solution.py:248
  66.3 8.8 %collective-permute-start.30 = (bf16[256,512]{1,0:T(8,128)(2,1)S(1)}, bf16[256,512]{1,0:T(8,128)(2,1)S(1)}, u32[]{:S(2)}, u32[]{:S(2)}) collective-permute-start(bf16[256,512]{1,0:T(8,128)(2,1)S(1)} %collective-permute-done.28.refs_3_), channel_id=1, source_target_pairs={{0,8},{8,0},{16,24},{24,16},{1,9},{9,1},{17,25},{25,17},{2,10},{10... | collective-permute-start | bytes 786440 | tf_op jit(solution)/shard_map/ppermute | solution.py:248
  67.3 11.7 %collective-permute-start.31 = (bf16[256,512]{1,0:T(8,128)(2,1)S(1)}, bf16[256,512]{1,0:T(8,128)(2,1)S(1)}, u32[]{:S(2)}, u32[]{:S(2)}) collective-permute-start(bf16[256,512]{1,0:T(8,128)(2,1)S(1)} %collective-permute-done.29.refs_4_), channel_id=1, source_target_pairs={{0,8},{8,0},{16,24},{24,16},{1,9},{9,1},{17,25},{25,17},{2,10},{10... | collective-permute-start | bytes 786440 | tf_op jit(solution)/shard_map/ppermute | solution.py:248
  75.1 38.7 %collective-permute-start.26 = (bf16[64,2048]{1,0:T(8,128)(2,1)S(1)}, bf16[64,2048]{1,0:T(8,128)(2,1)S(1)}, u32[]{:S(2)}, u32[]{:S(2)}) collective-permute-start(bf16[64,2048]{1,0:T(8,128)(2,1)S(1)} %get-tuple-element.35), channel_id=1, source_target_pairs={{0,16},{8,24},{16,0},{24,8},{1,17},{9,25},{17,1},{25,9},{2,18},{10... | collective-permute-start | bytes 786440 | tf_op jit(solution)/shard_map/ppermute | solution.py:248
  79.0 50.9 %collective-permute-start.22 = (bf16[64,2048]{1,0:T(8,128)(2,1)S(1)}, bf16[64,2048]{1,0:T(8,128)(2,1)S(1)}, u32[]{:S(2)}, u32[]{:S(2)}) collective-permute-start(bf16[64,2048]{1,0:T(8,128)(2,1)S(1)} %get-tuple-element.33), channel_id=1, source_target_pairs={{0,16},{8,24},{16,0},{24,8},{1,17},{9,25},{17,1},{25,9},{2,18},{10... | collective-permute-start | bytes 786440 | tf_op jit(solution)/shard_map/ppermute | solution.py:248
  85.7 44.0 %collective-permute-start.24 = (bf16[128,2048]{1,0:T(8,128)(2,1)S(1)}, bf16[128,2048]{1,0:T(8,128)(2,1)S(1)}, u32[]{:S(2)}, u32[]{:S(2)}) collective-permute-start(bf16[128,2048]{1,0:T(8,128)(2,1)S(1)} %get-tuple-element.34), channel_id=1, source_target_pairs={{0,16},{8,24},{16,0},{24,8},{1,17},{9,25},{17,1},{25,9},{2,18},{10... | collective-permute-start | bytes 1572872 | tf_op jit(solution)/shard_map/ppermute | solution.py:248
  112.3 18.3 %collective-permute-start.37 = (bf16[128,2048]{1,0:T(8,128)(2,1)S(1)}, bf16[128,2048]{1,0:T(8,128)(2,1)S(1)}, u32[]{:S(2)}, u32[]{:S(2)}) collective-permute-start(bf16[128,2048]{1,0:T(8,128)(2,1)S(1)} %get-tuple-element.37.refs_0_), channel_id=1, source_target_pairs={{0,8},{8,0},{16,24},{24,16},{1,9},{9,1},{17,25},{25,17},{2,10},{10... | collective-permute-start | bytes 1572872 | tf_op jit(solution)/shard_map/ppermute | solution.py:248
  113.3 17.3 %collective-permute-start.38 = (bf16[128,2048]{1,0:T(8,128)(2,1)S(1)}, bf16[128,2048]{1,0:T(8,128)(2,1)S(1)}, u32[]{:S(2)}, u32[]{:S(2)}) collective-permute-start(bf16[128,2048]{1,0:T(8,128)(2,1)S(1)} %get-tuple-element.38.refs_2_), channel_id=1, source_target_pairs={{0,8},{8,0},{16,24},{24,16},{1,9},{9,1},{17,25},{25,17},{2,10},{10... | collective-permute-start | bytes 1572872 | tf_op jit(solution)/shard_map/ppermute | solution.py:248
  113.8 18.1 %collective-permute-start.27 = (bf16[64,2048]{1,0:T(8,128)(2,1)S(1)}, bf16[64,2048]{1,0:T(8,128)(2,1)S(1)}, u32[]{:S(2)}, u32[]{:S(2)}) collective-permute-start(bf16[64,2048]{1,0:T(8,128)(2,1)S(1)} %add_convert_fusion.1.refs_2_), channel_id=1, source_target_pairs={{0,8},{8,0},{16,24},{24,16},{1,9},{9,1},{17,25},{25,17},{2,10},{10... | collective-permute-start | bytes 786440 | tf_op jit(solution)/shard_map/ppermute | solution.py:248
  130.0 3.1 %collective-permute-start.23 = (bf16[64,2048]{1,0:T(8,128)(2,1)S(1)}, bf16[64,2048]{1,0:T(8,128)(2,1)S(1)}, u32[]{:S(2)}, u32[]{:S(2)}) collective-permute-start(bf16[64,2048]{1,0:T(8,128)(2,1)S(1)} %add_convert_fusion.2.refs_0_), channel_id=1, source_target_pairs={{0,8},{8,0},{16,24},{24,16},{1,9},{9,1},{17,25},{25,17},{2,10},{10... | collective-permute-start | bytes 786440 | tf_op jit(solution)/shard_map/ppermute | solution.py:248
  (10 other events, 102.8 us)

commit v3 on v2

--- a/solution.py
+++ b/solution.py
@@ -53,8 +53,8 @@
     block = 256
     focal = 2.0 * iota((16, lane_count), 1) + 1.0 if lanes is None else lanes
     step = iota((16, lane_count), 0)
-    fine = unit_phasor(2.0 * step * focal, jnp.full((16, lane_count), period, F32))
-    mid = unit_phasor(32.0 * step * focal, jnp.full((16, lane_count), period, F32))
+    fine = unit_phasor(2.0 * step * focal, jnp.broadcast_to(period, (16, lane_count)))
+    mid = unit_phasor(32.0 * step * focal, jnp.broadcast_to(period, (16, lane_count)))
     for b in range(16):
         re, im = turn((mid[0][b : b + 1], mid[1][b : b + 1]), fine)
         fine_ref[0, 16 * b : 16 * b + 16, :] = re
@@ -65,7 +65,7 @@
     focal_top = 2.0 * iota((top, lane_count), 1) + 1.0 if lanes is None else jnp.broadcast_to(lanes[:1], (top, lane_count))
     coarse = unit_phasor(
         (start + 2.0 * block * iota((top, lane_count), 0)) * focal_top,
-        jnp.full((top, lane_count), period, F32),
+        jnp.broadcast_to(period, (top, lane_count)),
     )
     for a in range(count):
         for part in range(0, block, 64):
@@ -81,7 +81,7 @@
     shape = (focal_count, 128)
     focal = 2.0 * (focal_first + iota(shape, 0)) + 1.0
     lane = iota(shape, 1)
-    full = jnp.full(shape, period, F32)
+    full = jnp.broadcast_to(period, shape)
     fine = unit_phasor(2.0 * lane * focal, full)
     fine_ref[0, :focal_count, :128] = fine[0]
     fine_ref[1, :focal_count, :128] = fine[1]
@@ -110,7 +110,7 @@
 
 
 def slice_rows(source, target, sem, which, begin):
-    span = pl.ds(pl.multiple_of(which * (source.shape[1] // 2) + begin, target.shape[0]), target.shape[0])
+    span = pl.ds(pl.multiple_of(which * (source.shape[1] // 2) + begin, 16), target.shape[0])
     return pltpu.make_async_copy(source.at[0, span, :], target, sem)
 
 
@@ -130,7 +130,7 @@
     half_at = lax.rem(lax.axis_index("wl"), 2)
     slice_copy = slice_rows(inc_ref, slice_ref, sems.at[rows // block], 1 - half_at, begin)
     slice_copy.start()
-    period = quarter_period(index_ref[0])
+    period = quarter_period(index_ref[...])
 
     def write_col(at, amount, re, im):
         col_tab[at : at + amount, :HALF] = re
@@ -156,7 +156,7 @@
         inner[at : at + block, :M] = prod[:block].astype(BF16)
         inner[at : at + block, M:] = prod[block:].astype(BF16)
 
-    charge = charge_ref[0]
+    charge = charge_ref[...]
     even = jnp.where(charge % 2 == 0, 1.0, 0.0).astype(F32)
     odd = 1.0 - even
     scale = 4.0 / (extent * M)
@@ -220,10 +220,10 @@
     def kernel(*refs):
         forward_kernel(*refs, rows=rows, cols=cols, n_row=n_row, groups=groups, begin=begin)
 
-    smem = pl.BlockSpec(memory_space=pltpu.SMEM)
+    vmem = pl.BlockSpec(memory_space=pltpu.VMEM)
     outs = pl.pallas_call(
         kernel,
-        in_specs=[smem, smem, smem] + [pl.BlockSpec(memory_space=pltpu.HBM)] * 2,
+        in_specs=[vmem, vmem, pl.BlockSpec(memory_space=pltpu.SMEM)] + [pl.BlockSpec(memory_space=pltpu.HBM)] * 2,
         out_specs=[pl.BlockSpec(memory_space=pltpu.VMEM)] * len(out_shape),
         out_shape=out_shape,
         scratch_shapes=[
@@ -239,7 +239,7 @@
             flops=2 * rows * 2 * M * (cols + M), bytes_accessed=4 * rows * cols, transcendentals=0
         ),
         name="forward",
-    )(index, charge, tiles, in_hbm(cotangent), in_hbm(incident))
+    )(index.reshape(1, 1), charge.reshape(1, 1), tiles, in_hbm(cotangent), in_hbm(incident))
     return outs[:-2], outs[-2], outs[-1]
 
 
@@ -377,7 +377,7 @@
     )(index)
 
 
-def backward_kernel(tiles_ref, *refs, counts, wave_ids, part_first, chunks, tile_size, rows):
+def backward_kernel(tiles_ref, *refs, counts, wave_ids, part_first, chunks, tile_size, rows, emit):
     waves = len(counts)
     total_pieces = sum(counts)
     sources, refs = refs[:total_pieces], refs[total_pieces:]
@@ -386,14 +386,15 @@
     col_tabs, refs = refs[:waves], refs[waves:]
     incidents, refs = refs[:waves], refs[waves:]
     outs, refs = refs[: len(chunks)], refs[len(chunks) :]
-    matrices, (held, sems) = list(refs[:-2]), refs[-2:]
+    held, sems = refs[emit : emit + 2]
+    matrices = list(refs[:emit] + refs[emit + 2 :])
     half_at = lax.rem(lax.axis_index("wl"), 2)
     first = chunks[0][0]
     copies = []
     for k, (at, amount) in enumerate(chunks):
         for w in range(waves):
             if part_first[w] is None:
-                span = pl.ds(pl.multiple_of(half_at * rows + at, amount), amount)
+                span = pl.ds(pl.multiple_of(half_at * rows + at, 16), amount)
                 source = incidents[w].at[0, span, :]
             else:
                 source = incidents[w].at[pl.ds(at - part_first[w], amount), :]
@@ -434,18 +435,19 @@
             term = back * held[w, :, span].astype(F32)
             total = term if total is None else total + term
         for out, (at, size) in zip(outs, chunks):
-            for h in range(0, size, tile_size):
-                high = min(h + tile_size, size)
-                mask = live_row(tiles_ref, (half_at * rows + at + h) // tile_size, cols)[:, span]
-                out[h:high, span] = (total[at - first + h : at - first + high] * mask).astype(BF16)
-
-
-def backward(tiles, waves, chunks, tile_size, rows):
+            borders = [at] + list(range((at // tile_size + 1) * tile_size, at + size, tile_size)) + [at + size]
+            for low, high in zip(borders, borders[1:]):
+                mask = live_row(tiles_ref, half_at * (rows // tile_size) + low // tile_size, cols)[:, span]
+                out[low - at : high - at, span] = (total[low - first : high - first] * mask).astype(BF16)
+
+
+def backward(tiles, waves, chunks, tile_size, rows, keep=False):
     cols = tiles.shape[1] * tile_size
     flat = [piece for wave in waves for piece in wave[0]]
     amount = sum(n for _, n in chunks)
     counts = [len(wave[0]) for wave in waves]
-    emit = sum(count > 1 for count in counts)
+    built = sum(count > 1 for count in counts)
+    emit = built if keep else 0
     tables = []
     for wave in waves:
         if not any(wave[1] is table for table in tables):
@@ -461,6 +463,7 @@
             chunks=chunks,
             tile_size=tile_size,
             rows=rows,
+            emit=emit,
         )
 
     vmem = pl.BlockSpec(memory_space=pltpu.VMEM)
@@ -477,7 +480,8 @@
         scratch_shapes=[
             pltpu.VMEM((len(waves), amount, cols), BF16),
             pltpu.SemaphoreType.DMA((len(chunks), len(waves))),
-        ],
+        ]
+        + [pltpu.VMEM((M, M), BF16)] * (built - emit),
         compiler_params=pltpu.CompilerParams(vmem_limit_bytes=24 << 20),
         cost_estimate=pl.CostEstimate(
             flops=2 * len(waves) * amount * M * (cols + M), bytes_accessed=6 * amount * cols, transcendentals=0
@@ -494,7 +498,7 @@
     for k, (at, amount) in enumerate(chunks):
         for side in range(2):
             where = half_at if side == 0 else 1 - half_at
-            target = out.at[pl.ds(pl.multiple_of(where * rows + at, amount), amount), :]
+            target = out.at[pl.ds(pl.multiple_of(where * rows + at, 16), amount), :]
             copies.append(pltpu.make_async_copy(sources[2 * k + side], target, sems.at[k, side]))
     for copy in copies:
         copy.start()
@@ -543,8 +547,8 @@
     )(in_hbm(incident))
 
 
-EXCHANGED = (2, 1, 1)
-REPEATED = (2, 2)
+BOUNDS = (0, 4, 7, 9, 13, 16)
+EXCHANGED = 3
 
 
 def all_steps(cotangent, incident, tiles, charge, wl_index):
@@ -553,13 +557,9 @@
     n_col = lax.axis_size("col")
     tile_size = rows // tiles.shape[0]
     half = rows // 2
-    unit = half // 8
-    chunks = []
-    at = 0
-    for size in EXCHANGED + REPEATED:
-        chunks.append((at, size * unit))
-        at += size * unit
-    n_first = len(EXCHANGED)
+    bounds = [half * bound // 16 // 16 * 16 for bound in BOUNDS]
+    chunks = [(low, high - low) for low, high in zip(bounds, bounds[1:])]
+    n_first = EXCHANGED
     split = chunks[n_first][0]
 
     inc_straight = swap(own_slice(incident, split), "wl", 2)
@@ -595,7 +595,7 @@
 
     own = (aligned(pieces), row_near, 0, col_own, incident, None)
     mate = (aligned(pieces_core), row_near, 1, col_core, inc_core, None)
-    first, matrices = backward(tiles, [own, mate], chunks[:1], tile_size, half)
+    first, matrices = backward(tiles, [own, mate], chunks[:1], tile_size, half, keep=True)
     if len(matrices) == 2:
         own = ([matrices[0]],) + own[1:]
         mate = ([matrices[1]],) + mate[1:]

time: 134 us -> 132 us (0.985)
  waiting for transfers between devices: 68 us -> 63.9 us
    ppermute x39, waiting for transfers between devices: 68 us -> 63.9 us  [swap(): return lax.ppermute(value, axis, [(i, i ^ bits) for i in range(size)])]
  transfers between devices with their start and end apart: 39 -> 39, of which waited for: 20 -> 23; matrix products, arithmetic and copies ran while one was open for 2% -> 2% of each run, Pallas kernels for 21% -> 21%
where the time goes in v3:
time: 132 us
  waiting for transfers between devices  63.9 us (48%)
  starting transfers between devices  34.2 us (26%)
  Pallas kernels  29 us (22%)
  other arithmetic  2.4 us (2%)
  between operations  1.72 us (1%)
    ppermute x39, waiting for transfers between devices, swap(): return lax.ppermute(value, axis, [(i, i ^ bits) for i in range(size)])  63.9 us
    ppermute x39, starting transfers between devices, swap(): return lax.ppermute(value, axis, [(i, i ^ bits) for i in range(size)])  34.2 us
    pallas_call x3, Pallas kernels, backward(): pl.pallas_call(kernel, in_specs=[pl.BlockSpec(memory_space=pltpu.SMEM)] +...  11.1 us
    pallas_call x1, Pallas kernels, forward(): pl.pallas_call(kernel, in_specs=[vmem, vmem, pl.BlockSpec(memory_space=pl...  8.82 us
    pallas_call x3, Pallas kernels, place(): pl.pallas_call(kernel, in_specs=[hbm] * len(operands), out_specs=hbm, out...  3.35 us
    pallas_call x2, Pallas kernels, row_tables(): pl.pallas_call(kernel, in_specs=[pl.BlockSpec(memory_space=pltpu.SMEM)],...  3.2 us
  transfers between devices with their start and end apart: 39, of which 23 were waited for; matrix products, arithmetic and copies ran while one was open for 2% of the time, Pallas kernels for 21%

profile of v3, /device:TPU:0, one launch (start us, length us, event | category | flops | bytes accessed | tf_op | source)
XLA Modules:
  0.0 131.9 jit_solution(10486894723921926257)
XLA Ops:
  2.5 8.8 %forward.1 = (bf16[1,64,512]{2,1,0:T(8,128)(2,1)S(1)}, bf16[1,64,512]{2,1,0:T(8,128)(2,1)S(1)}, bf16[1,64,512]{2,1,0:T(8,128)(2,1)S(1)}, bf16[1,64,512]{2,1,0:T(...) custom-call(s32[1,1]{1,0:T(1,128)} %bitcast.14.refs_0_, ...), custom_call_target="tpu_custom_call" | custom-call | flops 5368709120 | bytes 8388608 | tf_op jit(solution)/shard_map/forward/pallas_call | solution.py:224
  11.3 2.6 %collective-permute-start.1 = (bf16[1,64,512]{2,1,0:T(8,128)(2,1)S(1)}, bf16[1,64,512]{2,1,0:T(8,128)(2,1)S(1)}, u32[]{:S(2)}, u32[]{:S(2)}) collective-permute-start(bf16[1,64,512]{2,1,0:T(8,128)(2,1)S(1)} %get-tuple-element.25), channel_id=1, source_target_pairs={{0,1},{1,0},{2,3},{3,2},{4,5},{5,4},{6,7},{7,6},{8,9},{9,8},{10,11... | collective-permute-start | bytes 196616 | tf_op jit(solution)/shard_map/ppermute | solution.py:248
  13.9 1.5 %collective-permute-start.32 = (s32[1]{0:T(128)}, s32[1]{0:T(128)}, u32[]{:S(2)}, u32[]{:S(2)}) collective-permute-start(s32[1]{0:T(128)} %param.9), channel_id=1, source_target_pairs={{0,16},{8,24},{16,0},{24,8},{1,17},{9,25},{17,1},{25,9},{2,18},{10... | collective-permute-start | bytes 20 | tf_op jit(solution)/shard_map/ppermute | solution.py:248
  15.9 1.5 %collective-permute-start.5 = (bf16[1,64,512]{2,1,0:T(8,128)(2,1)S(1)}, bf16[1,64,512]{2,1,0:T(8,128)(2,1)S(1)}, u32[]{:S(2)}, u32[]{:S(2)}) collective-permute-start(bf16[1,64,512]{2,1,0:T(8,128)(2,1)S(1)} %get-tuple-element.29), channel_id=1, source_target_pairs={{0,1},{1,0},{2,3},{3,2},{4,5},{5,4},{6,7},{7,6},{8,9},{9,8},{10,11... | collective-permute-start | bytes 196616 | tf_op jit(solution)/shard_map/ppermute | solution.py:248
  17.9 1.3 col_table.1.refs_11_
  21.4 2.6 %collective-permute-start.2 = (bf16[64,512]{1,0:T(8,128)(2,1)S(1)}, bf16[64,512]{1,0:T(8,128)(2,1)S(1)}, u32[]{:S(2)}, u32[]{:S(2)}) collective-permute-start(bf16[64,512]{1,0:T(8,128)(2,1)S(1)} %fusion.4), channel_id=1, source_target_pairs={{0,4},{2,6},{4,0},{6,2},{1,5},{3,7},{5,1},{7,3},{8,12},{10,14},{12... | collective-permute-start | bytes 196616 | tf_op jit(solution)/shard_map/ppermute | solution.py:248
  24.1 1.6 %collective-permute-start.4 = (bf16[64,512]{1,0:T(8,128)(2,1)S(1)}, bf16[64,512]{1,0:T(8,128)(2,1)S(1)}, u32[]{:S(2)}, u32[]{:S(2)}) collective-permute-start(bf16[64,512]{1,0:T(8,128)(2,1)S(1)} %fusion.5), channel_id=1, source_target_pairs={{0,2},{2,0},{4,6},{6,4},{1,3},{3,1},{5,7},{7,5},{8,10},{10,8},{12,... | collective-permute-start | bytes 196616 | tf_op jit(solution)/shard_map/ppermute | solution.py:248
  25.7 1.3 collective-permute-done.2
  27.0 3.9 %collective-permute-start.6 = (bf16[64,512]{1,0:T(8,128)(2,1)S(1)}, bf16[64,512]{1,0:T(8,128)(2,1)S(1)}, u32[]{:S(2)}, u32[]{:S(2)}) collective-permute-start(bf16[64,512]{1,0:T(8,128)(2,1)S(1)} %fusion.6), channel_id=1, source_target_pairs={{0,6},{2,4},{4,2},{6,0},{1,7},{3,5},{5,3},{7,1},{8,14},{10,12},{12... | collective-permute-start | bytes 196616 | tf_op jit(solution)/shard_map/ppermute | solution.py:248
  30.8 2.2 %collective-permute-done.6 = bf16[64,512]{1,0:T(8,128)(2,1)S(1)} collective-permute-done((bf16[64,512]{1,0:T(8,128)(2,1)S(1)}, bf16[64,512]{1,0:T(8,128)(2,1)S(1)}, u32[]{:S(2)}, u32[]{:S(2)}) %collective-permute-start.6) | collective-permute-done | bytes 65568 | tf_op jit(solution)/shard_map/ppermute | solution.py:248
  34.4 3.2 %collective-permute-start.8 = (bf16[64,512]{1,0:T(8,128)(2,1)S(1)}, bf16[64,512]{1,0:T(8,128)(2,1)S(1)}, u32[]{:S(2)}, u32[]{:S(2)}) collective-permute-start(bf16[64,512]{1,0:T(8,128)(2,1)S(1)} %fusion.2), channel_id=1, source_target_pairs={{0,4},{2,6},{4,0},{6,2},{1,5},{3,7},{5,1},{7,3},{8,12},{10,14},{12... | collective-permute-start | bytes 196616 | tf_op jit(solution)/shard_map/ppermute | solution.py:248
  37.7 3.8 %collective-permute-start.9 = (bf16[64,512]{1,0:T(8,128)(2,1)S(1)}, bf16[64,512]{1,0:T(8,128)(2,1)S(1)}, u32[]{:S(2)}, u32[]{:S(2)}) collective-permute-start(bf16[64,512]{1,0:T(8,128)(2,1)S(1)} %fusion.2), channel_id=1, source_target_pairs={{0,6},{2,4},{4,2},{6,0},{1,7},{3,5},{5,3},{7,1},{8,14},{10,12},{12... | collective-permute-start | bytes 196616 | tf_op jit(solution)/shard_map/ppermute | solution.py:248
  42.5 1.3 collective-permute-done.9
  44.6 2.0 %collective-permute-done.10.refs_2_ = bf16[64,512]{1,0:T(8,128)(2,1)S(1)} collective-permute-done((bf16[64,512]{1,0:T(8,128)(2,1)S(1)}, bf16[64,512]{1,0:T(8,128)(2,1)S(1)}, u32[]{:S(2)}, u32[]{:S(2)}) %collective-permute-start.10) | collective-permute-done | bytes 65568 | tf_op jit(solution)/shard_map/ppermute | solution.py:248
  48.9 2.0 %collective-permute-done.12.refs_4_ = bf16[64,512]{1,0:T(8,128)(2,1)S(1)} collective-permute-done((bf16[64,512]{1,0:T(8,128)(2,1)S(1)}, bf16[64,512]{1,0:T(8,128)(2,1)S(1)}, u32[]{:S(2)}, u32[]{:S(2)}) %collective-permute-start.12) | collective-permute-done | bytes 65568 | tf_op jit(solution)/shard_map/ppermute | solution.py:248
  50.9 1.4 %collective-permute-done.13.refs_5_ = bf16[64,512]{1,0:T(8,128)(2,1)S(1)} collective-permute-done((bf16[64,512]{1,0:T(8,128)(2,1)S(1)}, bf16[64,512]{1,0:T(8,128)(2,1)S(1)}, u32[]{:S(2)}, u32[]{:S(2)}) %collective-permute-start.13) | collective-permute-done | bytes 65568 | tf_op jit(solution)/shard_map/ppermute | solution.py:248
  57.1 2.6 %collective-permute-done.28.refs_3_ = bf16[256,512]{1,0:T(8,128)(2,1)S(1)} collective-permute-done((bf16[256,512]{1,0:T(8,128)(2,1)S(1)}, bf16[256,512]{1,0:T(8,128)(2,1)S(1)}, u32[]{:S(2)}, u32[]{:S(2)}) %collective-permute-start.28) | collective-permute-done | bytes 262176 | tf_op jit(solution)/shard_map/ppermute | solution.py:248
  61.7 4.5 %collective-permute-done.29.refs_4_ = bf16[256,512]{1,0:T(8,128)(2,1)S(1)} collective-permute-done((bf16[256,512]{1,0:T(8,128)(2,1)S(1)}, bf16[256,512]{1,0:T(8,128)(2,1)S(1)}, u32[]{:S(2)}, u32[]{:S(2)}) %collective-permute-start.29) | collective-permute-done | bytes 262176 | tf_op jit(solution)/shard_map/ppermute | solution.py:248
  67.6 1.6 %row_tables.2.refs_11_.refs_3_.refs_7_ = bf16[2,512,512]{2,1,0:T(8,128)(2,1)S(1)} custom-call(s32[2]{0:T(128)S(1)} %pad_add_fusion.refs_0_), custom_call_target="tpu_custom_call" | custom-call | flops 10485760 | bytes 1048576 | tf_op jit(solution)/shard_map/row_tables/pallas_call | solution.py:341
  69.7 2.8 %shard_map.55 = (bf16[128,2048]{1,0:T(8,128)(2,1)S(1)}, bf16[512,512]{1,0:T(8,128)(2,1)S(1)}, bf16[512,512]{1,0:T(8,128)(2,1)S(1)}) custom-call(s32[8,16]{1,0:T(8,128)S(1)} %copy-done.2, bf16[256,512]{1,0:T(8,128)(2,1)S(1)} %pad_maximum_fusion.refs_1_, bf16[64,512]{1,0:T(8,128)(2,1)S(1)} %collective-permute-done.10.refs_2_, ...), custom_call_target="tpu_custom_call" | custom-call | flops 671088640 | bytes 1572864 | tf_op jit(solution)/shard_map/pallas_call | solution.py:473
  72.5 3.1 %shard_map.56 = (bf16[96,2048]{1,0:T(8,128)(2,1)S(1)}, bf16[64,2048]{1,0:T(8,128)(2,1)S(1)}) custom-call(s32[8,16]{1,0:T(8,128)S(1)} %copy-done.2, bf16[512,512]{1,0:T(8,128)(2,1)S(1)} %get-tuple-element.31.refs_1_, bf16[512,512]{1,0:T(8,128)(2,1)S(1)} %get-tuple-element.32.refs_2_, bf16[2,512,512]{2,1,0:T(8,128)(2,1)S(1)} %row_tables.2.refs_11_.refs_3_.refs_7_, ...), custom_call_target="tpu_custom_call" | custom-call | flops 838860800 | bytes 1966080 | tf_op jit(solution)/shard_map/pallas_call | solution.py:473
  75.6 1.5 %collective-permute-start.26 = (bf16[96,2048]{1,0:T(8,128)(2,1)S(1)}, bf16[96,2048]{1,0:T(8,128)(2,1)S(1)}, u32[]{:S(2)}, u32[]{:S(2)}) collective-permute-start(bf16[96,2048]{1,0:T(8,128)(2,1)S(1)} %get-tuple-element.35), channel_id=1, source_target_pairs={{0,16},{8,24},{16,0},{24,8},{1,17},{9,25},{17,1},{25,9},{2,18},{10... | collective-permute-start | bytes 1179656 | tf_op jit(solution)/shard_map/ppermute | solution.py:248
  77.1 1.3 pad_add_fusion.1.refs_0_
  78.3 1.6 %row_tables.3.refs_8_ = bf16[2,512,512]{2,1,0:T(8,128)(2,1)S(1)} custom-call(s32[2]{0:T(128)S(1)} %pad_add_fusion.1.refs_0_), custom_call_target="tpu_custom_call" | custom-call | flops 10485760 | bytes 1048576 | tf_op jit(solution)/shard_map/row_tables/pallas_call | solution.py:341
  80.0 3.2 %collective-permute-done.36.refs_16_ = bf16[224,2048]{1,0:T(8,128)(2,1)S(1)} collective-permute-done((bf16[224,2048]{1,0:T(8,128)(2,1)S(1)}, bf16[224,2048]{1,0:T(8,128)(2,1)S(1)}, u32[]{:S(2)}, u32[]{:S(2)}) %collective-permute-start.36) | collective-permute-done | bytes 917536 | tf_op jit(solution)/shard_map/ppermute | solution.py:248
  83.2 1.4 %collective-permute-start.24 = (bf16[128,2048]{1,0:T(8,128)(2,1)S(1)}, bf16[128,2048]{1,0:T(8,128)(2,1)S(1)}, u32[]{:S(2)}, u32[]{:S(2)}) collective-permute-start(bf16[128,2048]{1,0:T(8,128)(2,1)S(1)} %get-tuple-element.34), channel_id=1, source_target_pairs={{0,16},{8,24},{16,0},{24,8},{1,17},{9,25},{17,1},{25,9},{2,18},{10... | collective-permute-start | bytes 1572872 | tf_op jit(solution)/shard_map/ppermute | solution.py:248
  84.6 18.2 %collective-permute-done.35.refs_15_ = bf16[224,2048]{1,0:T(8,128)(2,1)S(1)} collective-permute-done((bf16[224,2048]{1,0:T(8,128)(2,1)S(1)}, bf16[224,2048]{1,0:T(8,128)(2,1)S(1)}, u32[]{:S(2)}, u32[]{:S(2)}) %collective-permute-start.35) | collective-permute-done | bytes 917536 | tf_op jit(solution)/shard_map/ppermute | solution.py:248
  102.8 5.3 %shard_map.57 = (bf16[128,2048]{1,0:T(8,128)(2,1)S(1)}, bf16[96,2048]{1,0:T(8,128)(2,1)S(1)}) custom-call(s32[8,16]{1,0:T(8,128)S(1)} %copy-done.2, bf16[512,512]{1,0:T(8,128)(2,1)S(1)} %get-tuple-element.31.refs_1_, bf16[512,512]{1,0:T(8,128)(2,1)S(1)} %get-tuple-element.32.refs_2_, bf16[256,512]{1,0:T(8,128)(2,1)S(1)} %collective-permute-done.28.refs_3_, ...), custom_call_target="tpu_custom_call" | custom-call | flops 2348810240 | bytes 2752512 | tf_op jit(solution)/shard_map/pallas_call | solution.py:473
  109.8 1.4 %collective-permute-done.26 = bf16[96,2048]{1,0:T(8,128)(2,1)S(1)} collective-permute-done((bf16[96,2048]{1,0:T(8,128)(2,1)S(1)}, bf16[96,2048]{1,0:T(8,128)(2,1)S(1)}, u32[]{:S(2)}, u32[]{:S(2)}) %collective-permute-start.26) | collective-permute-done | bytes 393248 | tf_op jit(solution)/shard_map/ppermute | solution.py:248
  111.5 10.9 %collective-permute-done.24 = bf16[128,2048]{1,0:T(8,128)(2,1)S(1)} collective-permute-done((bf16[128,2048]{1,0:T(8,128)(2,1)S(1)}, bf16[128,2048]{1,0:T(8,128)(2,1)S(1)}, u32[]{:S(2)}, u32[]{:S(2)}) %collective-permute-start.24) | collective-permute-done | bytes 524320 | tf_op jit(solution)/shard_map/ppermute | solution.py:248
  122.8 5.2 %collective-permute-done.22 = bf16[64,2048]{1,0:T(8,128)(2,1)S(1)} collective-permute-done((bf16[64,2048]{1,0:T(8,128)(2,1)S(1)}, bf16[64,2048]{1,0:T(8,128)(2,1)S(1)}, u32[]{:S(2)}, u32[]{:S(2)}) %collective-permute-start.22) | collective-permute-done | bytes 262176 | tf_op jit(solution)/shard_map/ppermute | solution.py:248
  129.6 1.3 shard_map.59.refs_2_
  (73 shorter events, 23.4 us)
Async XLA Ops:
  0.0 69.2 %collective-permute-start.21 = (bf16[1,1024,2048]{2,1,0:T(8,128)(2,1)}, bf16[1,1024,2048]{2,1,0:T(8,128)(2,1)S(1)}, u32[]{:S(2)}, u32[]{:S(2)}) collective-permute-start(bf16[1,1024,2048]{2,1,0:T(8,128)(2,1)} %refs_13_.1), channel_id=1, source_target_pairs={{0,8},{8,0},{16,24},{24,16},{1,9},{9,1},{17,25},{25,17},{2,10},{10... | collective-permute-start | bytes 12582920 | tf_op jit(solution)/shard_map/ppermute | solution.py:248
  11.3 7.9 %collective-permute-start.1 = (bf16[1,64,512]{2,1,0:T(8,128)(2,1)S(1)}, bf16[1,64,512]{2,1,0:T(8,128)(2,1)S(1)}, u32[]{:S(2)}, u32[]{:S(2)}) collective-permute-start(bf16[1,64,512]{2,1,0:T(8,128)(2,1)S(1)} %get-tuple-element.25), channel_id=1, source_target_pairs={{0,1},{1,0},{2,3},{3,2},{4,5},{5,4},{6,7},{7,6},{8,9},{9,8},{10,11... | collective-permute-start | bytes 196616 | tf_op jit(solution)/shard_map/ppermute | solution.py:248
  13.9 3.7 %collective-permute-start.32 = (s32[1]{0:T(128)}, s32[1]{0:T(128)}, u32[]{:S(2)}, u32[]{:S(2)}) collective-permute-start(s32[1]{0:T(128)} %param.9), channel_id=1, source_target_pairs={{0,16},{8,24},{16,0},{24,8},{1,17},{9,25},{17,1},{25,9},{2,18},{10... | collective-permute-start | bytes 20 | tf_op jit(solution)/shard_map/ppermute | solution.py:248
  15.4 5.0 %collective-permute-start.3 = (bf16[1,64,512]{2,1,0:T(8,128)(2,1)S(1)}, bf16[1,64,512]{2,1,0:T(8,128)(2,1)S(1)}, u32[]{:S(2)}, u32[]{:S(2)}) collective-permute-start(bf16[1,64,512]{2,1,0:T(8,128)(2,1)S(1)} %get-tuple-element.27), channel_id=1, source_target_pairs={{0,1},{1,0},{2,3},{3,2},{4,5},{5,4},{6,7},{7,6},{8,9},{9,8},{10,11... | collective-permute-start | bytes 196616 | tf_op jit(solution)/shard_map/ppermute | solution.py:248
  15.9 5.5 %collective-permute-start.5 = (bf16[1,64,512]{2,1,0:T(8,128)(2,1)S(1)}, bf16[1,64,512]{2,1,0:T(8,128)(2,1)S(1)}, u32[]{:S(2)}, u32[]{:S(2)}) collective-permute-start(bf16[1,64,512]{2,1,0:T(8,128)(2,1)S(1)} %get-tuple-element.29), channel_id=1, source_target_pairs={{0,1},{1,0},{2,3},{3,2},{4,5},{5,4},{6,7},{7,6},{8,9},{9,8},{10,11... | collective-permute-start | bytes 196616 | tf_op jit(solution)/shard_map/ppermute | solution.py:248
  17.5 6.5 %collective-permute-start = (bf16[1,64,512]{2,1,0:T(8,128)(2,1)S(1)}, bf16[1,64,512]{2,1,0:T(8,128)(2,1)S(1)}, u32[]{:S(2)}, u32[]{:S(2)}) collective-permute-start(bf16[1,64,512]{2,1,0:T(8,128)(2,1)S(1)} %get-tuple-element.23), channel_id=1, source_target_pairs={{0,1},{1,0},{2,3},{3,2},{4,5},{5,4},{6,7},{7,6},{8,9},{9,8},{10,11... | collective-permute-start | bytes 196616 | tf_op jit(solution)/shard_map/ppermute | solution.py:248
  19.3 47.6 %collective-permute-start.20 = (bf16[2048,512]{1,0:T(8,128)(2,1)S(1)}, bf16[2048,512]{1,0:T(8,128)(2,1)S(1)}, u32[]{:S(2)}, u32[]{:S(2)}) collective-permute-start(bf16[2048,512]{1,0:T(8,128)(2,1)S(1)} %get-tuple-element.30.refs_12_.refs_4_.refs_9_), channel_id=1, source_target_pairs={{0,8},{8,0},{16,24},{24,16},{1,9},{9,1},{17,25},{25,17},{2,10},{10... | collective-permute-start | bytes 6291464 | tf_op jit(solution)/shard_map/ppermute | solution.py:248
  20.3 82.4 %collective-permute-start.34 = (bf16[2048,512]{1,0:T(8,128)(2,1)S(1)}, bf16[2048,512]{1,0:T(8,128)(2,1)S(1)}, u32[]{:S(2)}, u32[]{:S(2)}) collective-permute-start(bf16[2048,512]{1,0:T(8,128)(2,1)S(1)} %col_table.1.refs_11_), channel_id=1, source_target_pairs={{0,8},{8,0},{16,24},{24,16},{1,9},{9,1},{17,25},{25,17},{2,10},{10... | collective-permute-start | bytes 6291464 | tf_op jit(solution)/shard_map/ppermute | solution.py:248
  21.4 5.5 %collective-permute-start.2 = (bf16[64,512]{1,0:T(8,128)(2,1)S(1)}, bf16[64,512]{1,0:T(8,128)(2,1)S(1)}, u32[]{:S(2)}, u32[]{:S(2)}) collective-permute-start(bf16[64,512]{1,0:T(8,128)(2,1)S(1)} %fusion.4), channel_id=1, source_target_pairs={{0,4},{2,6},{4,0},{6,2},{1,5},{3,7},{5,1},{7,3},{8,12},{10,14},{12... | collective-permute-start | bytes 196616 | tf_op jit(solution)/shard_map/ppermute | solution.py:248
  24.1 6.8 %collective-permute-start.4 = (bf16[64,512]{1,0:T(8,128)(2,1)S(1)}, bf16[64,512]{1,0:T(8,128)(2,1)S(1)}, u32[]{:S(2)}, u32[]{:S(2)}) collective-permute-start(bf16[64,512]{1,0:T(8,128)(2,1)S(1)} %fusion.5), channel_id=1, source_target_pairs={{0,2},{2,0},{4,6},{6,4},{1,3},{3,1},{5,7},{7,5},{8,10},{10,8},{12,... | collective-permute-start | bytes 196616 | tf_op jit(solution)/shard_map/ppermute | solution.py:248
  27.0 6.1 %collective-permute-start.6 = (bf16[64,512]{1,0:T(8,128)(2,1)S(1)}, bf16[64,512]{1,0:T(8,128)(2,1)S(1)}, u32[]{:S(2)}, u32[]{:S(2)}) collective-permute-start(bf16[64,512]{1,0:T(8,128)(2,1)S(1)} %fusion.6), channel_id=1, source_target_pairs={{0,6},{2,4},{4,2},{6,0},{1,7},{3,5},{5,3},{7,1},{8,14},{10,12},{12... | collective-permute-start | bytes 196616 | tf_op jit(solution)/shard_map/ppermute | solution.py:248
  33.1 4.6 %collective-permute-start.7 = (bf16[64,512]{1,0:T(8,128)(2,1)S(1)}, bf16[64,512]{1,0:T(8,128)(2,1)S(1)}, u32[]{:S(2)}, u32[]{:S(2)}) collective-permute-start(bf16[64,512]{1,0:T(8,128)(2,1)S(1)} %fusion.2), channel_id=1, source_target_pairs={{0,2},{2,0},{4,6},{6,4},{1,3},{3,1},{5,7},{7,5},{8,10},{10,8},{12,... | collective-permute-start | bytes 196616 | tf_op jit(solution)/shard_map/ppermute | solution.py:248
  34.4 7.2 %collective-permute-start.8 = (bf16[64,512]{1,0:T(8,128)(2,1)S(1)}, bf16[64,512]{1,0:T(8,128)(2,1)S(1)}, u32[]{:S(2)}, u32[]{:S(2)}) collective-permute-start(bf16[64,512]{1,0:T(8,128)(2,1)S(1)} %fusion.2), channel_id=1, source_target_pairs={{0,4},{2,6},{4,0},{6,2},{1,5},{3,7},{5,1},{7,3},{8,12},{10,14},{12... | collective-permute-start | bytes 196616 | tf_op jit(solution)/shard_map/ppermute | solution.py:248
  37.7 6.1 %collective-permute-start.9 = (bf16[64,512]{1,0:T(8,128)(2,1)S(1)}, bf16[64,512]{1,0:T(8,128)(2,1)S(1)}, u32[]{:S(2)}, u32[]{:S(2)}) collective-permute-start(bf16[64,512]{1,0:T(8,128)(2,1)S(1)} %fusion.2), channel_id=1, source_target_pairs={{0,6},{2,4},{4,2},{6,0},{1,7},{3,5},{5,3},{7,1},{8,14},{10,12},{12... | collective-permute-start | bytes 196616 | tf_op jit(solution)/shard_map/ppermute | solution.py:248
  41.7 4.9 %collective-permute-start.10 = (bf16[64,512]{1,0:T(8,128)(2,1)S(1)}, bf16[64,512]{1,0:T(8,128)(2,1)S(1)}, u32[]{:S(2)}, u32[]{:S(2)}) collective-permute-start(bf16[64,512]{1,0:T(8,128)(2,1)S(1)} %fusion.2), channel_id=1, source_target_pairs={{0,1},{1,0},{2,3},{3,2},{4,5},{5,4},{6,7},{7,6},{8,9},{9,8},{10,11... | collective-permute-start | bytes 196616 | tf_op jit(solution)/shard_map/ppermute | solution.py:248
  43.8 4.3 %collective-permute-start.11 = (bf16[64,512]{1,0:T(8,128)(2,1)S(1)}, bf16[64,512]{1,0:T(8,128)(2,1)S(1)}, u32[]{:S(2)}, u32[]{:S(2)}) collective-permute-start(bf16[64,512]{1,0:T(8,128)(2,1)S(1)} %collective-permute-done.7), channel_id=1, source_target_pairs={{0,1},{1,0},{2,3},{3,2},{4,5},{5,4},{6,7},{7,6},{8,9},{9,8},{10,11... | collective-permute-start | bytes 196616 | tf_op jit(solution)/shard_map/ppermute | solution.py:248
  46.6 4.3 %collective-permute-start.12 = (bf16[64,512]{1,0:T(8,128)(2,1)S(1)}, bf16[64,512]{1,0:T(8,128)(2,1)S(1)}, u32[]{:S(2)}, u32[]{:S(2)}) collective-permute-start(bf16[64,512]{1,0:T(8,128)(2,1)S(1)} %collective-permute-done.8), channel_id=1, source_target_pairs={{0,1},{1,0},{2,3},{3,2},{4,5},{5,4},{6,7},{7,6},{8,9},{9,8},{10,11... | collective-permute-start | bytes 196616 | tf_op jit(solution)/shard_map/ppermute | solution.py:248
  48.1 4.3 %collective-permute-start.13 = (bf16[64,512]{1,0:T(8,128)(2,1)S(1)}, bf16[64,512]{1,0:T(8,128)(2,1)S(1)}, u32[]{:S(2)}, u32[]{:S(2)}) collective-permute-start(bf16[64,512]{1,0:T(8,128)(2,1)S(1)} %collective-permute-done.9), channel_id=1, source_target_pairs={{0,1},{1,0},{2,3},{3,2},{4,5},{5,4},{6,7},{7,6},{8,9},{9,8},{10,11... | collective-permute-start | bytes 196616 | tf_op jit(solution)/shard_map/ppermute | solution.py:248
  52.3 7.4 %collective-permute-start.28 = (bf16[256,512]{1,0:T(8,128)(2,1)S(1)}, bf16[256,512]{1,0:T(8,128)(2,1)S(1)}, u32[]{:S(2)}, u32[]{:S(2)}) collective-permute-start(bf16[256,512]{1,0:T(8,128)(2,1)S(1)} %pad_maximum_fusion.refs_1_), channel_id=1, source_target_pairs={{0,16},{8,24},{16,0},{24,8},{1,17},{9,25},{17,1},{25,9},{2,18},{10... | collective-permute-start | bytes 786440 | tf_op jit(solution)/shard_map/ppermute | solution.py:248
  57.0 3.6 %collective-permute-start.14 = (bf16[256,512]{1,0:T(8,128)(2,1)S(1)}, bf16[256,512]{1,0:T(8,128)(2,1)S(1)}, u32[]{:S(2)}, u32[]{:S(2)}) collective-permute-start(bf16[256,512]{1,0:T(8,128)(2,1)S(1)} %pad_maximum_fusion.refs_1_), channel_id=1, source_target_pairs={{0,8},{8,0},{16,24},{24,16},{1,9},{9,1},{17,25},{25,17},{2,10},{10... | collective-permute-start | bytes 786440 | tf_op jit(solution)/shard_map/ppermute | solution.py:248
  59.7 6.5 %collective-permute-start.29 = (bf16[256,512]{1,0:T(8,128)(2,1)S(1)}, bf16[256,512]{1,0:T(8,128)(2,1)S(1)}, u32[]{:S(2)}, u32[]{:S(2)}) collective-permute-start(bf16[256,512]{1,0:T(8,128)(2,1)S(1)} %collective-permute-done.28.refs_3_), channel_id=1, source_target_pairs={{0,1},{1,0},{2,3},{3,2},{4,5},{5,4},{6,7},{7,6},{8,9},{9,8},{10,11... | collective-permute-start | bytes 786440 | tf_op jit(solution)/shard_map/ppermute | solution.py:248
  60.5 22.6 %collective-permute-start.36 = (bf16[224,2048]{1,0:T(8,128)(2,1)S(1)}, bf16[224,2048]{1,0:T(8,128)(2,1)S(1)}, u32[]{:S(2)}, u32[]{:S(2)}) collective-permute-start(bf16[224,2048]{1,0:T(8,128)(2,1)S(1)} %get-tuple-element.36), channel_id=1, source_target_pairs={{0,24},{8,16},{16,8},{24,0},{1,25},{9,17},{17,9},{25,1},{2,26},{10... | collective-permute-start | bytes 2752520 | tf_op jit(solution)/shard_map/ppermute | solution.py:248
  66.2 36.6 %collective-permute-start.35 = (bf16[224,2048]{1,0:T(8,128)(2,1)S(1)}, bf16[224,2048]{1,0:T(8,128)(2,1)S(1)}, u32[]{:S(2)}, u32[]{:S(2)}) collective-permute-start(bf16[224,2048]{1,0:T(8,128)(2,1)S(1)} %own_slice.1), channel_id=1, source_target_pairs={{0,16},{8,24},{16,0},{24,8},{1,17},{9,25},{17,1},{25,9},{2,18},{10... | collective-permute-start | bytes 2752520 | tf_op jit(solution)/shard_map/ppermute | solution.py:248
  66.8 8.7 %collective-permute-start.30 = (bf16[256,512]{1,0:T(8,128)(2,1)S(1)}, bf16[256,512]{1,0:T(8,128)(2,1)S(1)}, u32[]{:S(2)}, u32[]{:S(2)}) collective-permute-start(bf16[256,512]{1,0:T(8,128)(2,1)S(1)} %collective-permute-done.28.refs_3_), channel_id=1, source_target_pairs={{0,8},{8,0},{16,24},{24,16},{1,9},{9,1},{17,25},{25,17},{2,10},{10... | collective-permute-start | bytes 786440 | tf_op jit(solution)/shard_map/ppermute | solution.py:248
  69.2 33.6 %collective-permute-start.31 = (bf16[256,512]{1,0:T(8,128)(2,1)S(1)}, bf16[256,512]{1,0:T(8,128)(2,1)S(1)}, u32[]{:S(2)}, u32[]{:S(2)}) collective-permute-start(bf16[256,512]{1,0:T(8,128)(2,1)S(1)} %collective-permute-done.29.refs_4_), channel_id=1, source_target_pairs={{0,8},{8,0},{16,24},{24,16},{1,9},{9,1},{17,25},{25,17},{2,10},{10... | collective-permute-start | bytes 786440 | tf_op jit(solution)/shard_map/ppermute | solution.py:248
  75.6 35.6 %collective-permute-start.26 = (bf16[96,2048]{1,0:T(8,128)(2,1)S(1)}, bf16[96,2048]{1,0:T(8,128)(2,1)S(1)}, u32[]{:S(2)}, u32[]{:S(2)}) collective-permute-start(bf16[96,2048]{1,0:T(8,128)(2,1)S(1)} %get-tuple-element.35), channel_id=1, source_target_pairs={{0,16},{8,24},{16,0},{24,8},{1,17},{9,25},{17,1},{25,9},{2,18},{10... | collective-permute-start | bytes 1179656 | tf_op jit(solution)/shard_map/ppermute | solution.py:248
  83.2 39.3 %collective-permute-start.24 = (bf16[128,2048]{1,0:T(8,128)(2,1)S(1)}, bf16[128,2048]{1,0:T(8,128)(2,1)S(1)}, u32[]{:S(2)}, u32[]{:S(2)}) collective-permute-start(bf16[128,2048]{1,0:T(8,128)(2,1)S(1)} %get-tuple-element.34), channel_id=1, source_target_pairs={{0,16},{8,24},{16,0},{24,8},{1,17},{9,25},{17,1},{25,9},{2,18},{10... | collective-permute-start | bytes 1572872 | tf_op jit(solution)/shard_map/ppermute | solution.py:248
  108.1 20.2 %collective-permute-start.37 = (bf16[128,2048]{1,0:T(8,128)(2,1)S(1)}, bf16[128,2048]{1,0:T(8,128)(2,1)S(1)}, u32[]{:S(2)}, u32[]{:S(2)}) collective-permute-start(bf16[128,2048]{1,0:T(8,128)(2,1)S(1)} %get-tuple-element.37.refs_0_), channel_id=1, source_target_pairs={{0,8},{8,0},{16,24},{24,16},{1,9},{9,1},{17,25},{25,17},{2,10},{10... | collective-permute-start | bytes 1572872 | tf_op jit(solution)/shard_map/ppermute | solution.py:248
  108.3 20.0 %collective-permute-start.38 = (bf16[96,2048]{1,0:T(8,128)(2,1)S(1)}, bf16[96,2048]{1,0:T(8,128)(2,1)S(1)}, u32[]{:S(2)}, u32[]{:S(2)}) collective-permute-start(bf16[96,2048]{1,0:T(8,128)(2,1)S(1)} %get-tuple-element.38.refs_2_), channel_id=1, source_target_pairs={{0,8},{8,0},{16,24},{24,16},{1,9},{9,1},{17,25},{25,17},{2,10},{10... | collective-permute-start | bytes 1179656 | tf_op jit(solution)/shard_map/ppermute | solution.py:248
  108.7 19.4 %collective-permute-start.22 = (bf16[64,2048]{1,0:T(8,128)(2,1)S(1)}, bf16[64,2048]{1,0:T(8,128)(2,1)S(1)}, u32[]{:S(2)}, u32[]{:S(2)}) collective-permute-start(bf16[64,2048]{1,0:T(8,128)(2,1)S(1)} %get-tuple-element.33), channel_id=1, source_target_pairs={{0,16},{8,24},{16,0},{24,8},{1,17},{9,25},{17,1},{25,9},{2,18},{10... | collective-permute-start | bytes 786440 | tf_op jit(solution)/shard_map/ppermute | solution.py:248
  111.3 18.3 %collective-permute-start.27 = (bf16[96,2048]{1,0:T(8,128)(2,1)S(1)}, bf16[96,2048]{1,0:T(8,128)(2,1)S(1)}, u32[]{:S(2)}, u32[]{:S(2)}) collective-permute-start(bf16[96,2048]{1,0:T(8,128)(2,1)S(1)} %add_convert_fusion.1.refs_2_), channel_id=1, source_target_pairs={{0,8},{8,0},{16,24},{24,16},{1,9},{9,1},{17,25},{25,17},{2,10},{10... | collective-permute-start | bytes 1179656 | tf_op jit(solution)/shard_map/ppermute | solution.py:248
  122.6 7.0 %collective-permute-start.25 = (bf16[128,2048]{1,0:T(8,128)(2,1)S(1)}, bf16[128,2048]{1,0:T(8,128)(2,1)S(1)}, u32[]{:S(2)}, u32[]{:S(2)}) collective-permute-start(bf16[128,2048]{1,0:T(8,128)(2,1)S(1)} %add_convert_fusion.refs_0_), channel_id=1, source_target_pairs={{0,8},{8,0},{16,24},{24,16},{1,9},{9,1},{17,25},{25,17},{2,10},{10... | collective-permute-start | bytes 1572872 | tf_op jit(solution)/shard_map/ppermute | solution.py:248
  (10 other events, 114.2 us)

commit v4 on v3

--- a/solution.py
+++ b/solution.py
@@ -130,7 +130,7 @@
     half_at = lax.rem(lax.axis_index("wl"), 2)
     slice_copy = slice_rows(inc_ref, slice_ref, sems.at[rows // block], 1 - half_at, begin)
     slice_copy.start()
-    period = quarter_period(index_ref[...])
+    period = quarter_period(index_ref[0])
 
     def write_col(at, amount, re, im):
         col_tab[at : at + amount, :HALF] = re
@@ -156,7 +156,7 @@
         inner[at : at + block, :M] = prod[:block].astype(BF16)
         inner[at : at + block, M:] = prod[block:].astype(BF16)
 
-    charge = charge_ref[...]
+    charge = charge_ref[0]
     even = jnp.where(charge % 2 == 0, 1.0, 0.0).astype(F32)
     odd = 1.0 - even
     scale = 4.0 / (extent * M)
@@ -220,10 +220,10 @@
     def kernel(*refs):
         forward_kernel(*refs, rows=rows, cols=cols, n_row=n_row, groups=groups, begin=begin)
 
-    vmem = pl.BlockSpec(memory_space=pltpu.VMEM)
+    hbm, smem = pl.BlockSpec(memory_space=pltpu.HBM), pl.BlockSpec(memory_space=pltpu.SMEM)
     outs = pl.pallas_call(
         kernel,
-        in_specs=[vmem, vmem, pl.BlockSpec(memory_space=pltpu.SMEM)] + [pl.BlockSpec(memory_space=pltpu.HBM)] * 2,
+        in_specs=[smem, smem, smem, hbm, hbm],
         out_specs=[pl.BlockSpec(memory_space=pltpu.VMEM)] * len(out_shape),
         out_shape=out_shape,
         scratch_shapes=[
@@ -239,7 +239,7 @@
             flops=2 * rows * 2 * M * (cols + M), bytes_accessed=4 * rows * cols, transcendentals=0
         ),
         name="forward",
-    )(index.reshape(1, 1), charge.reshape(1, 1), tiles, in_hbm(cotangent), in_hbm(incident))
+    )(index, charge, tiles, in_hbm(cotangent), in_hbm(incident))
     return outs[:-2], outs[-2], outs[-1]
 
 
@@ -262,7 +262,7 @@
 def slot_groups(n_row, n_col):
     order = hop_order(n_row) + [0]
     if n_row <= 4:
-        parts = [[kz] for kz in order]
+        parts = [order[:1], order[1:]]
     else:
         parts = [order[: n_row // 2], order[n_row // 2 :]]
     return [(ky, tuple(slots)) for slots in parts for ky in range(n_col)]

time: 132 us -> 130 us (0.985)
  starting transfers between devices: 34.2 us -> 29.8 us
  waiting for transfers between devices: 63.9 us -> 66.8 us
    ppermute x39 -> x37, starting transfers between devices: 34.2 us -> 29.8 us  [swap(): return lax.ppermute(value, axis, [(i, i ^ bits) for i in range(size)])]
    ppermute x39 -> x37, waiting for transfers between devices: 63.9 us -> 66.8 us  [swap(): return lax.ppermute(value, axis, [(i, i ^ bits) for i in range(size)])]
  transfers between devices with their start and end apart: 39 -> 37, of which waited for: 23 -> 22; matrix products, arithmetic and copies ran while one was open for 2% -> 2% of each run, Pallas kernels for 21% -> 22%
where the time goes in v4:
time: 130 us
  waiting for transfers between devices  66.8 us (51%)
  starting transfers between devices  29.8 us (23%)
  Pallas kernels  28.8 us (22%)
  other arithmetic  2.39 us (2%)
  between operations  1.71 us (1%)
    ppermute x37, waiting for transfers between devices, swap(): return lax.ppermute(value, axis, [(i, i ^ bits) for i in range(size)])  66.8 us
    ppermute x37, starting transfers between devices, swap(): return lax.ppermute(value, axis, [(i, i ^ bits) for i in range(size)])  29.8 us
    pallas_call x3, Pallas kernels, backward(): pl.pallas_call(kernel, in_specs=[pl.BlockSpec(memory_space=pltpu.SMEM)] +...  11.1 us
    pallas_call x1, Pallas kernels, forward(): pl.pallas_call(kernel, in_specs=[smem, smem, smem, hbm, hbm], out_specs=[...  8.72 us
    pallas_call x3, Pallas kernels, place(): pl.pallas_call(kernel, in_specs=[hbm] * len(operands), out_specs=hbm, out...  3.35 us
    pallas_call x2, Pallas kernels, row_tables(): pl.pallas_call(kernel, in_specs=[pl.BlockSpec(memory_space=pltpu.SMEM)],...  3.2 us
  transfers between devices with their start and end apart: 37, of which 22 were waited for; matrix products, arithmetic and copies ran while one was open for 2% of the time, Pallas kernels for 22%

profile of v4, /device:TPU:0, one launch (start us, length us, event | category | flops | bytes accessed | tf_op | source)
XLA Modules:
  0.0 130.1 jit_solution(11231784421711338833)
XLA Ops:
  2.5 8.7 %forward.1 = (bf16[1,64,512]{2,1,0:T(8,128)(2,1)S(1)}, bf16[1,64,512]{2,1,0:T(8,128)(2,1)S(1)}, bf16[3,64,512]{2,1,0:T(8,128)(2,1)S(1)}, bf16[3,64,512]{2,1,0:T(...) custom-call(s32[1]{0:T(128)S(6)} %copy.11.refs_0_, s32[1]{0:T(128)S(6)} %copy.10.refs_1_, ...), custom_call_target="tpu_custom_call" | custom-call | flops 5368709120 | bytes 8388608 | tf_op jit(solution)/shard_map/forward/pallas_call | solution.py:224
  11.2 2.6 %collective-permute-start.1 = (bf16[1,64,512]{2,1,0:T(8,128)(2,1)S(1)}, bf16[1,64,512]{2,1,0:T(8,128)(2,1)S(1)}, u32[]{:S(2)}, u32[]{:S(2)}) collective-permute-start(bf16[1,64,512]{2,1,0:T(8,128)(2,1)S(1)} %get-tuple-element.21), channel_id=1, source_target_pairs={{0,1},{1,0},{2,3},{3,2},{4,5},{5,4},{6,7},{7,6},{8,9},{9,8},{10,11... | collective-permute-start | bytes 196616 | tf_op jit(solution)/shard_map/ppermute | solution.py:248
  13.8 1.5 %collective-permute-start.30 = (s32[1]{0:T(128)}, s32[1]{0:T(128)}, u32[]{:S(2)}, u32[]{:S(2)}) collective-permute-start(s32[1]{0:T(128)} %param.9), channel_id=1, source_target_pairs={{0,16},{8,24},{16,0},{24,8},{1,17},{9,25},{17,1},{25,9},{2,18},{10... | collective-permute-start | bytes 20 | tf_op jit(solution)/shard_map/ppermute | solution.py:248
  15.8 1.8 %collective-permute-done.30.index_ref = s32[1]{0:T(128)} collective-permute-done((s32[1]{0:T(128)}, s32[1]{0:T(128)}, u32[]{:S(2)}, u32[]{:S(2)}) %collective-permute-start.30) | collective-permute-done | bytes 36 | tf_op jit(solution)/shard_map/ppermute | solution.py:248
  19.0 2.7 %collective-permute-start.2 = (bf16[64,512]{1,0:T(8,128)(2,1)S(1)}, bf16[64,512]{1,0:T(8,128)(2,1)S(1)}, u32[]{:S(2)}, u32[]{:S(2)}) collective-permute-start(bf16[64,512]{1,0:T(8,128)(2,1)S(1)} %fusion.3), channel_id=1, source_target_pairs={{0,4},{2,6},{4,0},{6,2},{1,5},{3,7},{5,1},{7,3},{8,12},{10,14},{12... | collective-permute-start | bytes 196616 | tf_op jit(solution)/shard_map/ppermute | solution.py:248
  22.1 1.6 %collective-permute-start.3 = (bf16[64,512]{1,0:T(8,128)(2,1)S(1)}, bf16[64,512]{1,0:T(8,128)(2,1)S(1)}, u32[]{:S(2)}, u32[]{:S(2)}) collective-permute-start(bf16[64,512]{1,0:T(8,128)(2,1)S(1)} %get-tuple-element.31), channel_id=1, source_target_pairs={{0,2},{2,0},{4,6},{6,4},{1,3},{3,1},{5,7},{7,5},{8,10},{10,8},{12,... | collective-permute-start | bytes 196616 | tf_op jit(solution)/shard_map/ppermute | solution.py:248
  23.7 2.1 %collective-permute-done.2 = bf16[64,512]{1,0:T(8,128)(2,1)S(1)} collective-permute-done((bf16[64,512]{1,0:T(8,128)(2,1)S(1)}, bf16[64,512]{1,0:T(8,128)(2,1)S(1)}, u32[]{:S(2)}, u32[]{:S(2)}) %collective-permute-start.2) | collective-permute-done | bytes 65568 | tf_op jit(solution)/shard_map/ppermute | solution.py:248
  25.8 3.6 %collective-permute-start.4 = (bf16[64,512]{1,0:T(8,128)(2,1)S(1)}, bf16[64,512]{1,0:T(8,128)(2,1)S(1)}, u32[]{:S(2)}, u32[]{:S(2)}) collective-permute-start(bf16[64,512]{1,0:T(8,128)(2,1)S(1)} %get-tuple-element.32), channel_id=1, source_target_pairs={{0,6},{2,4},{4,2},{6,0},{1,7},{3,5},{5,3},{7,1},{8,14},{10,12},{12... | collective-permute-start | bytes 196616 | tf_op jit(solution)/shard_map/ppermute | solution.py:248
  29.4 2.5 %collective-permute-done.4 = bf16[64,512]{1,0:T(8,128)(2,1)S(1)} collective-permute-done((bf16[64,512]{1,0:T(8,128)(2,1)S(1)}, bf16[64,512]{1,0:T(8,128)(2,1)S(1)}, u32[]{:S(2)}, u32[]{:S(2)}) %collective-permute-start.4) | collective-permute-done | bytes 65568 | tf_op jit(solution)/shard_map/ppermute | solution.py:248
  33.3 2.9 %collective-permute-start.6 = (bf16[64,512]{1,0:T(8,128)(2,1)S(1)}, bf16[64,512]{1,0:T(8,128)(2,1)S(1)}, u32[]{:S(2)}, u32[]{:S(2)}) collective-permute-start(bf16[64,512]{1,0:T(8,128)(2,1)S(1)} %fusion.2), channel_id=1, source_target_pairs={{0,4},{2,6},{4,0},{6,2},{1,5},{3,7},{5,1},{7,3},{8,12},{10,14},{12... | collective-permute-start | bytes 196616 | tf_op jit(solution)/shard_map/ppermute | solution.py:248
  36.5 3.6 %collective-permute-start.7 = (bf16[64,512]{1,0:T(8,128)(2,1)S(1)}, bf16[64,512]{1,0:T(8,128)(2,1)S(1)}, u32[]{:S(2)}, u32[]{:S(2)}) collective-permute-start(bf16[64,512]{1,0:T(8,128)(2,1)S(1)} %fusion.2), channel_id=1, source_target_pairs={{0,6},{2,4},{4,2},{6,0},{1,7},{3,5},{5,3},{7,1},{8,14},{10,12},{12... | collective-permute-start | bytes 196616 | tf_op jit(solution)/shard_map/ppermute | solution.py:248
  40.7 2.0 %collective-permute-done.7 = bf16[64,512]{1,0:T(8,128)(2,1)S(1)} collective-permute-done((bf16[64,512]{1,0:T(8,128)(2,1)S(1)}, bf16[64,512]{1,0:T(8,128)(2,1)S(1)}, u32[]{:S(2)}, u32[]{:S(2)}) %collective-permute-start.7) | collective-permute-done | bytes 65568 | tf_op jit(solution)/shard_map/ppermute | solution.py:248
  43.0 2.1 %collective-permute-done.8.refs_2_ = bf16[64,512]{1,0:T(8,128)(2,1)S(1)} collective-permute-done((bf16[64,512]{1,0:T(8,128)(2,1)S(1)}, bf16[64,512]{1,0:T(8,128)(2,1)S(1)}, u32[]{:S(2)}, u32[]{:S(2)}) %collective-permute-start.8) | collective-permute-done | bytes 65568 | tf_op jit(solution)/shard_map/ppermute | solution.py:248
  45.7 1.3 collective-permute-done.9.refs_3_
  47.3 2.1 %collective-permute-done.10.refs_4_ = bf16[64,512]{1,0:T(8,128)(2,1)S(1)} collective-permute-done((bf16[64,512]{1,0:T(8,128)(2,1)S(1)}, bf16[64,512]{1,0:T(8,128)(2,1)S(1)}, u32[]{:S(2)}, u32[]{:S(2)}) %collective-permute-start.10) | collective-permute-done | bytes 65568 | tf_op jit(solution)/shard_map/ppermute | solution.py:248
  49.5 1.7 %collective-permute-done.11.refs_5_ = bf16[64,512]{1,0:T(8,128)(2,1)S(1)} collective-permute-done((bf16[64,512]{1,0:T(8,128)(2,1)S(1)}, bf16[64,512]{1,0:T(8,128)(2,1)S(1)}, u32[]{:S(2)}, u32[]{:S(2)}) %collective-permute-start.11) | collective-permute-done | bytes 65568 | tf_op jit(solution)/shard_map/ppermute | solution.py:248
  51.2 1.3 collective-permute-start.26
  56.4 1.8 %collective-permute-done.26.refs_3_ = bf16[256,512]{1,0:T(8,128)(2,1)S(1)} collective-permute-done((bf16[256,512]{1,0:T(8,128)(2,1)S(1)}, bf16[256,512]{1,0:T(8,128)(2,1)S(1)}, u32[]{:S(2)}, u32[]{:S(2)}) %collective-permute-start.26) | collective-permute-done | bytes 262176 | tf_op jit(solution)/shard_map/ppermute | solution.py:248
  60.0 5.0 %collective-permute-done.27.refs_4_ = bf16[256,512]{1,0:T(8,128)(2,1)S(1)} collective-permute-done((bf16[256,512]{1,0:T(8,128)(2,1)S(1)}, bf16[256,512]{1,0:T(8,128)(2,1)S(1)}, u32[]{:S(2)}, u32[]{:S(2)}) %collective-permute-start.27) | collective-permute-done | bytes 262176 | tf_op jit(solution)/shard_map/ppermute | solution.py:248
  66.8 1.6 %row_tables.2.refs_11_.refs_3_.refs_7_ = bf16[2,512,512]{2,1,0:T(8,128)(2,1)S(1)} custom-call(s32[2]{0:T(128)S(1)} %pad_add_fusion.refs_0_), custom_call_target="tpu_custom_call" | custom-call | flops 10485760 | bytes 1048576 | tf_op jit(solution)/shard_map/row_tables/pallas_call | solution.py:341
  69.0 2.8 %shard_map.55 = (bf16[128,2048]{1,0:T(8,128)(2,1)S(1)}, bf16[512,512]{1,0:T(8,128)(2,1)S(1)}, bf16[512,512]{1,0:T(8,128)(2,1)S(1)}) custom-call(s32[8,16]{1,0:T(8,128)S(1)} %copy-done.2, bf16[256,512]{1,0:T(8,128)(2,1)S(1)} %pad_maximum_fusion.refs_1_, bf16[64,512]{1,0:T(8,128)(2,1)S(1)} %collective-permute-done.8.refs_2_, ...), custom_call_target="tpu_custom_call" | custom-call | flops 671088640 | bytes 1572864 | tf_op jit(solution)/shard_map/pallas_call | solution.py:473
  71.7 3.1 %shard_map.56 = (bf16[96,2048]{1,0:T(8,128)(2,1)S(1)}, bf16[64,2048]{1,0:T(8,128)(2,1)S(1)}) custom-call(s32[8,16]{1,0:T(8,128)S(1)} %copy-done.2, bf16[512,512]{1,0:T(8,128)(2,1)S(1)} %get-tuple-element.23.refs_1_, bf16[512,512]{1,0:T(8,128)(2,1)S(1)} %get-tuple-element.24.refs_2_, bf16[2,512,512]{2,1,0:T(8,128)(2,1)S(1)} %row_tables.2.refs_11_.refs_3_.refs_7_, ...), custom_call_target="tpu_custom_call" | custom-call | flops 838860800 | bytes 1966080 | tf_op jit(solution)/shard_map/pallas_call | solution.py:473
  75.8 1.4 %pad_add_fusion.1.refs_0_ = s32[2]{0:T(128)S(1)} fusion(s32[1]{0:T(128)} %collective-permute-done.31, s32[1]{0:T(128)} %collective-permute-done.30.index_ref), kind=kLoop, calls=%fused_computation.15 | loop fusion | flops 2 | bytes 16 | tf_op jit(solution)/shard_map/concatenate | solution.py:578
  77.1 1.6 %row_tables.3.refs_8_ = bf16[2,512,512]{2,1,0:T(8,128)(2,1)S(1)} custom-call(s32[2]{0:T(128)S(1)} %pad_add_fusion.1.refs_0_), custom_call_target="tpu_custom_call" | custom-call | flops 10485760 | bytes 1048576 | tf_op jit(solution)/shard_map/row_tables/pallas_call | solution.py:341
  78.7 2.6 %collective-permute-done.34.refs_16_ = bf16[224,2048]{1,0:T(8,128)(2,1)S(1)} collective-permute-done((bf16[224,2048]{1,0:T(8,128)(2,1)S(1)}, bf16[224,2048]{1,0:T(8,128)(2,1)S(1)}, u32[]{:S(2)}, u32[]{:S(2)}) %collective-permute-start.34) | collective-permute-done | bytes 917536 | tf_op jit(solution)/shard_map/ppermute | solution.py:248
  81.4 1.5 %collective-permute-start.22 = (bf16[128,2048]{1,0:T(8,128)(2,1)S(1)}, bf16[128,2048]{1,0:T(8,128)(2,1)S(1)}, u32[]{:S(2)}, u32[]{:S(2)}) collective-permute-start(bf16[128,2048]{1,0:T(8,128)(2,1)S(1)} %get-tuple-element.26), channel_id=1, source_target_pairs={{0,16},{8,24},{16,0},{24,8},{1,17},{9,25},{17,1},{25,9},{2,18},{10... | collective-permute-start | bytes 1572872 | tf_op jit(solution)/shard_map/ppermute | solution.py:248
  82.9 18.2 %collective-permute-done.33.refs_15_ = bf16[224,2048]{1,0:T(8,128)(2,1)S(1)} collective-permute-done((bf16[224,2048]{1,0:T(8,128)(2,1)S(1)}, bf16[224,2048]{1,0:T(8,128)(2,1)S(1)}, u32[]{:S(2)}, u32[]{:S(2)}) %collective-permute-start.33) | collective-permute-done | bytes 917536 | tf_op jit(solution)/shard_map/ppermute | solution.py:248
  101.1 5.3 %shard_map.57 = (bf16[128,2048]{1,0:T(8,128)(2,1)S(1)}, bf16[96,2048]{1,0:T(8,128)(2,1)S(1)}) custom-call(s32[8,16]{1,0:T(8,128)S(1)} %copy-done.2, bf16[512,512]{1,0:T(8,128)(2,1)S(1)} %get-tuple-element.23.refs_1_, bf16[512,512]{1,0:T(8,128)(2,1)S(1)} %get-tuple-element.24.refs_2_, bf16[256,512]{1,0:T(8,128)(2,1)S(1)} %collective-permute-done.26.refs_3_, ...), custom_call_target="tpu_custom_call" | custom-call | flops 2348810240 | bytes 2752512 | tf_op jit(solution)/shard_map/pallas_call | solution.py:473
  108.1 1.4 %collective-permute-done.24 = bf16[96,2048]{1,0:T(8,128)(2,1)S(1)} collective-permute-done((bf16[96,2048]{1,0:T(8,128)(2,1)S(1)}, bf16[96,2048]{1,0:T(8,128)(2,1)S(1)}, u32[]{:S(2)}, u32[]{:S(2)}) %collective-permute-start.24) | collective-permute-done | bytes 393248 | tf_op jit(solution)/shard_map/ppermute | solution.py:248
  109.7 11.0 %collective-permute-done.22 = bf16[128,2048]{1,0:T(8,128)(2,1)S(1)} collective-permute-done((bf16[128,2048]{1,0:T(8,128)(2,1)S(1)}, bf16[128,2048]{1,0:T(8,128)(2,1)S(1)}, u32[]{:S(2)}, u32[]{:S(2)}) %collective-permute-start.22) | collective-permute-done | bytes 524320 | tf_op jit(solution)/shard_map/ppermute | solution.py:248
  121.0 5.4 %collective-permute-done.20 = bf16[64,2048]{1,0:T(8,128)(2,1)S(1)} collective-permute-done((bf16[64,2048]{1,0:T(8,128)(2,1)S(1)}, bf16[64,2048]{1,0:T(8,128)(2,1)S(1)}, u32[]{:S(2)}, u32[]{:S(2)}) %collective-permute-start.20) | collective-permute-done | bytes 262176 | tf_op jit(solution)/shard_map/ppermute | solution.py:248
  127.9 1.3 shard_map.59.refs_2_
  (69 shorter events, 20.3 us)
Async XLA Ops:
  0.0 68.4 %collective-permute-start.19 = (bf16[1,1024,2048]{2,1,0:T(8,128)(2,1)}, bf16[1,1024,2048]{2,1,0:T(8,128)(2,1)S(1)}, u32[]{:S(2)}, u32[]{:S(2)}) collective-permute-start(bf16[1,1024,2048]{2,1,0:T(8,128)(2,1)} %refs_13_.1), channel_id=1, source_target_pairs={{0,8},{8,0},{16,24},{24,16},{1,9},{9,1},{17,25},{25,17},{2,10},{10... | collective-permute-start | bytes 12582920 | tf_op jit(solution)/shard_map/ppermute | solution.py:248
  11.2 7.7 %collective-permute-start.1 = (bf16[1,64,512]{2,1,0:T(8,128)(2,1)S(1)}, bf16[1,64,512]{2,1,0:T(8,128)(2,1)S(1)}, u32[]{:S(2)}, u32[]{:S(2)}) collective-permute-start(bf16[1,64,512]{2,1,0:T(8,128)(2,1)S(1)} %get-tuple-element.21), channel_id=1, source_target_pairs={{0,1},{1,0},{2,3},{3,2},{4,5},{5,4},{6,7},{7,6},{8,9},{9,8},{10,11... | collective-permute-start | bytes 196616 | tf_op jit(solution)/shard_map/ppermute | solution.py:248
  13.8 3.8 %collective-permute-start.30 = (s32[1]{0:T(128)}, s32[1]{0:T(128)}, u32[]{:S(2)}, u32[]{:S(2)}) collective-permute-start(s32[1]{0:T(128)} %param.9), channel_id=1, source_target_pairs={{0,16},{8,24},{16,0},{24,8},{1,17},{9,25},{17,1},{25,9},{2,18},{10... | collective-permute-start | bytes 20 | tf_op jit(solution)/shard_map/ppermute | solution.py:248
  15.3 6.8 %collective-permute-start = (bf16[3,64,512]{2,1,0:T(8,128)(2,1)S(1)}, bf16[3,64,512]{2,1,0:T(8,128)(2,1)S(1)}, u32[]{:S(2)}, u32[]{:S(2)}) collective-permute-start(bf16[3,64,512]{2,1,0:T(8,128)(2,1)S(1)} %get-tuple-element.19), channel_id=1, source_target_pairs={{0,1},{1,0},{2,3},{3,2},{4,5},{5,4},{6,7},{7,6},{8,9},{9,8},{10,11... | collective-permute-start | bytes 589832 | tf_op jit(solution)/shard_map/ppermute | solution.py:248
  15.8 50.4 %collective-permute-start.18 = (bf16[2048,512]{1,0:T(8,128)(2,1)S(1)}, bf16[2048,512]{1,0:T(8,128)(2,1)S(1)}, u32[]{:S(2)}, u32[]{:S(2)}) collective-permute-start(bf16[2048,512]{1,0:T(8,128)(2,1)S(1)} %get-tuple-element.22.refs_12_.refs_4_.refs_9_), channel_id=1, source_target_pairs={{0,8},{8,0},{16,24},{24,16},{1,9},{9,1},{17,25},{25,17},{2,10},{10... | collective-permute-start | bytes 6291464 | tf_op jit(solution)/shard_map/ppermute | solution.py:248
  18.9 82.3 %collective-permute-start.32 = (bf16[2048,512]{1,0:T(8,128)(2,1)S(1)}, bf16[2048,512]{1,0:T(8,128)(2,1)S(1)}, u32[]{:S(2)}, u32[]{:S(2)}) collective-permute-start(bf16[2048,512]{1,0:T(8,128)(2,1)S(1)} %col_table.1.refs_11_), channel_id=1, source_target_pairs={{0,8},{8,0},{16,24},{24,16},{1,9},{9,1},{17,25},{25,17},{2,10},{10... | collective-permute-start | bytes 6291464 | tf_op jit(solution)/shard_map/ppermute | solution.py:248
  19.0 6.9 %collective-permute-start.2 = (bf16[64,512]{1,0:T(8,128)(2,1)S(1)}, bf16[64,512]{1,0:T(8,128)(2,1)S(1)}, u32[]{:S(2)}, u32[]{:S(2)}) collective-permute-start(bf16[64,512]{1,0:T(8,128)(2,1)S(1)} %fusion.3), channel_id=1, source_target_pairs={{0,4},{2,6},{4,0},{6,2},{1,5},{3,7},{5,1},{7,3},{8,12},{10,14},{12... | collective-permute-start | bytes 196616 | tf_op jit(solution)/shard_map/ppermute | solution.py:248
  22.1 7.3 %collective-permute-start.3 = (bf16[64,512]{1,0:T(8,128)(2,1)S(1)}, bf16[64,512]{1,0:T(8,128)(2,1)S(1)}, u32[]{:S(2)}, u32[]{:S(2)}) collective-permute-start(bf16[64,512]{1,0:T(8,128)(2,1)S(1)} %get-tuple-element.31), channel_id=1, source_target_pairs={{0,2},{2,0},{4,6},{6,4},{1,3},{3,1},{5,7},{7,5},{8,10},{10,8},{12,... | collective-permute-start | bytes 196616 | tf_op jit(solution)/shard_map/ppermute | solution.py:248
  25.8 6.1 %collective-permute-start.4 = (bf16[64,512]{1,0:T(8,128)(2,1)S(1)}, bf16[64,512]{1,0:T(8,128)(2,1)S(1)}, u32[]{:S(2)}, u32[]{:S(2)}) collective-permute-start(bf16[64,512]{1,0:T(8,128)(2,1)S(1)} %get-tuple-element.32), channel_id=1, source_target_pairs={{0,6},{2,4},{4,2},{6,0},{1,7},{3,5},{5,3},{7,1},{8,14},{10,12},{12... | collective-permute-start | bytes 196616 | tf_op jit(solution)/shard_map/ppermute | solution.py:248
  29.4 2.5 %collective-permute-start.17 = (s32[1]{0:T(128)}, s32[1]{0:T(128)}, u32[]{:S(2)}, u32[]{:S(2)}) collective-permute-start(s32[1]{0:T(128)} %param.9), channel_id=1, source_target_pairs={{0,8},{8,0},{16,24},{24,16},{1,9},{9,1},{17,25},{25,17},{2,10},{10... | collective-permute-start | bytes 20 | tf_op jit(solution)/shard_map/ppermute | solution.py:248
  32.0 4.6 %collective-permute-start.5 = (bf16[64,512]{1,0:T(8,128)(2,1)S(1)}, bf16[64,512]{1,0:T(8,128)(2,1)S(1)}, u32[]{:S(2)}, u32[]{:S(2)}) collective-permute-start(bf16[64,512]{1,0:T(8,128)(2,1)S(1)} %fusion.2), channel_id=1, source_target_pairs={{0,2},{2,0},{4,6},{6,4},{1,3},{3,1},{5,7},{7,5},{8,10},{10,8},{12,... | collective-permute-start | bytes 196616 | tf_op jit(solution)/shard_map/ppermute | solution.py:248
  33.3 7.0 %collective-permute-start.6 = (bf16[64,512]{1,0:T(8,128)(2,1)S(1)}, bf16[64,512]{1,0:T(8,128)(2,1)S(1)}, u32[]{:S(2)}, u32[]{:S(2)}) collective-permute-start(bf16[64,512]{1,0:T(8,128)(2,1)S(1)} %fusion.2), channel_id=1, source_target_pairs={{0,4},{2,6},{4,0},{6,2},{1,5},{3,7},{5,1},{7,3},{8,12},{10,14},{12... | collective-permute-start | bytes 196616 | tf_op jit(solution)/shard_map/ppermute | solution.py:248
  36.5 6.2 %collective-permute-start.7 = (bf16[64,512]{1,0:T(8,128)(2,1)S(1)}, bf16[64,512]{1,0:T(8,128)(2,1)S(1)}, u32[]{:S(2)}, u32[]{:S(2)}) collective-permute-start(bf16[64,512]{1,0:T(8,128)(2,1)S(1)} %fusion.2), channel_id=1, source_target_pairs={{0,6},{2,4},{4,2},{6,0},{1,7},{3,5},{5,3},{7,1},{8,14},{10,12},{12... | collective-permute-start | bytes 196616 | tf_op jit(solution)/shard_map/ppermute | solution.py:248
  40.2 4.9 %collective-permute-start.8 = (bf16[64,512]{1,0:T(8,128)(2,1)S(1)}, bf16[64,512]{1,0:T(8,128)(2,1)S(1)}, u32[]{:S(2)}, u32[]{:S(2)}) collective-permute-start(bf16[64,512]{1,0:T(8,128)(2,1)S(1)} %fusion.2), channel_id=1, source_target_pairs={{0,1},{1,0},{2,3},{3,2},{4,5},{5,4},{6,7},{7,6},{8,9},{9,8},{10,11... | collective-permute-start | bytes 196616 | tf_op jit(solution)/shard_map/ppermute | solution.py:248
  42.7 4.3 %collective-permute-start.9 = (bf16[64,512]{1,0:T(8,128)(2,1)S(1)}, bf16[64,512]{1,0:T(8,128)(2,1)S(1)}, u32[]{:S(2)}, u32[]{:S(2)}) collective-permute-start(bf16[64,512]{1,0:T(8,128)(2,1)S(1)} %collective-permute-done.5), channel_id=1, source_target_pairs={{0,1},{1,0},{2,3},{3,2},{4,5},{5,4},{6,7},{7,6},{8,9},{9,8},{10,11... | collective-permute-start | bytes 196616 | tf_op jit(solution)/shard_map/ppermute | solution.py:248
  45.2 4.3 %collective-permute-start.10 = (bf16[64,512]{1,0:T(8,128)(2,1)S(1)}, bf16[64,512]{1,0:T(8,128)(2,1)S(1)}, u32[]{:S(2)}, u32[]{:S(2)}) collective-permute-start(bf16[64,512]{1,0:T(8,128)(2,1)S(1)} %collective-permute-done.6), channel_id=1, source_target_pairs={{0,1},{1,0},{2,3},{3,2},{4,5},{5,4},{6,7},{7,6},{8,9},{9,8},{10,11... | collective-permute-start | bytes 196616 | tf_op jit(solution)/shard_map/ppermute | solution.py:248
  47.0 4.3 %collective-permute-start.11 = (bf16[64,512]{1,0:T(8,128)(2,1)S(1)}, bf16[64,512]{1,0:T(8,128)(2,1)S(1)}, u32[]{:S(2)}, u32[]{:S(2)}) collective-permute-start(bf16[64,512]{1,0:T(8,128)(2,1)S(1)} %collective-permute-done.7), channel_id=1, source_target_pairs={{0,1},{1,0},{2,3},{3,2},{4,5},{5,4},{6,7},{7,6},{8,9},{9,8},{10,11... | collective-permute-start | bytes 196616 | tf_op jit(solution)/shard_map/ppermute | solution.py:248
  49.5 3.1 %collective-permute-start.13 = (bf16[64,512]{1,0:T(8,128)(2,1)S(1)}, bf16[64,512]{1,0:T(8,128)(2,1)S(1)}, u32[]{:S(2)}, u32[]{:S(2)}) collective-permute-start(bf16[64,512]{1,0:T(8,128)(2,1)S(1)} %collective-permute-done.8.refs_2_), channel_id=1, source_target_pairs={{0,8},{8,0},{16,24},{24,16},{1,9},{9,1},{17,25},{25,17},{2,10},{10... | collective-permute-start | bytes 196616 | tf_op jit(solution)/shard_map/ppermute | solution.py:248
  51.2 7.0 %collective-permute-start.26 = (bf16[256,512]{1,0:T(8,128)(2,1)S(1)}, bf16[256,512]{1,0:T(8,128)(2,1)S(1)}, u32[]{:S(2)}, u32[]{:S(2)}) collective-permute-start(bf16[256,512]{1,0:T(8,128)(2,1)S(1)} %pad_maximum_fusion.refs_1_), channel_id=1, source_target_pairs={{0,16},{8,24},{16,0},{24,8},{1,17},{9,25},{17,1},{25,9},{2,18},{10... | collective-permute-start | bytes 786440 | tf_op jit(solution)/shard_map/ppermute | solution.py:248
  58.3 6.7 %collective-permute-start.27 = (bf16[256,512]{1,0:T(8,128)(2,1)S(1)}, bf16[256,512]{1,0:T(8,128)(2,1)S(1)}, u32[]{:S(2)}, u32[]{:S(2)}) collective-permute-start(bf16[256,512]{1,0:T(8,128)(2,1)S(1)} %collective-permute-done.26.refs_3_), channel_id=1, source_target_pairs={{0,1},{1,0},{2,3},{3,2},{4,5},{5,4},{6,7},{7,6},{8,9},{9,8},{10,11... | collective-permute-start | bytes 786440 | tf_op jit(solution)/shard_map/ppermute | solution.py:248
  58.8 22.6 %collective-permute-start.34 = (bf16[224,2048]{1,0:T(8,128)(2,1)S(1)}, bf16[224,2048]{1,0:T(8,128)(2,1)S(1)}, u32[]{:S(2)}, u32[]{:S(2)}) collective-permute-start(bf16[224,2048]{1,0:T(8,128)(2,1)S(1)} %get-tuple-element.28), channel_id=1, source_target_pairs={{0,24},{8,16},{16,8},{24,0},{1,25},{9,17},{17,9},{25,1},{2,26},{10... | collective-permute-start | bytes 2752520 | tf_op jit(solution)/shard_map/ppermute | solution.py:248
  65.0 36.1 %collective-permute-start.33 = (bf16[224,2048]{1,0:T(8,128)(2,1)S(1)}, bf16[224,2048]{1,0:T(8,128)(2,1)S(1)}, u32[]{:S(2)}, u32[]{:S(2)}) collective-permute-start(bf16[224,2048]{1,0:T(8,128)(2,1)S(1)} %own_slice.1), channel_id=1, source_target_pairs={{0,16},{8,24},{16,0},{24,8},{1,17},{9,25},{17,1},{25,9},{2,18},{10... | collective-permute-start | bytes 2752520 | tf_op jit(solution)/shard_map/ppermute | solution.py:248
  66.2 8.7 %collective-permute-start.28 = (bf16[256,512]{1,0:T(8,128)(2,1)S(1)}, bf16[256,512]{1,0:T(8,128)(2,1)S(1)}, u32[]{:S(2)}, u32[]{:S(2)}) collective-permute-start(bf16[256,512]{1,0:T(8,128)(2,1)S(1)} %collective-permute-done.26.refs_3_), channel_id=1, source_target_pairs={{0,8},{8,0},{16,24},{24,16},{1,9},{9,1},{17,25},{25,17},{2,10},{10... | collective-permute-start | bytes 786440 | tf_op jit(solution)/shard_map/ppermute | solution.py:248
  68.4 32.7 %collective-permute-start.29 = (bf16[256,512]{1,0:T(8,128)(2,1)S(1)}, bf16[256,512]{1,0:T(8,128)(2,1)S(1)}, u32[]{:S(2)}, u32[]{:S(2)}) collective-permute-start(bf16[256,512]{1,0:T(8,128)(2,1)S(1)} %collective-permute-done.27.refs_4_), channel_id=1, source_target_pairs={{0,8},{8,0},{16,24},{24,16},{1,9},{9,1},{17,25},{25,17},{2,10},{10... | collective-permute-start | bytes 786440 | tf_op jit(solution)/shard_map/ppermute | solution.py:248
  74.8 34.7 %collective-permute-start.24 = (bf16[96,2048]{1,0:T(8,128)(2,1)S(1)}, bf16[96,2048]{1,0:T(8,128)(2,1)S(1)}, u32[]{:S(2)}, u32[]{:S(2)}) collective-permute-start(bf16[96,2048]{1,0:T(8,128)(2,1)S(1)} %get-tuple-element.27), channel_id=1, source_target_pairs={{0,16},{8,24},{16,0},{24,8},{1,17},{9,25},{17,1},{25,9},{2,18},{10... | collective-permute-start | bytes 1179656 | tf_op jit(solution)/shard_map/ppermute | solution.py:248
  81.4 39.4 %collective-permute-start.22 = (bf16[128,2048]{1,0:T(8,128)(2,1)S(1)}, bf16[128,2048]{1,0:T(8,128)(2,1)S(1)}, u32[]{:S(2)}, u32[]{:S(2)}) collective-permute-start(bf16[128,2048]{1,0:T(8,128)(2,1)S(1)} %get-tuple-element.26), channel_id=1, source_target_pairs={{0,16},{8,24},{16,0},{24,8},{1,17},{9,25},{17,1},{25,9},{2,18},{10... | collective-permute-start | bytes 1572872 | tf_op jit(solution)/shard_map/ppermute | solution.py:248
  106.4 20.1 %collective-permute-start.35 = (bf16[128,2048]{1,0:T(8,128)(2,1)S(1)}, bf16[128,2048]{1,0:T(8,128)(2,1)S(1)}, u32[]{:S(2)}, u32[]{:S(2)}) collective-permute-start(bf16[128,2048]{1,0:T(8,128)(2,1)S(1)} %get-tuple-element.29.refs_0_), channel_id=1, source_target_pairs={{0,8},{8,0},{16,24},{24,16},{1,9},{9,1},{17,25},{25,17},{2,10},{10... | collective-permute-start | bytes 1572872 | tf_op jit(solution)/shard_map/ppermute | solution.py:248
  106.5 20.1 %collective-permute-start.36 = (bf16[96,2048]{1,0:T(8,128)(2,1)S(1)}, bf16[96,2048]{1,0:T(8,128)(2,1)S(1)}, u32[]{:S(2)}, u32[]{:S(2)}) collective-permute-start(bf16[96,2048]{1,0:T(8,128)(2,1)S(1)} %get-tuple-element.30.refs_2_), channel_id=1, source_target_pairs={{0,8},{8,0},{16,24},{24,16},{1,9},{9,1},{17,25},{25,17},{2,10},{10... | collective-permute-start | bytes 1179656 | tf_op jit(solution)/shard_map/ppermute | solution.py:248
  107.0 19.4 %collective-permute-start.20 = (bf16[64,2048]{1,0:T(8,128)(2,1)S(1)}, bf16[64,2048]{1,0:T(8,128)(2,1)S(1)}, u32[]{:S(2)}, u32[]{:S(2)}) collective-permute-start(bf16[64,2048]{1,0:T(8,128)(2,1)S(1)} %get-tuple-element.25), channel_id=1, source_target_pairs={{0,16},{8,24},{16,0},{24,8},{1,17},{9,25},{17,1},{25,9},{2,18},{10... | collective-permute-start | bytes 786440 | tf_op jit(solution)/shard_map/ppermute | solution.py:248
  109.7 18.2 %collective-permute-start.25 = (bf16[96,2048]{1,0:T(8,128)(2,1)S(1)}, bf16[96,2048]{1,0:T(8,128)(2,1)S(1)}, u32[]{:S(2)}, u32[]{:S(2)}) collective-permute-start(bf16[96,2048]{1,0:T(8,128)(2,1)S(1)} %add_convert_fusion.1.refs_2_), channel_id=1, source_target_pairs={{0,8},{8,0},{16,24},{24,16},{1,9},{9,1},{17,25},{25,17},{2,10},{10... | collective-permute-start | bytes 1179656 | tf_op jit(solution)/shard_map/ppermute | solution.py:248
  120.9 6.9 %collective-permute-start.23 = (bf16[128,2048]{1,0:T(8,128)(2,1)S(1)}, bf16[128,2048]{1,0:T(8,128)(2,1)S(1)}, u32[]{:S(2)}, u32[]{:S(2)}) collective-permute-start(bf16[128,2048]{1,0:T(8,128)(2,1)S(1)} %add_convert_fusion.refs_0_), channel_id=1, source_target_pairs={{0,8},{8,0},{16,24},{24,16},{1,9},{9,1},{17,25},{25,17},{2,10},{10... | collective-permute-start | bytes 1572872 | tf_op jit(solution)/shard_map/ppermute | solution.py:248
  126.4 2.7 %collective-permute-start.21 = (bf16[64,2048]{1,0:T(8,128)(2,1)S(1)}, bf16[64,2048]{1,0:T(8,128)(2,1)S(1)}, u32[]{:S(2)}, u32[]{:S(2)}) collective-permute-start(bf16[64,2048]{1,0:T(8,128)(2,1)S(1)} %add_convert_fusion.2.refs_0_), channel_id=1, source_target_pairs={{0,8},{8,0},{16,24},{24,16},{1,9},{9,1},{17,25},{25,17},{2,10},{10... | collective-permute-start | bytes 786440 | tf_op jit(solution)/shard_map/ppermute | solution.py:248
  (8 other events, 108.5 us)

commit v5 on v4

--- a/solution.py
+++ b/solution.py
@@ -256,7 +256,7 @@
 
 
 def hop_order(n_row):
-    return sorted(range(1, n_row), key=lambda k: -(k & -k))
+    return list(range(n_row - 1, 0, -1))
 
 
 def slot_groups(n_row, n_col):
@@ -285,10 +285,7 @@
 
 
 def gather_row(mine, n_row):
-    found = {0: mine}
-    for kz in hop_order(n_row):
-        found[kz] = swap(mine, "row", kz)
-    return [found[kz] for kz in range(n_row)]
+    return [mine] + [swap(mine, "row", kz) for kz in hop_order(n_row)]
 
 
 def aligned(pieces):
@@ -305,7 +302,8 @@
     per = M // (n_row * n_col)
     lane = lax.broadcasted_iota(jnp.int32, (16, M), 1)
     block = lane // per
-    owner = ((block // n_row) ^ col_at) * n_row + ((block % n_row) ^ row_at)
+    hops = (n_row - block % n_row) % n_row
+    owner = ((block // n_row) ^ col_at) * n_row + (hops ^ row_at)
     place = owner * per + lane % per
     is_sin = place >= HALF
     focal = 2.0 * jnp.where(is_sin, place - HALF, place).astype(F32) + 1.0
@@ -580,9 +578,11 @@
     col_cross = swap(col_straight, "wl", 1)
 
     here = gather_row(mine, n_row)
+    joined = jnp.concatenate(here, axis=0)
     if n_row > 4:
-        here = [jnp.concatenate(here, axis=0)]
-    joined = jnp.concatenate(here, axis=0)
+        here = [joined]
+    elif n_row > 2:
+        here = here[:2] + [jnp.concatenate(here[2:], axis=0)]
     pieces, pieces_core = [joined], [swap(joined, "wl", 1)]
     for ky in range(1, n_col):
         for piece in here:

time: 130 us -> 129 us (level)
    ppermute x37 -> x35, starting transfers between devices: 29.8 us -> 28.9 us  [swap(): return lax.ppermute(value, axis, [(i, i ^ bits) for i in range(size)])]
    ppermute x37 -> x35, waiting for transfers between devices: 66.8 us -> 66.3 us  [swap(): return lax.ppermute(value, axis, [(i, i ^ bits) for i in range(size)])]
  transfers between devices with their start and end apart: 37 -> 35, of which waited for: 22 -> 19; matrix products, arithmetic and copies ran while one was open for 2% -> 2% of each run, Pallas kernels for 22% -> 22%
where the time goes in v5:
time: 129 us
  waiting for transfers between devices  66.3 us (51%)
  starting transfers between devices  28.9 us (22%)
  Pallas kernels  28.8 us (22%)
  other arithmetic  2.39 us (2%)
  between operations  1.73 us (1%)
    ppermute x35, waiting for transfers between devices, swap(): return lax.ppermute(value, axis, [(i, i ^ bits) for i in range(size)])  66.3 us
    ppermute x35, starting transfers between devices, swap(): return lax.ppermute(value, axis, [(i, i ^ bits) for i in range(size)])  28.9 us
    pallas_call x3, Pallas kernels, backward(): pl.pallas_call(kernel, in_specs=[pl.BlockSpec(memory_space=pltpu.SMEM)] +...  11.1 us
    pallas_call x1, Pallas kernels, forward(): pl.pallas_call(kernel, in_specs=[smem, smem, smem, hbm, hbm], out_specs=[...  8.72 us
    pallas_call x3, Pallas kernels, place(): pl.pallas_call(kernel, in_specs=[hbm] * len(operands), out_specs=hbm, out...  3.37 us
    pallas_call x2, Pallas kernels, row_tables(): pl.pallas_call(kernel, in_specs=[pl.BlockSpec(memory_space=pltpu.SMEM)],...  3.21 us
  transfers between devices with their start and end apart: 35, of which 19 were waited for; matrix products, arithmetic and copies ran while one was open for 2% of the time, Pallas kernels for 22%

profile of v5, /device:TPU:0, one launch (start us, length us, event | category | flops | bytes accessed | tf_op | source)
XLA Modules:
  0.0 128.8 jit_solution(1376223950869986560)
XLA Ops:
  2.5 8.7 %forward.1 = (bf16[1,64,512]{2,1,0:T(8,128)(2,1)S(1)}, bf16[1,64,512]{2,1,0:T(8,128)(2,1)S(1)}, bf16[3,64,512]{2,1,0:T(8,128)(2,1)S(1)}, bf16[3,64,512]{2,1,0:T(...) custom-call(s32[1]{0:T(128)S(6)} %copy.11.refs_0_, s32[1]{0:T(128)S(6)} %copy.10.refs_1_, ...), custom_call_target="tpu_custom_call" | custom-call | flops 5368709120 | bytes 8388608 | tf_op jit(solution)/shard_map/forward/pallas_call | solution.py:224
  11.2 2.6 %collective-permute-start.1 = (bf16[1,64,512]{2,1,0:T(8,128)(2,1)S(1)}, bf16[1,64,512]{2,1,0:T(8,128)(2,1)S(1)}, u32[]{:S(2)}, u32[]{:S(2)}) collective-permute-start(bf16[1,64,512]{2,1,0:T(8,128)(2,1)S(1)} %get-tuple-element.21), channel_id=1, source_target_pairs={{0,1},{1,0},{2,3},{3,2},{4,5},{5,4},{6,7},{7,6},{8,9},{9,8},{10,11... | collective-permute-start | bytes 196616 | tf_op jit(solution)/shard_map/ppermute | solution.py:248
  13.8 1.5 %collective-permute-start.28 = (s32[1]{0:T(128)}, s32[1]{0:T(128)}, u32[]{:S(2)}, u32[]{:S(2)}) collective-permute-start(s32[1]{0:T(128)} %param.9), channel_id=1, source_target_pairs={{0,16},{8,24},{16,0},{24,8},{1,17},{9,25},{17,1},{25,9},{2,18},{10... | collective-permute-start | bytes 20 | tf_op jit(solution)/shard_map/ppermute | solution.py:248
  16.6 3.9 %collective-permute-start.2 = (bf16[64,512]{1,0:T(8,128)(2,1)S(1)}, bf16[64,512]{1,0:T(8,128)(2,1)S(1)}, u32[]{:S(2)}, u32[]{:S(2)}) collective-permute-start(bf16[64,512]{1,0:T(8,128)(2,1)S(1)} %fusion.3), channel_id=1, source_target_pairs={{0,6},{2,4},{4,2},{6,0},{1,7},{3,5},{5,3},{7,1},{8,14},{10,12},{12... | collective-permute-start | bytes 196616 | tf_op jit(solution)/shard_map/ppermute | solution.py:248
  20.5 1.6 %collective-permute-done = bf16[3,64,512]{2,1,0:T(8,128)(2,1)S(1)} collective-permute-done((bf16[3,64,512]{2,1,0:T(8,128)(2,1)S(1)}, bf16[3,64,512]{2,1,0:T(8,128)(2,1)S(1)}, u32[]{:S(2)}, u32[]{:S(2)}) %collective-permute-start) | collective-permute-done | bytes 196640 | tf_op jit(solution)/shard_map/ppermute | solution.py:248
  22.1 2.6 %collective-permute-start.3 = (bf16[64,512]{1,0:T(8,128)(2,1)S(1)}, bf16[64,512]{1,0:T(8,128)(2,1)S(1)}, u32[]{:S(2)}, u32[]{:S(2)}) collective-permute-start(bf16[64,512]{1,0:T(8,128)(2,1)S(1)} %get-tuple-element.31), channel_id=1, source_target_pairs={{0,4},{2,6},{4,0},{6,2},{1,5},{3,7},{5,1},{7,3},{8,12},{10,14},{12... | collective-permute-start | bytes 196616 | tf_op jit(solution)/shard_map/ppermute | solution.py:248
  24.8 1.6 %collective-permute-start.4 = (bf16[64,512]{1,0:T(8,128)(2,1)S(1)}, bf16[64,512]{1,0:T(8,128)(2,1)S(1)}, u32[]{:S(2)}, u32[]{:S(2)}) collective-permute-start(bf16[64,512]{1,0:T(8,128)(2,1)S(1)} %get-tuple-element.32), channel_id=1, source_target_pairs={{0,2},{2,0},{4,6},{6,4},{1,3},{3,1},{5,7},{7,5},{8,10},{10,8},{12,... | collective-permute-start | bytes 196616 | tf_op jit(solution)/shard_map/ppermute | solution.py:248
  27.6 1.4 %collective-permute-done.4 = bf16[64,512]{1,0:T(8,128)(2,1)S(1)} collective-permute-done((bf16[64,512]{1,0:T(8,128)(2,1)S(1)}, bf16[64,512]{1,0:T(8,128)(2,1)S(1)}, u32[]{:S(2)}, u32[]{:S(2)}) %collective-permute-start.4) | collective-permute-done | bytes 65568 | tf_op jit(solution)/shard_map/ppermute | solution.py:248
  30.2 1.7 %collective-permute-done.15 = s32[1]{0:T(128)} collective-permute-done((s32[1]{0:T(128)}, s32[1]{0:T(128)}, u32[]{:S(2)}, u32[]{:S(2)}) %collective-permute-start.15) | collective-permute-done | bytes 36 | tf_op jit(solution)/shard_map/ppermute | solution.py:248
  33.3 1.8 %collective-permute-start.7 = (bf16[64,512]{1,0:T(8,128)(2,1)S(1)}, bf16[64,512]{1,0:T(8,128)(2,1)S(1)}, u32[]{:S(2)}, u32[]{:S(2)}) collective-permute-start(bf16[64,512]{1,0:T(8,128)(2,1)S(1)} %fusion.2), channel_id=1, source_target_pairs={{0,2},{2,0},{4,6},{6,4},{1,3},{3,1},{5,7},{7,5},{8,10},{10,8},{12,... | collective-permute-start | bytes 196616 | tf_op jit(solution)/shard_map/ppermute | solution.py:248
  35.0 2.0 %collective-permute-start.5 = (bf16[64,512]{1,0:T(8,128)(2,1)S(1)}, bf16[64,512]{1,0:T(8,128)(2,1)S(1)}, u32[]{:S(2)}, u32[]{:S(2)}) collective-permute-start(bf16[64,512]{1,0:T(8,128)(2,1)S(1)} %fusion.2), channel_id=1, source_target_pairs={{0,6},{2,4},{4,2},{6,0},{1,7},{3,5},{5,3},{7,1},{8,14},{10,12},{12... | collective-permute-start | bytes 196616 | tf_op jit(solution)/shard_map/ppermute | solution.py:248
  38.0 3.1 %collective-permute-done.5 = bf16[64,512]{1,0:T(8,128)(2,1)S(1)} collective-permute-done((bf16[64,512]{1,0:T(8,128)(2,1)S(1)}, bf16[64,512]{1,0:T(8,128)(2,1)S(1)}, u32[]{:S(2)}, u32[]{:S(2)}) %collective-permute-start.5) | collective-permute-done | bytes 65568 | tf_op jit(solution)/shard_map/ppermute | solution.py:248
  41.8 1.4 %collective-permute-start.10 = (bf16[128,512]{1,0:T(8,128)(2,1)S(1)}, bf16[128,512]{1,0:T(8,128)(2,1)S(1)}, u32[]{:S(2)}, u32[]{:S(2)}) collective-permute-start(bf16[128,512]{1,0:T(8,128)(2,1)S(1)} %pad_maximum_fusion.1), channel_id=1, source_target_pairs={{0,1},{1,0},{2,3},{3,2},{4,5},{5,4},{6,7},{7,6},{8,9},{9,8},{10,11... | collective-permute-start | bytes 393224 | tf_op jit(solution)/shard_map/ppermute | solution.py:248
  43.2 2.2 %collective-permute-done.9.refs_3_ = bf16[64,512]{1,0:T(8,128)(2,1)S(1)} collective-permute-done((bf16[64,512]{1,0:T(8,128)(2,1)S(1)}, bf16[64,512]{1,0:T(8,128)(2,1)S(1)}, u32[]{:S(2)}, u32[]{:S(2)}) %collective-permute-start.9) | collective-permute-done | bytes 65568 | tf_op jit(solution)/shard_map/ppermute | solution.py:248
  45.4 1.2 collective-permute-done.12.refs_6_
  47.7 1.3 collective-permute-done.13.refs_7_
  49.1 5.9 %collective-permute-done.24.refs_3_ = bf16[256,512]{1,0:T(8,128)(2,1)S(1)} collective-permute-done((bf16[256,512]{1,0:T(8,128)(2,1)S(1)}, bf16[256,512]{1,0:T(8,128)(2,1)S(1)}, u32[]{:S(2)}, u32[]{:S(2)}) %collective-permute-start.24) | collective-permute-done | bytes 262176 | tf_op jit(solution)/shard_map/ppermute | solution.py:248
  56.1 1.3 %collective-permute-done.14.refs_8_ = bf16[128,512]{1,0:T(8,128)(2,1)S(1)} collective-permute-done((bf16[128,512]{1,0:T(8,128)(2,1)S(1)}, bf16[128,512]{1,0:T(8,128)(2,1)S(1)}, u32[]{:S(2)}, u32[]{:S(2)}) %collective-permute-start.14) | collective-permute-done | bytes 131104 | tf_op jit(solution)/shard_map/ppermute | solution.py:248
  59.3 3.2 %collective-permute-done.25.refs_4_ = bf16[256,512]{1,0:T(8,128)(2,1)S(1)} collective-permute-done((bf16[256,512]{1,0:T(8,128)(2,1)S(1)}, bf16[256,512]{1,0:T(8,128)(2,1)S(1)}, u32[]{:S(2)}, u32[]{:S(2)}) %collective-permute-start.25) | collective-permute-done | bytes 262176 | tf_op jit(solution)/shard_map/ppermute | solution.py:248
  64.3 1.6 %row_tables.2.refs_9_.refs_3_.refs_7_ = bf16[2,512,512]{2,1,0:T(8,128)(2,1)S(1)} custom-call(s32[2]{0:T(128)S(1)} %pad_add_fusion.refs_0_), custom_call_target="tpu_custom_call" | custom-call | flops 10485760 | bytes 1048576 | tf_op jit(solution)/shard_map/row_tables/pallas_call | solution.py:339
  66.5 2.8 %shard_map.55 = (bf16[128,2048]{1,0:T(8,128)(2,1)S(1)}, bf16[512,512]{1,0:T(8,128)(2,1)S(1)}, bf16[512,512]{1,0:T(8,128)(2,1)S(1)}) custom-call(s32[8,16]{1,0:T(8,128)S(1)} %copy-done.2, bf16[256,512]{1,0:T(8,128)(2,1)S(1)} %pad_maximum_fusion.refs_1_, bf16[64,512]{1,0:T(8,128)(2,1)S(1)} %collective-permute-done.8.refs_2_, ...), custom_call_target="tpu_custom_call" | custom-call | flops 671088640 | bytes 1572864 | tf_op jit(solution)/shard_map/pallas_call | solution.py:471
  69.2 3.1 %shard_map.56 = (bf16[96,2048]{1,0:T(8,128)(2,1)S(1)}, bf16[64,2048]{1,0:T(8,128)(2,1)S(1)}) custom-call(s32[8,16]{1,0:T(8,128)S(1)} %copy-done.2, bf16[512,512]{1,0:T(8,128)(2,1)S(1)} %get-tuple-element.23.refs_1_, bf16[512,512]{1,0:T(8,128)(2,1)S(1)} %get-tuple-element.24.refs_2_, bf16[2,512,512]{2,1,0:T(8,128)(2,1)S(1)} %row_tables.2.refs_9_.refs_3_.refs_7_, ...), custom_call_target="tpu_custom_call" | custom-call | flops 838860800 | bytes 1966080 | tf_op jit(solution)/shard_map/pallas_call | solution.py:471
  73.3 1.3 pad_add_fusion.1.refs_0_
  74.6 1.6 %row_tables.3.refs_8_ = bf16[2,512,512]{2,1,0:T(8,128)(2,1)S(1)} custom-call(s32[2]{0:T(128)S(1)} %pad_add_fusion.1.refs_0_), custom_call_target="tpu_custom_call" | custom-call | flops 10485760 | bytes 1048576 | tf_op jit(solution)/shard_map/row_tables/pallas_call | solution.py:339
  76.2 3.6 %collective-permute-done.32.refs_16_ = bf16[224,2048]{1,0:T(8,128)(2,1)S(1)} collective-permute-done((bf16[224,2048]{1,0:T(8,128)(2,1)S(1)}, bf16[224,2048]{1,0:T(8,128)(2,1)S(1)}, u32[]{:S(2)}, u32[]{:S(2)}) %collective-permute-start.32) | collective-permute-done | bytes 917536 | tf_op jit(solution)/shard_map/ppermute | solution.py:248
  80.6 19.5 %collective-permute-done.31.refs_15_ = bf16[224,2048]{1,0:T(8,128)(2,1)S(1)} collective-permute-done((bf16[224,2048]{1,0:T(8,128)(2,1)S(1)}, bf16[224,2048]{1,0:T(8,128)(2,1)S(1)}, u32[]{:S(2)}, u32[]{:S(2)}) %collective-permute-start.31) | collective-permute-done | bytes 917536 | tf_op jit(solution)/shard_map/ppermute | solution.py:248
  100.1 5.3 %shard_map.57 = (bf16[128,2048]{1,0:T(8,128)(2,1)S(1)}, bf16[96,2048]{1,0:T(8,128)(2,1)S(1)}) custom-call(s32[8,16]{1,0:T(8,128)S(1)} %copy-done.2, bf16[512,512]{1,0:T(8,128)(2,1)S(1)} %get-tuple-element.23.refs_1_, bf16[512,512]{1,0:T(8,128)(2,1)S(1)} %get-tuple-element.24.refs_2_, bf16[256,512]{1,0:T(8,128)(2,1)S(1)} %collective-permute-done.24.refs_3_, ...), custom_call_target="tpu_custom_call" | custom-call | flops 2348810240 | bytes 2752512 | tf_op jit(solution)/shard_map/pallas_call | solution.py:471
  106.8 1.7 %collective-permute-done.22 = bf16[96,2048]{1,0:T(8,128)(2,1)S(1)} collective-permute-done((bf16[96,2048]{1,0:T(8,128)(2,1)S(1)}, bf16[96,2048]{1,0:T(8,128)(2,1)S(1)}, u32[]{:S(2)}, u32[]{:S(2)}) %collective-permute-start.22) | collective-permute-done | bytes 393248 | tf_op jit(solution)/shard_map/ppermute | solution.py:248
  108.7 11.1 %collective-permute-done.20 = bf16[128,2048]{1,0:T(8,128)(2,1)S(1)} collective-permute-done((bf16[128,2048]{1,0:T(8,128)(2,1)S(1)}, bf16[128,2048]{1,0:T(8,128)(2,1)S(1)}, u32[]{:S(2)}, u32[]{:S(2)}) %collective-permute-start.20) | collective-permute-done | bytes 524320 | tf_op jit(solution)/shard_map/ppermute | solution.py:248
  120.0 5.1 %collective-permute-done.18 = bf16[64,2048]{1,0:T(8,128)(2,1)S(1)} collective-permute-done((bf16[64,2048]{1,0:T(8,128)(2,1)S(1)}, bf16[64,2048]{1,0:T(8,128)(2,1)S(1)}, u32[]{:S(2)}, u32[]{:S(2)}) %collective-permute-start.18) | collective-permute-done | bytes 262176 | tf_op jit(solution)/shard_map/ppermute | solution.py:248
  125.2 1.3 shard_map.58.refs_4_
  126.5 1.3 shard_map.59.refs_2_
  (66 shorter events, 19.3 us)
Async XLA Ops:
  0.0 65.9 %collective-permute-start.17 = (bf16[1,1024,2048]{2,1,0:T(8,128)(2,1)}, bf16[1,1024,2048]{2,1,0:T(8,128)(2,1)S(1)}, u32[]{:S(2)}, u32[]{:S(2)}) collective-permute-start(bf16[1,1024,2048]{2,1,0:T(8,128)(2,1)} %refs_13_.1), channel_id=1, source_target_pairs={{0,8},{8,0},{16,24},{24,16},{1,9},{9,1},{17,25},{25,17},{2,10},{10... | collective-permute-start | bytes 12582920 | tf_op jit(solution)/shard_map/ppermute | solution.py:248
  11.2 5.3 %collective-permute-start.1 = (bf16[1,64,512]{2,1,0:T(8,128)(2,1)S(1)}, bf16[1,64,512]{2,1,0:T(8,128)(2,1)S(1)}, u32[]{:S(2)}, u32[]{:S(2)}) collective-permute-start(bf16[1,64,512]{2,1,0:T(8,128)(2,1)S(1)} %get-tuple-element.21), channel_id=1, source_target_pairs={{0,1},{1,0},{2,3},{3,2},{4,5},{5,4},{6,7},{7,6},{8,9},{9,8},{10,11... | collective-permute-start | bytes 196616 | tf_op jit(solution)/shard_map/ppermute | solution.py:248
  13.8 11.0 %collective-permute-start.28 = (s32[1]{0:T(128)}, s32[1]{0:T(128)}, u32[]{:S(2)}, u32[]{:S(2)}) collective-permute-start(s32[1]{0:T(128)} %param.9), channel_id=1, source_target_pairs={{0,16},{8,24},{16,0},{24,8},{1,17},{9,25},{17,1},{25,9},{2,18},{10... | collective-permute-start | bytes 20 | tf_op jit(solution)/shard_map/ppermute | solution.py:248
  15.3 6.8 %collective-permute-start = (bf16[3,64,512]{2,1,0:T(8,128)(2,1)S(1)}, bf16[3,64,512]{2,1,0:T(8,128)(2,1)S(1)}, u32[]{:S(2)}, u32[]{:S(2)}) collective-permute-start(bf16[3,64,512]{2,1,0:T(8,128)(2,1)S(1)} %get-tuple-element.19), channel_id=1, source_target_pairs={{0,1},{1,0},{2,3},{3,2},{4,5},{5,4},{6,7},{7,6},{8,9},{9,8},{10,11... | collective-permute-start | bytes 589832 | tf_op jit(solution)/shard_map/ppermute | solution.py:248
  15.8 47.8 %collective-permute-start.16 = (bf16[2048,512]{1,0:T(8,128)(2,1)S(1)}, bf16[2048,512]{1,0:T(8,128)(2,1)S(1)}, u32[]{:S(2)}, u32[]{:S(2)}) collective-permute-start(bf16[2048,512]{1,0:T(8,128)(2,1)S(1)} %get-tuple-element.22.refs_10_.refs_4_.refs_9_), channel_id=1, source_target_pairs={{0,8},{8,0},{16,24},{24,16},{1,9},{9,1},{17,25},{25,17},{2,10},{10... | collective-permute-start | bytes 6291464 | tf_op jit(solution)/shard_map/ppermute | solution.py:248
  16.6 11.0 %collective-permute-start.2 = (bf16[64,512]{1,0:T(8,128)(2,1)S(1)}, bf16[64,512]{1,0:T(8,128)(2,1)S(1)}, u32[]{:S(2)}, u32[]{:S(2)}) collective-permute-start(bf16[64,512]{1,0:T(8,128)(2,1)S(1)} %fusion.3), channel_id=1, source_target_pairs={{0,6},{2,4},{4,2},{6,0},{1,7},{3,5},{5,3},{7,1},{8,14},{10,12},{12... | collective-permute-start | bytes 196616 | tf_op jit(solution)/shard_map/ppermute | solution.py:248
  22.1 5.5 %collective-permute-start.3 = (bf16[64,512]{1,0:T(8,128)(2,1)S(1)}, bf16[64,512]{1,0:T(8,128)(2,1)S(1)}, u32[]{:S(2)}, u32[]{:S(2)}) collective-permute-start(bf16[64,512]{1,0:T(8,128)(2,1)S(1)} %get-tuple-element.31), channel_id=1, source_target_pairs={{0,4},{2,6},{4,0},{6,2},{1,5},{3,7},{5,1},{7,3},{8,12},{10,14},{12... | collective-permute-start | bytes 196616 | tf_op jit(solution)/shard_map/ppermute | solution.py:248
  24.8 4.3 %collective-permute-start.4 = (bf16[64,512]{1,0:T(8,128)(2,1)S(1)}, bf16[64,512]{1,0:T(8,128)(2,1)S(1)}, u32[]{:S(2)}, u32[]{:S(2)}) collective-permute-start(bf16[64,512]{1,0:T(8,128)(2,1)S(1)} %get-tuple-element.32), channel_id=1, source_target_pairs={{0,2},{2,0},{4,6},{6,4},{1,3},{3,1},{5,7},{7,5},{8,10},{10,8},{12,... | collective-permute-start | bytes 196616 | tf_op jit(solution)/shard_map/ppermute | solution.py:248
  27.6 72.6 %collective-permute-start.30 = (bf16[2048,512]{1,0:T(8,128)(2,1)S(1)}, bf16[2048,512]{1,0:T(8,128)(2,1)S(1)}, u32[]{:S(2)}, u32[]{:S(2)}) collective-permute-start(bf16[2048,512]{1,0:T(8,128)(2,1)S(1)} %col_table.1.refs_11_), channel_id=1, source_target_pairs={{0,8},{8,0},{16,24},{24,16},{1,9},{9,1},{17,25},{25,17},{2,10},{10... | collective-permute-start | bytes 6291464 | tf_op jit(solution)/shard_map/ppermute | solution.py:248
  29.1 6.0 %collective-permute-start.6 = (bf16[64,512]{1,0:T(8,128)(2,1)S(1)}, bf16[64,512]{1,0:T(8,128)(2,1)S(1)}, u32[]{:S(2)}, u32[]{:S(2)}) collective-permute-start(bf16[64,512]{1,0:T(8,128)(2,1)S(1)} %fusion.2), channel_id=1, source_target_pairs={{0,4},{2,6},{4,0},{6,2},{1,5},{3,7},{5,1},{7,3},{8,12},{10,14},{12... | collective-permute-start | bytes 196616 | tf_op jit(solution)/shard_map/ppermute | solution.py:248
  30.2 1.7 %collective-permute-start.15 = (s32[1]{0:T(128)}, s32[1]{0:T(128)}, u32[]{:S(2)}, u32[]{:S(2)}) collective-permute-start(s32[1]{0:T(128)} %param.9), channel_id=1, source_target_pairs={{0,8},{8,0},{16,24},{24,16},{1,9},{9,1},{17,25},{25,17},{2,10},{10... | collective-permute-start | bytes 20 | tf_op jit(solution)/shard_map/ppermute | solution.py:248
  31.9 1.4 %collective-permute-start.29 = (s32[1]{0:T(128)}, s32[1]{0:T(128)}, u32[]{:S(2)}, u32[]{:S(2)}) collective-permute-start(s32[1]{0:T(128)} %collective-permute-done.28.index_ref), channel_id=1, source_target_pairs={{0,8},{8,0},{16,24},{24,16},{1,9},{9,1},{17,25},{25,17},{2,10},{10... | collective-permute-start | bytes 20 | tf_op jit(solution)/shard_map/ppermute | solution.py:248
  33.3 4.3 %collective-permute-start.7 = (bf16[64,512]{1,0:T(8,128)(2,1)S(1)}, bf16[64,512]{1,0:T(8,128)(2,1)S(1)}, u32[]{:S(2)}, u32[]{:S(2)}) collective-permute-start(bf16[64,512]{1,0:T(8,128)(2,1)S(1)} %fusion.2), channel_id=1, source_target_pairs={{0,2},{2,0},{4,6},{6,4},{1,3},{3,1},{5,7},{7,5},{8,10},{10,8},{12,... | collective-permute-start | bytes 196616 | tf_op jit(solution)/shard_map/ppermute | solution.py:248
  35.0 6.1 %collective-permute-start.5 = (bf16[64,512]{1,0:T(8,128)(2,1)S(1)}, bf16[64,512]{1,0:T(8,128)(2,1)S(1)}, u32[]{:S(2)}, u32[]{:S(2)}) collective-permute-start(bf16[64,512]{1,0:T(8,128)(2,1)S(1)} %fusion.2), channel_id=1, source_target_pairs={{0,6},{2,4},{4,2},{6,0},{1,7},{3,5},{5,3},{7,1},{8,14},{10,12},{12... | collective-permute-start | bytes 196616 | tf_op jit(solution)/shard_map/ppermute | solution.py:248
  37.5 4.3 %collective-permute-start.8 = (bf16[64,512]{1,0:T(8,128)(2,1)S(1)}, bf16[64,512]{1,0:T(8,128)(2,1)S(1)}, u32[]{:S(2)}, u32[]{:S(2)}) collective-permute-start(bf16[64,512]{1,0:T(8,128)(2,1)S(1)} %fusion.2), channel_id=1, source_target_pairs={{0,1},{1,0},{2,3},{3,2},{4,5},{5,4},{6,7},{7,6},{8,9},{9,8},{10,11... | collective-permute-start | bytes 196616 | tf_op jit(solution)/shard_map/ppermute | solution.py:248
  41.1 4.3 %collective-permute-start.9 = (bf16[64,512]{1,0:T(8,128)(2,1)S(1)}, bf16[64,512]{1,0:T(8,128)(2,1)S(1)}, u32[]{:S(2)}, u32[]{:S(2)}) collective-permute-start(bf16[64,512]{1,0:T(8,128)(2,1)S(1)} %collective-permute-done.5), channel_id=1, source_target_pairs={{0,1},{1,0},{2,3},{3,2},{4,5},{5,4},{6,7},{7,6},{8,9},{9,8},{10,11... | collective-permute-start | bytes 196616 | tf_op jit(solution)/shard_map/ppermute | solution.py:248
  41.8 5.9 %collective-permute-start.10 = (bf16[128,512]{1,0:T(8,128)(2,1)S(1)}, bf16[128,512]{1,0:T(8,128)(2,1)S(1)}, u32[]{:S(2)}, u32[]{:S(2)}) collective-permute-start(bf16[128,512]{1,0:T(8,128)(2,1)S(1)} %pad_maximum_fusion.1), channel_id=1, source_target_pairs={{0,1},{1,0},{2,3},{3,2},{4,5},{5,4},{6,7},{7,6},{8,9},{9,8},{10,11... | collective-permute-start | bytes 393224 | tf_op jit(solution)/shard_map/ppermute | solution.py:248
  46.6 8.4 %collective-permute-start.24 = (bf16[256,512]{1,0:T(8,128)(2,1)S(1)}, bf16[256,512]{1,0:T(8,128)(2,1)S(1)}, u32[]{:S(2)}, u32[]{:S(2)}) collective-permute-start(bf16[256,512]{1,0:T(8,128)(2,1)S(1)} %pad_maximum_fusion.refs_1_), channel_id=1, source_target_pairs={{0,16},{8,24},{16,0},{24,8},{1,17},{9,25},{17,1},{25,9},{2,18},{10... | collective-permute-start | bytes 786440 | tf_op jit(solution)/shard_map/ppermute | solution.py:248
  49.0 7.2 %collective-permute-start.11 = (bf16[256,512]{1,0:T(8,128)(2,1)S(1)}, bf16[256,512]{1,0:T(8,128)(2,1)S(1)}, u32[]{:S(2)}, u32[]{:S(2)}) collective-permute-start(bf16[256,512]{1,0:T(8,128)(2,1)S(1)} %pad_maximum_fusion.refs_1_), channel_id=1, source_target_pairs={{0,8},{8,0},{16,24},{24,16},{1,9},{9,1},{17,25},{25,17},{2,10},{10... | collective-permute-start | bytes 786440 | tf_op jit(solution)/shard_map/ppermute | solution.py:248
  55.0 7.5 %collective-permute-start.25 = (bf16[256,512]{1,0:T(8,128)(2,1)S(1)}, bf16[256,512]{1,0:T(8,128)(2,1)S(1)}, u32[]{:S(2)}, u32[]{:S(2)}) collective-permute-start(bf16[256,512]{1,0:T(8,128)(2,1)S(1)} %collective-permute-done.24.refs_3_), channel_id=1, source_target_pairs={{0,1},{1,0},{2,3},{3,2},{4,5},{5,4},{6,7},{7,6},{8,9},{9,8},{10,11... | collective-permute-start | bytes 786440 | tf_op jit(solution)/shard_map/ppermute | solution.py:248
  57.5 22.3 %collective-permute-start.32 = (bf16[224,2048]{1,0:T(8,128)(2,1)S(1)}, bf16[224,2048]{1,0:T(8,128)(2,1)S(1)}, u32[]{:S(2)}, u32[]{:S(2)}) collective-permute-start(bf16[224,2048]{1,0:T(8,128)(2,1)S(1)} %get-tuple-element.28), channel_id=1, source_target_pairs={{0,24},{8,16},{16,8},{24,0},{1,25},{9,17},{17,9},{25,1},{2,26},{10... | collective-permute-start | bytes 2752520 | tf_op jit(solution)/shard_map/ppermute | solution.py:248
  62.5 37.6 %collective-permute-start.31 = (bf16[224,2048]{1,0:T(8,128)(2,1)S(1)}, bf16[224,2048]{1,0:T(8,128)(2,1)S(1)}, u32[]{:S(2)}, u32[]{:S(2)}) collective-permute-start(bf16[224,2048]{1,0:T(8,128)(2,1)S(1)} %own_slice.1), channel_id=1, source_target_pairs={{0,16},{8,24},{16,0},{24,8},{1,17},{9,25},{17,1},{25,9},{2,18},{10... | collective-permute-start | bytes 2752520 | tf_op jit(solution)/shard_map/ppermute | solution.py:248
  63.6 8.7 %collective-permute-start.26 = (bf16[256,512]{1,0:T(8,128)(2,1)S(1)}, bf16[256,512]{1,0:T(8,128)(2,1)S(1)}, u32[]{:S(2)}, u32[]{:S(2)}) collective-permute-start(bf16[256,512]{1,0:T(8,128)(2,1)S(1)} %collective-permute-done.24.refs_3_), channel_id=1, source_target_pairs={{0,8},{8,0},{16,24},{24,16},{1,9},{9,1},{17,25},{25,17},{2,10},{10... | collective-permute-start | bytes 786440 | tf_op jit(solution)/shard_map/ppermute | solution.py:248
  65.9 34.2 %collective-permute-start.27 = (bf16[256,512]{1,0:T(8,128)(2,1)S(1)}, bf16[256,512]{1,0:T(8,128)(2,1)S(1)}, u32[]{:S(2)}, u32[]{:S(2)}) collective-permute-start(bf16[256,512]{1,0:T(8,128)(2,1)S(1)} %collective-permute-done.25.refs_4_), channel_id=1, source_target_pairs={{0,8},{8,0},{16,24},{24,16},{1,9},{9,1},{17,25},{25,17},{2,10},{10... | collective-permute-start | bytes 786440 | tf_op jit(solution)/shard_map/ppermute | solution.py:248
  72.3 36.2 %collective-permute-start.22 = (bf16[96,2048]{1,0:T(8,128)(2,1)S(1)}, bf16[96,2048]{1,0:T(8,128)(2,1)S(1)}, u32[]{:S(2)}, u32[]{:S(2)}) collective-permute-start(bf16[96,2048]{1,0:T(8,128)(2,1)S(1)} %get-tuple-element.27), channel_id=1, source_target_pairs={{0,16},{8,24},{16,0},{24,8},{1,17},{9,25},{17,1},{25,9},{2,18},{10... | collective-permute-start | bytes 1179656 | tf_op jit(solution)/shard_map/ppermute | solution.py:248
  79.8 40.0 %collective-permute-start.20 = (bf16[128,2048]{1,0:T(8,128)(2,1)S(1)}, bf16[128,2048]{1,0:T(8,128)(2,1)S(1)}, u32[]{:S(2)}, u32[]{:S(2)}) collective-permute-start(bf16[128,2048]{1,0:T(8,128)(2,1)S(1)} %get-tuple-element.26), channel_id=1, source_target_pairs={{0,16},{8,24},{16,0},{24,8},{1,17},{9,25},{17,1},{25,9},{2,18},{10... | collective-permute-start | bytes 1572872 | tf_op jit(solution)/shard_map/ppermute | solution.py:248
  105.4 19.8 %collective-permute-start.33 = (bf16[128,2048]{1,0:T(8,128)(2,1)S(1)}, bf16[128,2048]{1,0:T(8,128)(2,1)S(1)}, u32[]{:S(2)}, u32[]{:S(2)}) collective-permute-start(bf16[128,2048]{1,0:T(8,128)(2,1)S(1)} %get-tuple-element.29.refs_0_), channel_id=1, source_target_pairs={{0,8},{8,0},{16,24},{24,16},{1,9},{9,1},{17,25},{25,17},{2,10},{10... | collective-permute-start | bytes 1572872 | tf_op jit(solution)/shard_map/ppermute | solution.py:248
  105.5 19.7 %collective-permute-start.34 = (bf16[96,2048]{1,0:T(8,128)(2,1)S(1)}, bf16[96,2048]{1,0:T(8,128)(2,1)S(1)}, u32[]{:S(2)}, u32[]{:S(2)}) collective-permute-start(bf16[96,2048]{1,0:T(8,128)(2,1)S(1)} %get-tuple-element.30.refs_2_), channel_id=1, source_target_pairs={{0,8},{8,0},{16,24},{24,16},{1,9},{9,1},{17,25},{25,17},{2,10},{10... | collective-permute-start | bytes 1179656 | tf_op jit(solution)/shard_map/ppermute | solution.py:248
  106.0 19.1 %collective-permute-start.18 = (bf16[64,2048]{1,0:T(8,128)(2,1)S(1)}, bf16[64,2048]{1,0:T(8,128)(2,1)S(1)}, u32[]{:S(2)}, u32[]{:S(2)}) collective-permute-start(bf16[64,2048]{1,0:T(8,128)(2,1)S(1)} %get-tuple-element.25), channel_id=1, source_target_pairs={{0,16},{8,24},{16,0},{24,8},{1,17},{9,25},{17,1},{25,9},{2,18},{10... | collective-permute-start | bytes 786440 | tf_op jit(solution)/shard_map/ppermute | solution.py:248
  108.6 17.9 %collective-permute-start.23 = (bf16[96,2048]{1,0:T(8,128)(2,1)S(1)}, bf16[96,2048]{1,0:T(8,128)(2,1)S(1)}, u32[]{:S(2)}, u32[]{:S(2)}) collective-permute-start(bf16[96,2048]{1,0:T(8,128)(2,1)S(1)} %add_convert_fusion.1.refs_2_), channel_id=1, source_target_pairs={{0,8},{8,0},{16,24},{24,16},{1,9},{9,1},{17,25},{25,17},{2,10},{10... | collective-permute-start | bytes 1179656 | tf_op jit(solution)/shard_map/ppermute | solution.py:248
  119.9 6.6 %collective-permute-start.21 = (bf16[128,2048]{1,0:T(8,128)(2,1)S(1)}, bf16[128,2048]{1,0:T(8,128)(2,1)S(1)}, u32[]{:S(2)}, u32[]{:S(2)}) collective-permute-start(bf16[128,2048]{1,0:T(8,128)(2,1)S(1)} %add_convert_fusion.refs_0_), channel_id=1, source_target_pairs={{0,8},{8,0},{16,24},{24,16},{1,9},{9,1},{17,25},{25,17},{2,10},{10... | collective-permute-start | bytes 1572872 | tf_op jit(solution)/shard_map/ppermute | solution.py:248
  125.1 2.7 %collective-permute-start.19 = (bf16[64,2048]{1,0:T(8,128)(2,1)S(1)}, bf16[64,2048]{1,0:T(8,128)(2,1)S(1)}, u32[]{:S(2)}, u32[]{:S(2)}) collective-permute-start(bf16[64,2048]{1,0:T(8,128)(2,1)S(1)} %add_convert_fusion.2.refs_0_), channel_id=1, source_target_pairs={{0,8},{8,0},{16,24},{24,16},{1,9},{9,1},{17,25},{25,17},{2,10},{10... | collective-permute-start | bytes 786440 | tf_op jit(solution)/shard_map/ppermute | solution.py:248
  (6 other events, 88.0 us)

commit v6 on v4

--- a/solution.py
+++ b/solution.py
@@ -115,20 +115,15 @@
 
 
 def forward_kernel(index_ref, charge_ref, tiles_ref, cot_ref, inc_ref, *refs, rows, cols, n_row, groups, begin):
-    outs, (col_tab, slice_ref) = refs[:-8], refs[-8:-6]
-    row_tab, inner, fine_ref, t_ref, held, sems = refs[-6:]
+    outs, (col_tab, slice_ref) = refs[:-7], refs[-7:-5]
+    row_tab, inner, fine_ref, t_ref, sem = refs[-5:]
     block = min(256, rows)
     extent = rows * n_row
     row_at = lax.axis_index("row")
     col_at = lax.axis_index("col")
     tile_size = rows // tiles_ref.shape[0]
-    copies = []
-    for step in range(rows // block):
-        span = pl.ds(step * block, block)
-        copies.append(pltpu.make_async_copy(cot_ref.at[0, :, span, :], held.at[:, span, :], sems.at[step]))
-        copies[-1].start()
     half_at = lax.rem(lax.axis_index("wl"), 2)
-    slice_copy = slice_rows(inc_ref, slice_ref, sems.at[rows // block], 1 - half_at, begin)
+    slice_copy = slice_rows(inc_ref, slice_ref, sem, 1 - half_at, begin)
     slice_copy.start()
     period = quarter_period(index_ref[0])
 
@@ -145,12 +140,11 @@
     table_pupil_lanes(write_row, period, row_at * rows, extent, rows, fine_ref, 0.0, HALF)
 
     for step in range(rows // block):
-        copies[step].wait()
         halves = []
         for part in range(2):
             for at in range(step * block, (step + 1) * block, tile_size):
                 mask = live_row(tiles_ref, at // tile_size, cols).astype(BF16)
-                halves.append(held[part, at : at + tile_size, :] * mask)
+                halves.append(cot_ref[0, part, at : at + tile_size, :] * mask)
         prod = jnp.dot(jnp.concatenate(halves, axis=0), col_tab[...], preferred_element_type=F32)
         at = step * block
         inner[at : at + block, :M] = prod[:block].astype(BF16)
@@ -211,7 +205,6 @@
 
 def forward(index, charge, tiles, cotangent, incident, begin, n_row, n_col, groups):
     rows, cols = cotangent.shape[2:]
-    block = min(256, rows)
     per = M // (n_row * n_col)
     out_shape = [jax.ShapeDtypeStruct((len(slots), per, M), BF16) for _, slots in groups]
     out_shape.append(jax.ShapeDtypeStruct((cols, M), BF16))
@@ -223,7 +216,7 @@
     hbm, smem = pl.BlockSpec(memory_space=pltpu.HBM), pl.BlockSpec(memory_space=pltpu.SMEM)
     outs = pl.pallas_call(
         kernel,
-        in_specs=[smem, smem, smem, hbm, hbm],
+        in_specs=[smem, smem, smem, pl.BlockSpec(memory_space=pltpu.VMEM), hbm],
         out_specs=[pl.BlockSpec(memory_space=pltpu.VMEM)] * len(out_shape),
         out_shape=out_shape,
         scratch_shapes=[
@@ -231,15 +224,14 @@
             pltpu.VMEM((rows, 2 * M), BF16),
             pltpu.VMEM((2, HALF, HALF), F32),
             pltpu.VMEM((n_row * n_col, per, M), F32),
-            pltpu.VMEM((2, rows, cols), BF16),
-            pltpu.SemaphoreType.DMA((rows // block + 1,)),
+            pltpu.SemaphoreType.DMA,
         ],
         compiler_params=pltpu.CompilerParams(vmem_limit_bytes=36 << 20),
         cost_estimate=pl.CostEstimate(
             flops=2 * rows * 2 * M * (cols + M), bytes_accessed=4 * rows * cols, transcendentals=0
         ),
         name="forward",
-    )(index, charge, tiles, in_hbm(cotangent), in_hbm(incident))
+    )(index, charge, tiles, cotangent, in_hbm(incident))
     return outs[:-2], outs[-2], outs[-1]
 
 
@@ -542,7 +534,7 @@
         out_shape=jax.ShapeDtypeStruct((amount, cols), BF16),
         scratch_shapes=[pltpu.SemaphoreType.DMA],
         compiler_params=pltpu.CompilerParams(vmem_limit_bytes=4 << 20),
-        cost_estimate=pl.CostEstimate(flops=0, bytes_accessed=4 * amount * cols, transcendentals=0),
+        cost_estimate=pl.CostEstimate(flops=4 << 30, bytes_accessed=4 * amount * cols, transcendentals=0),
         name="own_slice",
     )(in_hbm(incident))
 

time: 130 us -> 133 us (1.023)
  local copies, waits for them, and re-layouts: 0.71 us -> 4.08 us
  waiting for transfers between devices: 66.8 us -> 68.5 us
  Pallas kernels: 28.8 us -> 27.2 us
    unnamed x6 -> x8, local copies, waits for them, and re-layouts: 0.69 us -> 4.07 us
    ppermute x37, waiting for transfers between devices: 66.8 us -> 68.5 us  [swap(): return lax.ppermute(value, axis, [(i, i ^ bits) for i in range(size)])]
    pallas_call x1, Pallas kernels: 8.72 us -> 7.07 us  [forward(): pl.pallas_call(kernel, in_specs=[smem, smem, smem, pl.BlockSpec(memory_sp...]
  transfers between devices with their start and end apart: 37 -> 37, of which waited for: 22 -> 19; matrix products, arithmetic and copies ran while one was open for 2% -> 2% of each run, Pallas kernels for 22% -> 20%
where the time goes in v6:
time: 133 us; the launch traced here: 132 us
  waiting for transfers between devices  68.5 us (52%)
  starting transfers between devices  28.5 us (21%)
  Pallas kernels  27.2 us (20%)
  local copies, waits for them, and re-layouts  4.08 us (3%)
  other arithmetic  2.4 us (2%)
  between operations  1.76 us (1%)
    ppermute x37, waiting for transfers between devices, swap(): return lax.ppermute(value, axis, [(i, i ^ bits) for i in range(size)])  68.5 us
    ppermute x37, starting transfers between devices, swap(): return lax.ppermute(value, axis, [(i, i ^ bits) for i in range(size)])  28.5 us
    pallas_call x3, Pallas kernels, backward(): pl.pallas_call(kernel, in_specs=[pl.BlockSpec(memory_space=pltpu.SMEM)] +...  11.1 us
    pallas_call x1, Pallas kernels, forward(): pl.pallas_call(kernel, in_specs=[smem, smem, smem, pl.BlockSpec(memory_sp...  7.07 us
    unnamed x8, local copies, waits for them, and re-layouts  4.07 us
    pallas_call x3, Pallas kernels, place(): pl.pallas_call(kernel, in_specs=[hbm] * len(operands), out_specs=hbm, out...  3.37 us
    pallas_call x2, Pallas kernels, row_tables(): pl.pallas_call(kernel, in_specs=[pl.BlockSpec(memory_space=pltpu.SMEM)],...  3.2 us
  transfers between devices with their start and end apart: 37, of which 19 were waited for; matrix products, arithmetic and copies ran while one was open for 2% of the time, Pallas kernels for 20%

profile of v6, /device:TPU:0, one launch (start us, length us, event | category | flops | bytes accessed | tf_op | source)
XLA Modules:
  0.0 132.4 jit_solution(6469038007841269590)
XLA Ops:
  2.5 3.4 %copy-done.3 = bf16[1,2,1024,2048]{3,2,1,0:T(8,128)(2,1)S(1)} copy-done((bf16[1,2,1024,2048]{3,2,1,0:T(8,128)(2,1)S(1)}, bf16[1,2,1024,2048]{3,2,1,0:T(8,128)(2,1)}, u32[]{:S(2)}) %copy-start.3) | copy-done | bytes 8388632
  5.9 7.1 %forward.1 = (bf16[1,64,512]{2,1,0:T(8,128)(2,1)S(1)}, bf16[1,64,512]{2,1,0:T(8,128)(2,1)S(1)}, bf16[3,64,512]{2,1,0:T(8,128)(2,1)S(1)}, bf16[3,64,512]{2,1,0:T(...) custom-call(s32[1]{0:T(128)S(6)} %copy.11.refs_0_, s32[1]{0:T(128)S(6)} %copy.10.refs_1_, ...), custom_call_target="tpu_custom_call" | custom-call | flops 5368709120 | bytes 8388608 | tf_op jit(solution)/shard_map/forward/pallas_call | solution.py:217
  12.9 2.6 %collective-permute-start.1 = (bf16[1,64,512]{2,1,0:T(8,128)(2,1)S(1)}, bf16[1,64,512]{2,1,0:T(8,128)(2,1)S(1)}, u32[]{:S(2)}, u32[]{:S(2)}) collective-permute-start(bf16[1,64,512]{2,1,0:T(8,128)(2,1)S(1)} %get-tuple-element.21), channel_id=1, source_target_pairs={{0,1},{1,0},{2,3},{3,2},{4,5},{5,4},{6,7},{7,6},{8,9},{9,8},{10,11... | collective-permute-start | bytes 196616 | tf_op jit(solution)/shard_map/ppermute | solution.py:240
  15.5 1.5 %collective-permute-start.30 = (s32[1]{0:T(128)}, s32[1]{0:T(128)}, u32[]{:S(2)}, u32[]{:S(2)}) collective-permute-start(s32[1]{0:T(128)} %param.9), channel_id=1, source_target_pairs={{0,16},{8,24},{16,0},{24,8},{1,17},{9,25},{17,1},{25,9},{2,18},{10... | collective-permute-start | bytes 20 | tf_op jit(solution)/shard_map/ppermute | solution.py:240
  18.3 2.9 %collective-permute-start.2 = (bf16[64,512]{1,0:T(8,128)(2,1)S(1)}, bf16[64,512]{1,0:T(8,128)(2,1)S(1)}, u32[]{:S(2)}, u32[]{:S(2)}) collective-permute-start(bf16[64,512]{1,0:T(8,128)(2,1)S(1)} %fusion.3), channel_id=1, source_target_pairs={{0,4},{2,6},{4,0},{6,2},{1,5},{3,7},{5,1},{7,3},{8,12},{10,14},{12... | collective-permute-start | bytes 196616 | tf_op jit(solution)/shard_map/ppermute | solution.py:240
  21.2 2.6 %collective-permute-done = bf16[3,64,512]{2,1,0:T(8,128)(2,1)S(1)} collective-permute-done((bf16[3,64,512]{2,1,0:T(8,128)(2,1)S(1)}, bf16[3,64,512]{2,1,0:T(8,128)(2,1)S(1)}, u32[]{:S(2)}, u32[]{:S(2)}) %collective-permute-start) | collective-permute-done | bytes 196640 | tf_op jit(solution)/shard_map/ppermute | solution.py:240
  23.8 1.6 %collective-permute-start.3 = (bf16[64,512]{1,0:T(8,128)(2,1)S(1)}, bf16[64,512]{1,0:T(8,128)(2,1)S(1)}, u32[]{:S(2)}, u32[]{:S(2)}) collective-permute-start(bf16[64,512]{1,0:T(8,128)(2,1)S(1)} %get-tuple-element.31), channel_id=1, source_target_pairs={{0,2},{2,0},{4,6},{6,4},{1,3},{3,1},{5,7},{7,5},{8,10},{10,8},{12,... | collective-permute-start | bytes 196616 | tf_op jit(solution)/shard_map/ppermute | solution.py:240
  25.5 2.5 %collective-permute-start.4 = (bf16[64,512]{1,0:T(8,128)(2,1)S(1)}, bf16[64,512]{1,0:T(8,128)(2,1)S(1)}, u32[]{:S(2)}, u32[]{:S(2)}) collective-permute-start(bf16[64,512]{1,0:T(8,128)(2,1)S(1)} %get-tuple-element.32), channel_id=1, source_target_pairs={{0,6},{2,4},{4,2},{6,0},{1,7},{3,5},{5,3},{7,1},{8,14},{10,12},{12... | collective-permute-start | bytes 196616 | tf_op jit(solution)/shard_map/ppermute | solution.py:240
  27.9 1.3 col_table.1.refs_11_
  29.4 2.2 %collective-permute-done.4 = bf16[64,512]{1,0:T(8,128)(2,1)S(1)} collective-permute-done((bf16[64,512]{1,0:T(8,128)(2,1)S(1)}, bf16[64,512]{1,0:T(8,128)(2,1)S(1)}, u32[]{:S(2)}, u32[]{:S(2)}) %collective-permute-start.4) | collective-permute-done | bytes 65568 | tf_op jit(solution)/shard_map/ppermute | solution.py:240
  31.7 1.7 %collective-permute-done.17 = s32[1]{0:T(128)} collective-permute-done((s32[1]{0:T(128)}, s32[1]{0:T(128)}, u32[]{:S(2)}, u32[]{:S(2)}) %collective-permute-start.17) | collective-permute-done | bytes 36 | tf_op jit(solution)/shard_map/ppermute | solution.py:240
  33.6 1.2 collective-permute-done.31
  34.8 2.5 %collective-permute-start.6 = (bf16[64,512]{1,0:T(8,128)(2,1)S(1)}, bf16[64,512]{1,0:T(8,128)(2,1)S(1)}, u32[]{:S(2)}, u32[]{:S(2)}) collective-permute-start(bf16[64,512]{1,0:T(8,128)(2,1)S(1)} %fusion.2), channel_id=1, source_target_pairs={{0,4},{2,6},{4,0},{6,2},{1,5},{3,7},{5,1},{7,3},{8,12},{10,14},{12... | collective-permute-start | bytes 196616 | tf_op jit(solution)/shard_map/ppermute | solution.py:240
  37.3 1.4 %collective-permute-start.7 = (bf16[64,512]{1,0:T(8,128)(2,1)S(1)}, bf16[64,512]{1,0:T(8,128)(2,1)S(1)}, u32[]{:S(2)}, u32[]{:S(2)}) collective-permute-start(bf16[64,512]{1,0:T(8,128)(2,1)S(1)} %fusion.2), channel_id=1, source_target_pairs={{0,6},{2,4},{4,2},{6,0},{1,7},{3,5},{5,3},{7,1},{8,14},{10,12},{12... | collective-permute-start | bytes 196616 | tf_op jit(solution)/shard_map/ppermute | solution.py:240
  38.7 4.8 %collective-permute-done.6 = bf16[64,512]{1,0:T(8,128)(2,1)S(1)} collective-permute-done((bf16[64,512]{1,0:T(8,128)(2,1)S(1)}, bf16[64,512]{1,0:T(8,128)(2,1)S(1)}, u32[]{:S(2)}, u32[]{:S(2)}) %collective-permute-start.6) | collective-permute-done | bytes 65568 | tf_op jit(solution)/shard_map/ppermute | solution.py:240
  44.0 1.5 %collective-permute-start.9 = (bf16[64,512]{1,0:T(8,128)(2,1)S(1)}, bf16[64,512]{1,0:T(8,128)(2,1)S(1)}, u32[]{:S(2)}, u32[]{:S(2)}) collective-permute-start(bf16[64,512]{1,0:T(8,128)(2,1)S(1)} %collective-permute-done.5), channel_id=1, source_target_pairs={{0,1},{1,0},{2,3},{3,2},{4,5},{5,4},{6,7},{7,6},{8,9},{9,8},{10,11... | collective-permute-start | bytes 196616 | tf_op jit(solution)/shard_map/ppermute | solution.py:240
  45.5 2.2 %collective-permute-done.8.refs_2_ = bf16[64,512]{1,0:T(8,128)(2,1)S(1)} collective-permute-done((bf16[64,512]{1,0:T(8,128)(2,1)S(1)}, bf16[64,512]{1,0:T(8,128)(2,1)S(1)}, u32[]{:S(2)}, u32[]{:S(2)}) %collective-permute-start.8) | collective-permute-done | bytes 65568 | tf_op jit(solution)/shard_map/ppermute | solution.py:240
  49.9 2.2 %collective-permute-done.10.refs_4_ = bf16[64,512]{1,0:T(8,128)(2,1)S(1)} collective-permute-done((bf16[64,512]{1,0:T(8,128)(2,1)S(1)}, bf16[64,512]{1,0:T(8,128)(2,1)S(1)}, u32[]{:S(2)}, u32[]{:S(2)}) %collective-permute-start.10) | collective-permute-done | bytes 65568 | tf_op jit(solution)/shard_map/ppermute | solution.py:240
  57.2 7.7 %collective-permute-done.26.refs_3_ = bf16[256,512]{1,0:T(8,128)(2,1)S(1)} collective-permute-done((bf16[256,512]{1,0:T(8,128)(2,1)S(1)}, bf16[256,512]{1,0:T(8,128)(2,1)S(1)}, u32[]{:S(2)}, u32[]{:S(2)}) %collective-permute-start.26) | collective-permute-done | bytes 262176 | tf_op jit(solution)/shard_map/ppermute | solution.py:240
  67.0 4.6 %collective-permute-done.27.refs_4_ = bf16[256,512]{1,0:T(8,128)(2,1)S(1)} collective-permute-done((bf16[256,512]{1,0:T(8,128)(2,1)S(1)}, bf16[256,512]{1,0:T(8,128)(2,1)S(1)}, u32[]{:S(2)}, u32[]{:S(2)}) %collective-permute-start.27) | collective-permute-done | bytes 262176 | tf_op jit(solution)/shard_map/ppermute | solution.py:240
  73.3 1.6 %row_tables.2.refs_11_.refs_3_.refs_7_ = bf16[2,512,512]{2,1,0:T(8,128)(2,1)S(1)} custom-call(s32[2]{0:T(128)S(1)} %pad_add_fusion.refs_0_), custom_call_target="tpu_custom_call" | custom-call | flops 10485760 | bytes 1048576 | tf_op jit(solution)/shard_map/row_tables/pallas_call | solution.py:333
  75.5 2.8 %shard_map.55 = (bf16[128,2048]{1,0:T(8,128)(2,1)S(1)}, bf16[512,512]{1,0:T(8,128)(2,1)S(1)}, bf16[512,512]{1,0:T(8,128)(2,1)S(1)}) custom-call(s32[8,16]{1,0:T(8,128)S(1)} %copy-done.2, bf16[256,512]{1,0:T(8,128)(2,1)S(1)} %pad_maximum_fusion.refs_1_, bf16[64,512]{1,0:T(8,128)(2,1)S(1)} %collective-permute-done.8.refs_2_, ...), custom_call_target="tpu_custom_call" | custom-call | flops 671088640 | bytes 1572864 | tf_op jit(solution)/shard_map/pallas_call | solution.py:465
  78.2 3.1 %shard_map.56 = (bf16[96,2048]{1,0:T(8,128)(2,1)S(1)}, bf16[64,2048]{1,0:T(8,128)(2,1)S(1)}) custom-call(s32[8,16]{1,0:T(8,128)S(1)} %copy-done.2, bf16[512,512]{1,0:T(8,128)(2,1)S(1)} %get-tuple-element.23.refs_1_, bf16[512,512]{1,0:T(8,128)(2,1)S(1)} %get-tuple-element.24.refs_2_, bf16[2,512,512]{2,1,0:T(8,128)(2,1)S(1)} %row_tables.2.refs_11_.refs_3_.refs_7_, ...), custom_call_target="tpu_custom_call" | custom-call | flops 838860800 | bytes 1966080 | tf_op jit(solution)/shard_map/pallas_call | solution.py:465
  82.4 1.3 pad_add_fusion.1.refs_0_
  83.7 1.6 %row_tables.3.refs_8_ = bf16[2,512,512]{2,1,0:T(8,128)(2,1)S(1)} custom-call(s32[2]{0:T(128)S(1)} %pad_add_fusion.1.refs_0_), custom_call_target="tpu_custom_call" | custom-call | flops 10485760 | bytes 1048576 | tf_op jit(solution)/shard_map/row_tables/pallas_call | solution.py:333
  86.4 17.9 %collective-permute-done.33.refs_15_ = bf16[224,2048]{1,0:T(8,128)(2,1)S(1)} collective-permute-done((bf16[224,2048]{1,0:T(8,128)(2,1)S(1)}, bf16[224,2048]{1,0:T(8,128)(2,1)S(1)}, u32[]{:S(2)}, u32[]{:S(2)}) %collective-permute-start.33) | collective-permute-done | bytes 917536 | tf_op jit(solution)/shard_map/ppermute | solution.py:240
  104.2 5.3 %shard_map.57 = (bf16[128,2048]{1,0:T(8,128)(2,1)S(1)}, bf16[96,2048]{1,0:T(8,128)(2,1)S(1)}) custom-call(s32[8,16]{1,0:T(8,128)S(1)} %copy-done.2, bf16[512,512]{1,0:T(8,128)(2,1)S(1)} %get-tuple-element.23.refs_1_, bf16[512,512]{1,0:T(8,128)(2,1)S(1)} %get-tuple-element.24.refs_2_, bf16[256,512]{1,0:T(8,128)(2,1)S(1)} %collective-permute-done.26.refs_3_, ...), custom_call_target="tpu_custom_call" | custom-call | flops 2348810240 | bytes 2752512 | tf_op jit(solution)/shard_map/pallas_call | solution.py:465
  111.0 1.6 %collective-permute-done.24 = bf16[96,2048]{1,0:T(8,128)(2,1)S(1)} collective-permute-done((bf16[96,2048]{1,0:T(8,128)(2,1)S(1)}, bf16[96,2048]{1,0:T(8,128)(2,1)S(1)}, u32[]{:S(2)}, u32[]{:S(2)}) %collective-permute-start.24) | collective-permute-done | bytes 393248 | tf_op jit(solution)/shard_map/ppermute | solution.py:240
  112.8 11.1 %collective-permute-done.22 = bf16[128,2048]{1,0:T(8,128)(2,1)S(1)} collective-permute-done((bf16[128,2048]{1,0:T(8,128)(2,1)S(1)}, bf16[128,2048]{1,0:T(8,128)(2,1)S(1)}, u32[]{:S(2)}, u32[]{:S(2)}) %collective-permute-start.22) | collective-permute-done | bytes 524320 | tf_op jit(solution)/shard_map/ppermute | solution.py:240
  124.1 4.6 %collective-permute-done.20 = bf16[64,2048]{1,0:T(8,128)(2,1)S(1)} collective-permute-done((bf16[64,2048]{1,0:T(8,128)(2,1)S(1)}, bf16[64,2048]{1,0:T(8,128)(2,1)S(1)}, u32[]{:S(2)}, u32[]{:S(2)}) %collective-permute-start.20) | collective-permute-done | bytes 262176 | tf_op jit(solution)/shard_map/ppermute | solution.py:240
  128.9 1.3 shard_map.58.refs_4_
  130.2 1.3 shard_map.59.refs_2_
  (71 shorter events, 20.1 us)
Async XLA Ops:
  0.0 74.9 %collective-permute-start.19 = (bf16[1,1024,2048]{2,1,0:T(8,128)(2,1)}, bf16[1,1024,2048]{2,1,0:T(8,128)(2,1)S(1)}, u32[]{:S(2)}, u32[]{:S(2)}) collective-permute-start(bf16[1,1024,2048]{2,1,0:T(8,128)(2,1)} %refs_13_.1), channel_id=1, source_target_pairs={{0,8},{8,0},{16,24},{24,16},{1,9},{9,1},{17,25},{25,17},{2,10},{10... | collective-permute-start | bytes 12582920 | tf_op jit(solution)/shard_map/ppermute | solution.py:240
  12.9 5.3 %collective-permute-start.1 = (bf16[1,64,512]{2,1,0:T(8,128)(2,1)S(1)}, bf16[1,64,512]{2,1,0:T(8,128)(2,1)S(1)}, u32[]{:S(2)}, u32[]{:S(2)}) collective-permute-start(bf16[1,64,512]{2,1,0:T(8,128)(2,1)S(1)} %get-tuple-element.21), channel_id=1, source_target_pairs={{0,1},{1,0},{2,3},{3,2},{4,5},{5,4},{6,7},{7,6},{8,9},{9,8},{10,11... | collective-permute-start | bytes 196616 | tf_op jit(solution)/shard_map/ppermute | solution.py:240
  15.5 10.0 %collective-permute-start.30 = (s32[1]{0:T(128)}, s32[1]{0:T(128)}, u32[]{:S(2)}, u32[]{:S(2)}) collective-permute-start(s32[1]{0:T(128)} %param.9), channel_id=1, source_target_pairs={{0,16},{8,24},{16,0},{24,8},{1,17},{9,25},{17,1},{25,9},{2,18},{10... | collective-permute-start | bytes 20 | tf_op jit(solution)/shard_map/ppermute | solution.py:240
  17.0 6.8 %collective-permute-start = (bf16[3,64,512]{2,1,0:T(8,128)(2,1)S(1)}, bf16[3,64,512]{2,1,0:T(8,128)(2,1)S(1)}, u32[]{:S(2)}, u32[]{:S(2)}) collective-permute-start(bf16[3,64,512]{2,1,0:T(8,128)(2,1)S(1)} %get-tuple-element.19), channel_id=1, source_target_pairs={{0,1},{1,0},{2,3},{3,2},{4,5},{5,4},{6,7},{7,6},{8,9},{9,8},{10,11... | collective-permute-start | bytes 589832 | tf_op jit(solution)/shard_map/ppermute | solution.py:240
  17.5 55.0 %collective-permute-start.18 = (bf16[2048,512]{1,0:T(8,128)(2,1)S(1)}, bf16[2048,512]{1,0:T(8,128)(2,1)S(1)}, u32[]{:S(2)}, u32[]{:S(2)}) collective-permute-start(bf16[2048,512]{1,0:T(8,128)(2,1)S(1)} %get-tuple-element.22.refs_12_.refs_4_.refs_9_), channel_id=1, source_target_pairs={{0,8},{8,0},{16,24},{24,16},{1,9},{9,1},{17,25},{25,17},{2,10},{10... | collective-permute-start | bytes 6291464 | tf_op jit(solution)/shard_map/ppermute | solution.py:240
  18.3 11.0 %collective-permute-start.2 = (bf16[64,512]{1,0:T(8,128)(2,1)S(1)}, bf16[64,512]{1,0:T(8,128)(2,1)S(1)}, u32[]{:S(2)}, u32[]{:S(2)}) collective-permute-start(bf16[64,512]{1,0:T(8,128)(2,1)S(1)} %fusion.3), channel_id=1, source_target_pairs={{0,4},{2,6},{4,0},{6,2},{1,5},{3,7},{5,1},{7,3},{8,12},{10,14},{12... | collective-permute-start | bytes 196616 | tf_op jit(solution)/shard_map/ppermute | solution.py:240
  23.8 5.5 %collective-permute-start.3 = (bf16[64,512]{1,0:T(8,128)(2,1)S(1)}, bf16[64,512]{1,0:T(8,128)(2,1)S(1)}, u32[]{:S(2)}, u32[]{:S(2)}) collective-permute-start(bf16[64,512]{1,0:T(8,128)(2,1)S(1)} %get-tuple-element.31), channel_id=1, source_target_pairs={{0,2},{2,0},{4,6},{6,4},{1,3},{3,1},{5,7},{7,5},{8,10},{10,8},{12,... | collective-permute-start | bytes 196616 | tf_op jit(solution)/shard_map/ppermute | solution.py:240
  25.5 6.1 %collective-permute-start.4 = (bf16[64,512]{1,0:T(8,128)(2,1)S(1)}, bf16[64,512]{1,0:T(8,128)(2,1)S(1)}, u32[]{:S(2)}, u32[]{:S(2)}) collective-permute-start(bf16[64,512]{1,0:T(8,128)(2,1)S(1)} %get-tuple-element.32), channel_id=1, source_target_pairs={{0,6},{2,4},{4,2},{6,0},{1,7},{3,5},{5,3},{7,1},{8,14},{10,12},{12... | collective-permute-start | bytes 196616 | tf_op jit(solution)/shard_map/ppermute | solution.py:240
  29.3 75.0 %collective-permute-start.32 = (bf16[2048,512]{1,0:T(8,128)(2,1)S(1)}, bf16[2048,512]{1,0:T(8,128)(2,1)S(1)}, u32[]{:S(2)}, u32[]{:S(2)}) collective-permute-start(bf16[2048,512]{1,0:T(8,128)(2,1)S(1)} %col_table.1.refs_11_), channel_id=1, source_target_pairs={{0,8},{8,0},{16,24},{24,16},{1,9},{9,1},{17,25},{25,17},{2,10},{10... | collective-permute-start | bytes 6291464 | tf_op jit(solution)/shard_map/ppermute | solution.py:240
  31.6 5.7 %collective-permute-start.5 = (bf16[64,512]{1,0:T(8,128)(2,1)S(1)}, bf16[64,512]{1,0:T(8,128)(2,1)S(1)}, u32[]{:S(2)}, u32[]{:S(2)}) collective-permute-start(bf16[64,512]{1,0:T(8,128)(2,1)S(1)} %fusion.2), channel_id=1, source_target_pairs={{0,2},{2,0},{4,6},{6,4},{1,3},{3,1},{5,7},{7,5},{8,10},{10,8},{12,... | collective-permute-start | bytes 196616 | tf_op jit(solution)/shard_map/ppermute | solution.py:240
  31.7 1.8 %collective-permute-start.17 = (s32[1]{0:T(128)}, s32[1]{0:T(128)}, u32[]{:S(2)}, u32[]{:S(2)}) collective-permute-start(s32[1]{0:T(128)} %param.9), channel_id=1, source_target_pairs={{0,8},{8,0},{16,24},{24,16},{1,9},{9,1},{17,25},{25,17},{2,10},{10... | collective-permute-start | bytes 20 | tf_op jit(solution)/shard_map/ppermute | solution.py:240
  34.8 8.6 %collective-permute-start.6 = (bf16[64,512]{1,0:T(8,128)(2,1)S(1)}, bf16[64,512]{1,0:T(8,128)(2,1)S(1)}, u32[]{:S(2)}, u32[]{:S(2)}) collective-permute-start(bf16[64,512]{1,0:T(8,128)(2,1)S(1)} %fusion.2), channel_id=1, source_target_pairs={{0,4},{2,6},{4,0},{6,2},{1,5},{3,7},{5,1},{7,3},{8,12},{10,14},{12... | collective-permute-start | bytes 196616 | tf_op jit(solution)/shard_map/ppermute | solution.py:240
  37.3 6.7 %collective-permute-start.7 = (bf16[64,512]{1,0:T(8,128)(2,1)S(1)}, bf16[64,512]{1,0:T(8,128)(2,1)S(1)}, u32[]{:S(2)}, u32[]{:S(2)}) collective-permute-start(bf16[64,512]{1,0:T(8,128)(2,1)S(1)} %fusion.2), channel_id=1, source_target_pairs={{0,6},{2,4},{4,2},{6,0},{1,7},{3,5},{5,3},{7,1},{8,14},{10,12},{12... | collective-permute-start | bytes 196616 | tf_op jit(solution)/shard_map/ppermute | solution.py:240
  43.5 4.3 %collective-permute-start.8 = (bf16[64,512]{1,0:T(8,128)(2,1)S(1)}, bf16[64,512]{1,0:T(8,128)(2,1)S(1)}, u32[]{:S(2)}, u32[]{:S(2)}) collective-permute-start(bf16[64,512]{1,0:T(8,128)(2,1)S(1)} %fusion.2), channel_id=1, source_target_pairs={{0,1},{1,0},{2,3},{3,2},{4,5},{5,4},{6,7},{7,6},{8,9},{9,8},{10,11... | collective-permute-start | bytes 196616 | tf_op jit(solution)/shard_map/ppermute | solution.py:240
  44.0 5.0 %collective-permute-start.9 = (bf16[64,512]{1,0:T(8,128)(2,1)S(1)}, bf16[64,512]{1,0:T(8,128)(2,1)S(1)}, u32[]{:S(2)}, u32[]{:S(2)}) collective-permute-start(bf16[64,512]{1,0:T(8,128)(2,1)S(1)} %collective-permute-done.5), channel_id=1, source_target_pairs={{0,1},{1,0},{2,3},{3,2},{4,5},{5,4},{6,7},{7,6},{8,9},{9,8},{10,11... | collective-permute-start | bytes 196616 | tf_op jit(solution)/shard_map/ppermute | solution.py:240
  47.7 4.3 %collective-permute-start.10 = (bf16[64,512]{1,0:T(8,128)(2,1)S(1)}, bf16[64,512]{1,0:T(8,128)(2,1)S(1)}, u32[]{:S(2)}, u32[]{:S(2)}) collective-permute-start(bf16[64,512]{1,0:T(8,128)(2,1)S(1)} %collective-permute-done.6), channel_id=1, source_target_pairs={{0,1},{1,0},{2,3},{3,2},{4,5},{5,4},{6,7},{7,6},{8,9},{9,8},{10,11... | collective-permute-start | bytes 196616 | tf_op jit(solution)/shard_map/ppermute | solution.py:240
  48.9 4.3 %collective-permute-start.11 = (bf16[64,512]{1,0:T(8,128)(2,1)S(1)}, bf16[64,512]{1,0:T(8,128)(2,1)S(1)}, u32[]{:S(2)}, u32[]{:S(2)}) collective-permute-start(bf16[64,512]{1,0:T(8,128)(2,1)S(1)} %collective-permute-done.7), channel_id=1, source_target_pairs={{0,1},{1,0},{2,3},{3,2},{4,5},{5,4},{6,7},{7,6},{8,9},{9,8},{10,11... | collective-permute-start | bytes 196616 | tf_op jit(solution)/shard_map/ppermute | solution.py:240
  54.7 2.0 %collective-permute-start.12 = (bf16[256,512]{1,0:T(8,128)(2,1)S(1)}, bf16[256,512]{1,0:T(8,128)(2,1)S(1)}, u32[]{:S(2)}, u32[]{:S(2)}) collective-permute-start(bf16[256,512]{1,0:T(8,128)(2,1)S(1)} %pad_maximum_fusion.refs_1_), channel_id=1, source_target_pairs={{0,8},{8,0},{16,24},{24,16},{1,9},{9,1},{17,25},{25,17},{2,10},{10... | collective-permute-start | bytes 786440 | tf_op jit(solution)/shard_map/ppermute | solution.py:240
  55.7 9.2 %collective-permute-start.26 = (bf16[256,512]{1,0:T(8,128)(2,1)S(1)}, bf16[256,512]{1,0:T(8,128)(2,1)S(1)}, u32[]{:S(2)}, u32[]{:S(2)}) collective-permute-start(bf16[256,512]{1,0:T(8,128)(2,1)S(1)} %pad_maximum_fusion.refs_1_), channel_id=1, source_target_pairs={{0,16},{8,24},{16,0},{24,8},{1,17},{9,25},{17,1},{25,9},{2,18},{10... | collective-permute-start | bytes 786440 | tf_op jit(solution)/shard_map/ppermute | solution.py:240
  56.7 28.7 %collective-permute-start.34 = (bf16[224,2048]{1,0:T(8,128)(2,1)S(1)}, bf16[224,2048]{1,0:T(8,128)(2,1)S(1)}, u32[]{:S(2)}, u32[]{:S(2)}) collective-permute-start(bf16[224,2048]{1,0:T(8,128)(2,1)S(1)} %get-tuple-element.28), channel_id=1, source_target_pairs={{0,24},{8,16},{16,8},{24,0},{1,25},{9,17},{17,9},{25,1},{2,26},{10... | collective-permute-start | bytes 2752520 | tf_op jit(solution)/shard_map/ppermute | solution.py:240
  64.9 6.7 %collective-permute-start.27 = (bf16[256,512]{1,0:T(8,128)(2,1)S(1)}, bf16[256,512]{1,0:T(8,128)(2,1)S(1)}, u32[]{:S(2)}, u32[]{:S(2)}) collective-permute-start(bf16[256,512]{1,0:T(8,128)(2,1)S(1)} %collective-permute-done.26.refs_3_), channel_id=1, source_target_pairs={{0,1},{1,0},{2,3},{3,2},{4,5},{5,4},{6,7},{7,6},{8,9},{9,8},{10,11... | collective-permute-start | bytes 786440 | tf_op jit(solution)/shard_map/ppermute | solution.py:240
  71.6 32.6 %collective-permute-start.33 = (bf16[224,2048]{1,0:T(8,128)(2,1)S(1)}, bf16[224,2048]{1,0:T(8,128)(2,1)S(1)}, u32[]{:S(2)}, u32[]{:S(2)}) collective-permute-start(bf16[224,2048]{1,0:T(8,128)(2,1)S(1)} %own_slice.1), channel_id=1, source_target_pairs={{0,16},{8,24},{16,0},{24,8},{1,17},{9,25},{17,1},{25,9},{2,18},{10... | collective-permute-start | bytes 2752520 | tf_op jit(solution)/shard_map/ppermute | solution.py:240
  72.6 8.7 %collective-permute-start.28 = (bf16[256,512]{1,0:T(8,128)(2,1)S(1)}, bf16[256,512]{1,0:T(8,128)(2,1)S(1)}, u32[]{:S(2)}, u32[]{:S(2)}) collective-permute-start(bf16[256,512]{1,0:T(8,128)(2,1)S(1)} %collective-permute-done.26.refs_3_), channel_id=1, source_target_pairs={{0,8},{8,0},{16,24},{24,16},{1,9},{9,1},{17,25},{25,17},{2,10},{10... | collective-permute-start | bytes 786440 | tf_op jit(solution)/shard_map/ppermute | solution.py:240
  74.9 29.4 %collective-permute-start.29 = (bf16[256,512]{1,0:T(8,128)(2,1)S(1)}, bf16[256,512]{1,0:T(8,128)(2,1)S(1)}, u32[]{:S(2)}, u32[]{:S(2)}) collective-permute-start(bf16[256,512]{1,0:T(8,128)(2,1)S(1)} %collective-permute-done.27.refs_4_), channel_id=1, source_target_pairs={{0,8},{8,0},{16,24},{24,16},{1,9},{9,1},{17,25},{25,17},{2,10},{10... | collective-permute-start | bytes 786440 | tf_op jit(solution)/shard_map/ppermute | solution.py:240
  81.3 31.4 %collective-permute-start.24 = (bf16[96,2048]{1,0:T(8,128)(2,1)S(1)}, bf16[96,2048]{1,0:T(8,128)(2,1)S(1)}, u32[]{:S(2)}, u32[]{:S(2)}) collective-permute-start(bf16[96,2048]{1,0:T(8,128)(2,1)S(1)} %get-tuple-element.27), channel_id=1, source_target_pairs={{0,16},{8,24},{16,0},{24,8},{1,17},{9,25},{17,1},{25,9},{2,18},{10... | collective-permute-start | bytes 1179656 | tf_op jit(solution)/shard_map/ppermute | solution.py:240
  85.4 38.5 %collective-permute-start.22 = (bf16[128,2048]{1,0:T(8,128)(2,1)S(1)}, bf16[128,2048]{1,0:T(8,128)(2,1)S(1)}, u32[]{:S(2)}, u32[]{:S(2)}) collective-permute-start(bf16[128,2048]{1,0:T(8,128)(2,1)S(1)} %get-tuple-element.26), channel_id=1, source_target_pairs={{0,16},{8,24},{16,0},{24,8},{1,17},{9,25},{17,1},{25,9},{2,18},{10... | collective-permute-start | bytes 1572872 | tf_op jit(solution)/shard_map/ppermute | solution.py:240
  109.5 19.3 %collective-permute-start.35 = (bf16[128,2048]{1,0:T(8,128)(2,1)S(1)}, bf16[128,2048]{1,0:T(8,128)(2,1)S(1)}, u32[]{:S(2)}, u32[]{:S(2)}) collective-permute-start(bf16[128,2048]{1,0:T(8,128)(2,1)S(1)} %get-tuple-element.29.refs_0_), channel_id=1, source_target_pairs={{0,8},{8,0},{16,24},{24,16},{1,9},{9,1},{17,25},{25,17},{2,10},{10... | collective-permute-start | bytes 1572872 | tf_op jit(solution)/shard_map/ppermute | solution.py:240
  109.6 19.3 %collective-permute-start.36 = (bf16[96,2048]{1,0:T(8,128)(2,1)S(1)}, bf16[96,2048]{1,0:T(8,128)(2,1)S(1)}, u32[]{:S(2)}, u32[]{:S(2)}) collective-permute-start(bf16[96,2048]{1,0:T(8,128)(2,1)S(1)} %get-tuple-element.30.refs_2_), channel_id=1, source_target_pairs={{0,8},{8,0},{16,24},{24,16},{1,9},{9,1},{17,25},{25,17},{2,10},{10... | collective-permute-start | bytes 1179656 | tf_op jit(solution)/shard_map/ppermute | solution.py:240
  110.1 18.6 %collective-permute-start.20 = (bf16[64,2048]{1,0:T(8,128)(2,1)S(1)}, bf16[64,2048]{1,0:T(8,128)(2,1)S(1)}, u32[]{:S(2)}, u32[]{:S(2)}) collective-permute-start(bf16[64,2048]{1,0:T(8,128)(2,1)S(1)} %get-tuple-element.25), channel_id=1, source_target_pairs={{0,16},{8,24},{16,0},{24,8},{1,17},{9,25},{17,1},{25,9},{2,18},{10... | collective-permute-start | bytes 786440 | tf_op jit(solution)/shard_map/ppermute | solution.py:240
  112.8 17.4 %collective-permute-start.25 = (bf16[96,2048]{1,0:T(8,128)(2,1)S(1)}, bf16[96,2048]{1,0:T(8,128)(2,1)S(1)}, u32[]{:S(2)}, u32[]{:S(2)}) collective-permute-start(bf16[96,2048]{1,0:T(8,128)(2,1)S(1)} %add_convert_fusion.1.refs_2_), channel_id=1, source_target_pairs={{0,8},{8,0},{16,24},{24,16},{1,9},{9,1},{17,25},{25,17},{2,10},{10... | collective-permute-start | bytes 1179656 | tf_op jit(solution)/shard_map/ppermute | solution.py:240
  124.0 6.1 %collective-permute-start.23 = (bf16[128,2048]{1,0:T(8,128)(2,1)S(1)}, bf16[128,2048]{1,0:T(8,128)(2,1)S(1)}, u32[]{:S(2)}, u32[]{:S(2)}) collective-permute-start(bf16[128,2048]{1,0:T(8,128)(2,1)S(1)} %add_convert_fusion.refs_0_), channel_id=1, source_target_pairs={{0,8},{8,0},{16,24},{24,16},{1,9},{9,1},{17,25},{25,17},{2,10},{10... | collective-permute-start | bytes 1572872 | tf_op jit(solution)/shard_map/ppermute | solution.py:240
  128.8 2.7 %collective-permute-start.21 = (bf16[64,2048]{1,0:T(8,128)(2,1)S(1)}, bf16[64,2048]{1,0:T(8,128)(2,1)S(1)}, u32[]{:S(2)}, u32[]{:S(2)}) collective-permute-start(bf16[64,2048]{1,0:T(8,128)(2,1)S(1)} %add_convert_fusion.2.refs_0_), channel_id=1, source_target_pairs={{0,8},{8,0},{16,24},{24,16},{1,9},{9,1},{17,25},{25,17},{2,10},{10... | collective-permute-start | bytes 786440 | tf_op jit(solution)/shard_map/ppermute | solution.py:240
  (9 other events, 48.1 us)

commit v7 on v6

--- a/solution.py
+++ b/solution.py
@@ -115,8 +115,8 @@
 
 
 def forward_kernel(index_ref, charge_ref, tiles_ref, cot_ref, inc_ref, *refs, rows, cols, n_row, groups, begin):
-    outs, (col_tab, slice_ref) = refs[:-7], refs[-7:-5]
-    row_tab, inner, fine_ref, t_ref, sem = refs[-5:]
+    outs, (col_tab, slice_ref) = refs[:-8], refs[-8:-6]
+    row_tab, inner, fine_ref, t_ref, phase_ref, sem = refs[-6:]
     block = min(256, rows)
     extent = rows * n_row
     row_at = lax.axis_index("row")
@@ -138,6 +138,22 @@
         row_tab[HALF + part : HALF + part + 64, at : at + 128] = im
 
     table_pupil_lanes(write_row, period, row_at * rows, extent, rows, fine_ref, 0.0, HALF)
+
+    charge = charge_ref[0]
+    scale = 4.0 / (extent * M)
+    shape = (64, HALF)
+    for ub in range(HALF // 64):
+        u = 2.0 * (iota(shape, 0) + float(ub * 64)) + 1.0
+        v = 2.0 * iota(shape, 1) + 1.0
+        inv = 1.0 / jnp.sqrt(u * u + v * v)
+        power = (u * inv, v * inv)
+        total = (jnp.full(shape, scale, F32), jnp.zeros(shape, F32))
+        for bit in range(4):
+            taken = (charge >> bit) % 2 == 1
+            multiplied = turn(total, power)
+            total = tuple(jnp.where(taken, new, old) for new, old in zip(multiplied, total))
+            power = turn(power, power)
+        phase_ref[0, ub * 64 : (ub + 1) * 64, :], phase_ref[1, ub * 64 : (ub + 1) * 64, :] = total
 
     for step in range(rows // block):
         halves = []
@@ -163,17 +179,7 @@
         )
         q = jnp.dot(both, inner[...], preferred_element_type=F32)
         q_c, q_s = q[:chunk], q[chunk:]
-        u = 2.0 * (iota(shape, 0) + float(ub * chunk)) + 1.0
-        v = 2.0 * iota(shape, 1) + 1.0
-        inv = 1.0 / jnp.sqrt(u * u + v * v)
-        power = (u * inv, v * inv)
-        total = (jnp.full(shape, scale, F32), jnp.zeros(shape, F32))
-        for bit in range(4):
-            taken = (charge >> bit) % 2 == 1
-            multiplied = turn(total, power)
-            total = tuple(jnp.where(taken, new, old) for new, old in zip(multiplied, total))
-            power = turn(power, power)
-        c, s = total
+        c, s = phase_ref[0, ub * chunk : (ub + 1) * chunk, :], phase_ref[1, ub * chunk : (ub + 1) * chunk, :]
         ce, se, co, so = c * even, s * even, c * odd, s * odd
         ca, cb, cc, cd = (q_c[:, k * HALF : (k + 1) * HALF] for k in range(4))
         sa, sb, sc, sd = (q_s[:, k * HALF : (k + 1) * HALF] for k in range(4))
@@ -224,6 +230,7 @@
             pltpu.VMEM((rows, 2 * M), BF16),
             pltpu.VMEM((2, HALF, HALF), F32),
             pltpu.VMEM((n_row * n_col, per, M), F32),
+            pltpu.VMEM((2, HALF, HALF), F32),
             pltpu.SemaphoreType.DMA,
         ],
         compiler_params=pltpu.CompilerParams(vmem_limit_bytes=36 << 20),
@@ -483,23 +490,21 @@
 
 
 def place_kernel(*refs, chunks, rows):
-    sources = refs[: 2 * len(chunks)]
+    sources = refs[: len(chunks)]
     out, sems = refs[-2:]
     half_at = lax.rem(lax.axis_index("wl"), 2)
     copies = []
-    for k, (at, amount) in enumerate(chunks):
-        for side in range(2):
-            where = half_at if side == 0 else 1 - half_at
-            target = out.at[pl.ds(pl.multiple_of(where * rows + at, 16), amount), :]
-            copies.append(pltpu.make_async_copy(sources[2 * k + side], target, sems.at[k, side]))
+    for k, (at, amount, side) in enumerate(chunks):
+        where = half_at if side == 0 else 1 - half_at
+        target = out.at[pl.ds(pl.multiple_of(where * rows + at, 16), amount), :]
+        copies.append(pltpu.make_async_copy(sources[k], target, sems.at[k]))
     for copy in copies:
         copy.start()
     for copy in copies:
         copy.wait()
 
 
-def place(done, chunks, rows, into=None):
-    flat = [part for pair in done for part in pair]
+def place(flat, chunks, rows, into=None):
     cols = flat[0].shape[1]
     operands = flat + ([into] if into is not None else [])
 
@@ -512,10 +517,12 @@
         in_specs=[hbm] * len(operands),
         out_specs=hbm,
         out_shape=jax.ShapeDtypeStruct((2 * rows, cols), BF16),
-        scratch_shapes=[pltpu.SemaphoreType.DMA((len(chunks), 2))],
+        scratch_shapes=[pltpu.SemaphoreType.DMA((len(chunks),))],
         input_output_aliases={len(flat): 0} if into is not None else {},
         compiler_params=pltpu.CompilerParams(vmem_limit_bytes=1 << 20),
-        cost_estimate=pl.CostEstimate(flops=0, bytes_accessed=4 * cols * sum(n for _, n in chunks), transcendentals=0),
+        cost_estimate=pl.CostEstimate(
+            flops=0, bytes_accessed=4 * cols * sum(n for _, n, _ in chunks), transcendentals=0
+        ),
     )(*operands)
 
 
@@ -600,9 +607,16 @@
         total = add_up([pair, swap(pair, "wl", 2)]).astype(BF16)
         done.append((total, swap(total, "wl", 1)))
     ready = [(part, swap(part, "wl", 1)) for part in both]
-    result = place(ready, chunks[n_first:], half)
-    result = place(done[:-1], chunks[: n_first - 1], half, result)
-    return place(done[-1:], chunks[n_first - 1 : n_first], half, result)
+
+    def sides(pairs, some):
+        flat = [part for pair in pairs for part in pair]
+        return flat, [(at, amount, side) for at, amount in some for side in range(2)]
+
+    flat, where = sides(ready, chunks[n_first:])
+    result = place(flat, where, half)
+    flat, where = sides(done, chunks[:n_first])
+    result = place(flat[:-1], where[:-1], half, result)
+    return place(flat[-1:], where[-1:], half, result)
 
 
 def solution(mesh):

time: 133 us -> 133 us (level)
  no operation moved by 1% of the time
where the time goes in v7:
time: 133 us; the launch traced here: 132 us
  waiting for transfers between devices  68.4 us (51%)
  starting transfers between devices  28.6 us (22%)
  Pallas kernels  27.2 us (20%)
  local copies, waits for them, and re-layouts  4.08 us (3%)
  other arithmetic  2.4 us (2%)
  between operations  1.76 us (1%)
    ppermute x37, waiting for transfers between devices, swap(): return lax.ppermute(value, axis, [(i, i ^ bits) for i in range(size)])  68.4 us
    ppermute x37, starting transfers between devices, swap(): return lax.ppermute(value, axis, [(i, i ^ bits) for i in range(size)])  28.6 us
    pallas_call x3, Pallas kernels, backward(): pl.pallas_call(kernel, in_specs=[pl.BlockSpec(memory_space=pltpu.SMEM)] +...  11.1 us
    pallas_call x1, Pallas kernels, forward(): pl.pallas_call(kernel, in_specs=[smem, smem, smem, pl.BlockSpec(memory_sp...  7.09 us
    unnamed x8, local copies, waits for them, and re-layouts  4.07 us
    pallas_call x3, Pallas kernels, place(): pl.pallas_call(kernel, in_specs=[hbm] * len(operands), out_specs=hbm, out...  3.37 us
    pallas_call x2, Pallas kernels, row_tables(): pl.pallas_call(kernel, in_specs=[pl.BlockSpec(memory_space=pltpu.SMEM)],...  3.2 us
  transfers between devices with their start and end apart: 37, of which 19 were waited for; matrix products, arithmetic and copies ran while one was open for 2% of the time, Pallas kernels for 20%

profile of v7, /device:TPU:0, one launch (start us, length us, event | category | flops | bytes accessed | tf_op | source)
XLA Modules:
  0.0 132.5 jit_solution(9159480316538170129)
XLA Ops:
  2.5 3.4 %copy-done.3 = bf16[1,2,1024,2048]{3,2,1,0:T(8,128)(2,1)S(1)} copy-done((bf16[1,2,1024,2048]{3,2,1,0:T(8,128)(2,1)S(1)}, bf16[1,2,1024,2048]{3,2,1,0:T(8,128)(2,1)}, u32[]{:S(2)}) %copy-start.3) | copy-done | bytes 8388632
  5.9 7.1 %forward.1 = (bf16[1,64,512]{2,1,0:T(8,128)(2,1)S(1)}, bf16[1,64,512]{2,1,0:T(8,128)(2,1)S(1)}, bf16[3,64,512]{2,1,0:T(8,128)(2,1)S(1)}, bf16[3,64,512]{2,1,0:T(...) custom-call(s32[1]{0:T(128)S(6)} %copy.11.refs_0_, s32[1]{0:T(128)S(6)} %copy.10.refs_1_, ...), custom_call_target="tpu_custom_call" | custom-call | flops 5368709120 | bytes 8388608 | tf_op jit(solution)/shard_map/forward/pallas_call | solution.py:223
  13.0 2.6 %collective-permute-start.1 = (bf16[1,64,512]{2,1,0:T(8,128)(2,1)S(1)}, bf16[1,64,512]{2,1,0:T(8,128)(2,1)S(1)}, u32[]{:S(2)}, u32[]{:S(2)}) collective-permute-start(bf16[1,64,512]{2,1,0:T(8,128)(2,1)S(1)} %get-tuple-element.21), channel_id=1, source_target_pairs={{0,1},{1,0},{2,3},{3,2},{4,5},{5,4},{6,7},{7,6},{8,9},{9,8},{10,11... | collective-permute-start | bytes 196616 | tf_op jit(solution)/shard_map/ppermute | solution.py:247
  15.5 1.5 %collective-permute-start.30 = (s32[1]{0:T(128)}, s32[1]{0:T(128)}, u32[]{:S(2)}, u32[]{:S(2)}) collective-permute-start(s32[1]{0:T(128)} %param.9), channel_id=1, source_target_pairs={{0,16},{8,24},{16,0},{24,8},{1,17},{9,25},{17,1},{25,9},{2,18},{10... | collective-permute-start | bytes 20 | tf_op jit(solution)/shard_map/ppermute | solution.py:247
  18.3 2.9 %collective-permute-start.2 = (bf16[64,512]{1,0:T(8,128)(2,1)S(1)}, bf16[64,512]{1,0:T(8,128)(2,1)S(1)}, u32[]{:S(2)}, u32[]{:S(2)}) collective-permute-start(bf16[64,512]{1,0:T(8,128)(2,1)S(1)} %fusion.3), channel_id=1, source_target_pairs={{0,4},{2,6},{4,0},{6,2},{1,5},{3,7},{5,1},{7,3},{8,12},{10,14},{12... | collective-permute-start | bytes 196616 | tf_op jit(solution)/shard_map/ppermute | solution.py:247
  21.2 2.6 %collective-permute-done = bf16[3,64,512]{2,1,0:T(8,128)(2,1)S(1)} collective-permute-done((bf16[3,64,512]{2,1,0:T(8,128)(2,1)S(1)}, bf16[3,64,512]{2,1,0:T(8,128)(2,1)S(1)}, u32[]{:S(2)}, u32[]{:S(2)}) %collective-permute-start) | collective-permute-done | bytes 196640 | tf_op jit(solution)/shard_map/ppermute | solution.py:247
  23.8 1.6 %collective-permute-start.3 = (bf16[64,512]{1,0:T(8,128)(2,1)S(1)}, bf16[64,512]{1,0:T(8,128)(2,1)S(1)}, u32[]{:S(2)}, u32[]{:S(2)}) collective-permute-start(bf16[64,512]{1,0:T(8,128)(2,1)S(1)} %get-tuple-element.31), channel_id=1, source_target_pairs={{0,2},{2,0},{4,6},{6,4},{1,3},{3,1},{5,7},{7,5},{8,10},{10,8},{12,... | collective-permute-start | bytes 196616 | tf_op jit(solution)/shard_map/ppermute | solution.py:247
  25.5 2.5 %collective-permute-start.4 = (bf16[64,512]{1,0:T(8,128)(2,1)S(1)}, bf16[64,512]{1,0:T(8,128)(2,1)S(1)}, u32[]{:S(2)}, u32[]{:S(2)}) collective-permute-start(bf16[64,512]{1,0:T(8,128)(2,1)S(1)} %get-tuple-element.32), channel_id=1, source_target_pairs={{0,6},{2,4},{4,2},{6,0},{1,7},{3,5},{5,3},{7,1},{8,14},{10,12},{12... | collective-permute-start | bytes 196616 | tf_op jit(solution)/shard_map/ppermute | solution.py:247
  28.0 1.3 col_table.1.refs_11_
  29.4 2.2 %collective-permute-done.4 = bf16[64,512]{1,0:T(8,128)(2,1)S(1)} collective-permute-done((bf16[64,512]{1,0:T(8,128)(2,1)S(1)}, bf16[64,512]{1,0:T(8,128)(2,1)S(1)}, u32[]{:S(2)}, u32[]{:S(2)}) %collective-permute-start.4) | collective-permute-done | bytes 65568 | tf_op jit(solution)/shard_map/ppermute | solution.py:247
  31.8 1.7 %collective-permute-done.17 = s32[1]{0:T(128)} collective-permute-done((s32[1]{0:T(128)}, s32[1]{0:T(128)}, u32[]{:S(2)}, u32[]{:S(2)}) %collective-permute-start.17) | collective-permute-done | bytes 36 | tf_op jit(solution)/shard_map/ppermute | solution.py:247
  33.6 1.2 collective-permute-done.31
  34.9 2.5 %collective-permute-start.6 = (bf16[64,512]{1,0:T(8,128)(2,1)S(1)}, bf16[64,512]{1,0:T(8,128)(2,1)S(1)}, u32[]{:S(2)}, u32[]{:S(2)}) collective-permute-start(bf16[64,512]{1,0:T(8,128)(2,1)S(1)} %fusion.2), channel_id=1, source_target_pairs={{0,4},{2,6},{4,0},{6,2},{1,5},{3,7},{5,1},{7,3},{8,12},{10,14},{12... | collective-permute-start | bytes 196616 | tf_op jit(solution)/shard_map/ppermute | solution.py:247
  37.3 1.4 %collective-permute-start.7 = (bf16[64,512]{1,0:T(8,128)(2,1)S(1)}, bf16[64,512]{1,0:T(8,128)(2,1)S(1)}, u32[]{:S(2)}, u32[]{:S(2)}) collective-permute-start(bf16[64,512]{1,0:T(8,128)(2,1)S(1)} %fusion.2), channel_id=1, source_target_pairs={{0,6},{2,4},{4,2},{6,0},{1,7},{3,5},{5,3},{7,1},{8,14},{10,12},{12... | collective-permute-start | bytes 196616 | tf_op jit(solution)/shard_map/ppermute | solution.py:247
  38.7 4.8 %collective-permute-done.6 = bf16[64,512]{1,0:T(8,128)(2,1)S(1)} collective-permute-done((bf16[64,512]{1,0:T(8,128)(2,1)S(1)}, bf16[64,512]{1,0:T(8,128)(2,1)S(1)}, u32[]{:S(2)}, u32[]{:S(2)}) %collective-permute-start.6) | collective-permute-done | bytes 65568 | tf_op jit(solution)/shard_map/ppermute | solution.py:247
  44.0 1.5 %collective-permute-start.9 = (bf16[64,512]{1,0:T(8,128)(2,1)S(1)}, bf16[64,512]{1,0:T(8,128)(2,1)S(1)}, u32[]{:S(2)}, u32[]{:S(2)}) collective-permute-start(bf16[64,512]{1,0:T(8,128)(2,1)S(1)} %collective-permute-done.5), channel_id=1, source_target_pairs={{0,1},{1,0},{2,3},{3,2},{4,5},{5,4},{6,7},{7,6},{8,9},{9,8},{10,11... | collective-permute-start | bytes 196616 | tf_op jit(solution)/shard_map/ppermute | solution.py:247
  45.5 2.2 %collective-permute-done.8.refs_2_ = bf16[64,512]{1,0:T(8,128)(2,1)S(1)} collective-permute-done((bf16[64,512]{1,0:T(8,128)(2,1)S(1)}, bf16[64,512]{1,0:T(8,128)(2,1)S(1)}, u32[]{:S(2)}, u32[]{:S(2)}) %collective-permute-start.8) | collective-permute-done | bytes 65568 | tf_op jit(solution)/shard_map/ppermute | solution.py:247
  49.9 2.2 %collective-permute-done.10.refs_4_ = bf16[64,512]{1,0:T(8,128)(2,1)S(1)} collective-permute-done((bf16[64,512]{1,0:T(8,128)(2,1)S(1)}, bf16[64,512]{1,0:T(8,128)(2,1)S(1)}, u32[]{:S(2)}, u32[]{:S(2)}) %collective-permute-start.10) | collective-permute-done | bytes 65568 | tf_op jit(solution)/shard_map/ppermute | solution.py:247
  57.3 7.7 %collective-permute-done.26.refs_3_ = bf16[256,512]{1,0:T(8,128)(2,1)S(1)} collective-permute-done((bf16[256,512]{1,0:T(8,128)(2,1)S(1)}, bf16[256,512]{1,0:T(8,128)(2,1)S(1)}, u32[]{:S(2)}, u32[]{:S(2)}) %collective-permute-start.26) | collective-permute-done | bytes 262176 | tf_op jit(solution)/shard_map/ppermute | solution.py:247
  67.0 4.6 %collective-permute-done.27.refs_4_ = bf16[256,512]{1,0:T(8,128)(2,1)S(1)} collective-permute-done((bf16[256,512]{1,0:T(8,128)(2,1)S(1)}, bf16[256,512]{1,0:T(8,128)(2,1)S(1)}, u32[]{:S(2)}, u32[]{:S(2)}) %collective-permute-start.27) | collective-permute-done | bytes 262176 | tf_op jit(solution)/shard_map/ppermute | solution.py:247
  73.3 1.6 %row_tables.2.refs_11_.refs_3_.refs_7_ = bf16[2,512,512]{2,1,0:T(8,128)(2,1)S(1)} custom-call(s32[2]{0:T(128)S(1)} %pad_add_fusion.refs_0_), custom_call_target="tpu_custom_call" | custom-call | flops 10485760 | bytes 1048576 | tf_op jit(solution)/shard_map/row_tables/pallas_call | solution.py:340
  75.5 2.8 %shard_map.55 = (bf16[128,2048]{1,0:T(8,128)(2,1)S(1)}, bf16[512,512]{1,0:T(8,128)(2,1)S(1)}, bf16[512,512]{1,0:T(8,128)(2,1)S(1)}) custom-call(s32[8,16]{1,0:T(8,128)S(1)} %copy-done.2, bf16[256,512]{1,0:T(8,128)(2,1)S(1)} %pad_maximum_fusion.refs_1_, bf16[64,512]{1,0:T(8,128)(2,1)S(1)} %collective-permute-done.8.refs_2_, ...), custom_call_target="tpu_custom_call" | custom-call | flops 671088640 | bytes 1572864 | tf_op jit(solution)/shard_map/pallas_call | solution.py:472
  78.2 3.1 %shard_map.56 = (bf16[96,2048]{1,0:T(8,128)(2,1)S(1)}, bf16[64,2048]{1,0:T(8,128)(2,1)S(1)}) custom-call(s32[8,16]{1,0:T(8,128)S(1)} %copy-done.2, bf16[512,512]{1,0:T(8,128)(2,1)S(1)} %get-tuple-element.23.refs_1_, bf16[512,512]{1,0:T(8,128)(2,1)S(1)} %get-tuple-element.24.refs_2_, bf16[2,512,512]{2,1,0:T(8,128)(2,1)S(1)} %row_tables.2.refs_11_.refs_3_.refs_7_, ...), custom_call_target="tpu_custom_call" | custom-call | flops 838860800 | bytes 1966080 | tf_op jit(solution)/shard_map/pallas_call | solution.py:472
  82.5 1.3 pad_add_fusion.1.refs_0_
  83.8 1.6 %row_tables.3.refs_8_ = bf16[2,512,512]{2,1,0:T(8,128)(2,1)S(1)} custom-call(s32[2]{0:T(128)S(1)} %pad_add_fusion.1.refs_0_), custom_call_target="tpu_custom_call" | custom-call | flops 10485760 | bytes 1048576 | tf_op jit(solution)/shard_map/row_tables/pallas_call | solution.py:340
  86.4 17.9 %collective-permute-done.33.refs_15_ = bf16[224,2048]{1,0:T(8,128)(2,1)S(1)} collective-permute-done((bf16[224,2048]{1,0:T(8,128)(2,1)S(1)}, bf16[224,2048]{1,0:T(8,128)(2,1)S(1)}, u32[]{:S(2)}, u32[]{:S(2)}) %collective-permute-start.33) | collective-permute-done | bytes 917536 | tf_op jit(solution)/shard_map/ppermute | solution.py:247
  104.3 5.3 %shard_map.57 = (bf16[128,2048]{1,0:T(8,128)(2,1)S(1)}, bf16[96,2048]{1,0:T(8,128)(2,1)S(1)}) custom-call(s32[8,16]{1,0:T(8,128)S(1)} %copy-done.2, bf16[512,512]{1,0:T(8,128)(2,1)S(1)} %get-tuple-element.23.refs_1_, bf16[512,512]{1,0:T(8,128)(2,1)S(1)} %get-tuple-element.24.refs_2_, bf16[256,512]{1,0:T(8,128)(2,1)S(1)} %collective-permute-done.26.refs_3_, ...), custom_call_target="tpu_custom_call" | custom-call | flops 2348810240 | bytes 2752512 | tf_op jit(solution)/shard_map/pallas_call | solution.py:472
  111.1 1.6 %collective-permute-done.24 = bf16[96,2048]{1,0:T(8,128)(2,1)S(1)} collective-permute-done((bf16[96,2048]{1,0:T(8,128)(2,1)S(1)}, bf16[96,2048]{1,0:T(8,128)(2,1)S(1)}, u32[]{:S(2)}, u32[]{:S(2)}) %collective-permute-start.24) | collective-permute-done | bytes 393248 | tf_op jit(solution)/shard_map/ppermute | solution.py:247
  112.9 11.1 %collective-permute-done.22 = bf16[128,2048]{1,0:T(8,128)(2,1)S(1)} collective-permute-done((bf16[128,2048]{1,0:T(8,128)(2,1)S(1)}, bf16[128,2048]{1,0:T(8,128)(2,1)S(1)}, u32[]{:S(2)}, u32[]{:S(2)}) %collective-permute-start.22) | collective-permute-done | bytes 524320 | tf_op jit(solution)/shard_map/ppermute | solution.py:247
  124.1 4.6 %collective-permute-done.20 = bf16[64,2048]{1,0:T(8,128)(2,1)S(1)} collective-permute-done((bf16[64,2048]{1,0:T(8,128)(2,1)S(1)}, bf16[64,2048]{1,0:T(8,128)(2,1)S(1)}, u32[]{:S(2)}, u32[]{:S(2)}) %collective-permute-start.20) | collective-permute-done | bytes 262176 | tf_op jit(solution)/shard_map/ppermute | solution.py:247
  128.9 1.3 shard_map.58.refs_5_
  130.2 1.4 %shard_map.59.refs_1_ = bf16[1024,2048]{1,0:T(8,128)(2,1)} custom-call(bf16[128,2048]{1,0:T(8,128)(2,1)S(1)} %add_convert_fusion.refs_0_, bf16[128,2048]{1,0:T(8,128)(2,1)S(1)} %collective-permute-done.23.refs_1_, bf16[96,2048]{1,0:T(8,128)(2,1)S(1)} %add_convert_fusion.1.refs_2_, ...), custom_call_target="tpu_custom_call", output_to_operand_aliasing={{}: (5, {})} | custom-call | bytes 4194304 | tf_op jit(solution)/shard_map/pallas_call | solution.py:515
  (71 shorter events, 20.0 us)
Async XLA Ops:
  0.0 74.9 %collective-permute-start.19 = (bf16[1,1024,2048]{2,1,0:T(8,128)(2,1)}, bf16[1,1024,2048]{2,1,0:T(8,128)(2,1)S(1)}, u32[]{:S(2)}, u32[]{:S(2)}) collective-permute-start(bf16[1,1024,2048]{2,1,0:T(8,128)(2,1)} %refs_13_.1), channel_id=1, source_target_pairs={{0,8},{8,0},{16,24},{24,16},{1,9},{9,1},{17,25},{25,17},{2,10},{10... | collective-permute-start | bytes 12582920 | tf_op jit(solution)/shard_map/ppermute | solution.py:247
  13.0 5.3 %collective-permute-start.1 = (bf16[1,64,512]{2,1,0:T(8,128)(2,1)S(1)}, bf16[1,64,512]{2,1,0:T(8,128)(2,1)S(1)}, u32[]{:S(2)}, u32[]{:S(2)}) collective-permute-start(bf16[1,64,512]{2,1,0:T(8,128)(2,1)S(1)} %get-tuple-element.21), channel_id=1, source_target_pairs={{0,1},{1,0},{2,3},{3,2},{4,5},{5,4},{6,7},{7,6},{8,9},{9,8},{10,11... | collective-permute-start | bytes 196616 | tf_op jit(solution)/shard_map/ppermute | solution.py:247
  15.5 10.0 %collective-permute-start.30 = (s32[1]{0:T(128)}, s32[1]{0:T(128)}, u32[]{:S(2)}, u32[]{:S(2)}) collective-permute-start(s32[1]{0:T(128)} %param.9), channel_id=1, source_target_pairs={{0,16},{8,24},{16,0},{24,8},{1,17},{9,25},{17,1},{25,9},{2,18},{10... | collective-permute-start | bytes 20 | tf_op jit(solution)/shard_map/ppermute | solution.py:247
  17.0 6.7 %collective-permute-start = (bf16[3,64,512]{2,1,0:T(8,128)(2,1)S(1)}, bf16[3,64,512]{2,1,0:T(8,128)(2,1)S(1)}, u32[]{:S(2)}, u32[]{:S(2)}) collective-permute-start(bf16[3,64,512]{2,1,0:T(8,128)(2,1)S(1)} %get-tuple-element.19), channel_id=1, source_target_pairs={{0,1},{1,0},{2,3},{3,2},{4,5},{5,4},{6,7},{7,6},{8,9},{9,8},{10,11... | collective-permute-start | bytes 589832 | tf_op jit(solution)/shard_map/ppermute | solution.py:247
  17.5 55.0 %collective-permute-start.18 = (bf16[2048,512]{1,0:T(8,128)(2,1)S(1)}, bf16[2048,512]{1,0:T(8,128)(2,1)S(1)}, u32[]{:S(2)}, u32[]{:S(2)}) collective-permute-start(bf16[2048,512]{1,0:T(8,128)(2,1)S(1)} %get-tuple-element.22.refs_12_.refs_4_.refs_9_), channel_id=1, source_target_pairs={{0,8},{8,0},{16,24},{24,16},{1,9},{9,1},{17,25},{25,17},{2,10},{10... | collective-permute-start | bytes 6291464 | tf_op jit(solution)/shard_map/ppermute | solution.py:247
  18.3 11.0 %collective-permute-start.2 = (bf16[64,512]{1,0:T(8,128)(2,1)S(1)}, bf16[64,512]{1,0:T(8,128)(2,1)S(1)}, u32[]{:S(2)}, u32[]{:S(2)}) collective-permute-start(bf16[64,512]{1,0:T(8,128)(2,1)S(1)} %fusion.3), channel_id=1, source_target_pairs={{0,4},{2,6},{4,0},{6,2},{1,5},{3,7},{5,1},{7,3},{8,12},{10,14},{12... | collective-permute-start | bytes 196616 | tf_op jit(solution)/shard_map/ppermute | solution.py:247
  23.8 5.5 %collective-permute-start.3 = (bf16[64,512]{1,0:T(8,128)(2,1)S(1)}, bf16[64,512]{1,0:T(8,128)(2,1)S(1)}, u32[]{:S(2)}, u32[]{:S(2)}) collective-permute-start(bf16[64,512]{1,0:T(8,128)(2,1)S(1)} %get-tuple-element.31), channel_id=1, source_target_pairs={{0,2},{2,0},{4,6},{6,4},{1,3},{3,1},{5,7},{7,5},{8,10},{10,8},{12,... | collective-permute-start | bytes 196616 | tf_op jit(solution)/shard_map/ppermute | solution.py:247
  25.5 6.1 %collective-permute-start.4 = (bf16[64,512]{1,0:T(8,128)(2,1)S(1)}, bf16[64,512]{1,0:T(8,128)(2,1)S(1)}, u32[]{:S(2)}, u32[]{:S(2)}) collective-permute-start(bf16[64,512]{1,0:T(8,128)(2,1)S(1)} %get-tuple-element.32), channel_id=1, source_target_pairs={{0,6},{2,4},{4,2},{6,0},{1,7},{3,5},{5,3},{7,1},{8,14},{10,12},{12... | collective-permute-start | bytes 196616 | tf_op jit(solution)/shard_map/ppermute | solution.py:247
  29.3 75.0 %collective-permute-start.32 = (bf16[2048,512]{1,0:T(8,128)(2,1)S(1)}, bf16[2048,512]{1,0:T(8,128)(2,1)S(1)}, u32[]{:S(2)}, u32[]{:S(2)}) collective-permute-start(bf16[2048,512]{1,0:T(8,128)(2,1)S(1)} %col_table.1.refs_11_), channel_id=1, source_target_pairs={{0,8},{8,0},{16,24},{24,16},{1,9},{9,1},{17,25},{25,17},{2,10},{10... | collective-permute-start | bytes 6291464 | tf_op jit(solution)/shard_map/ppermute | solution.py:247
  31.6 5.7 %collective-permute-start.5 = (bf16[64,512]{1,0:T(8,128)(2,1)S(1)}, bf16[64,512]{1,0:T(8,128)(2,1)S(1)}, u32[]{:S(2)}, u32[]{:S(2)}) collective-permute-start(bf16[64,512]{1,0:T(8,128)(2,1)S(1)} %fusion.2), channel_id=1, source_target_pairs={{0,2},{2,0},{4,6},{6,4},{1,3},{3,1},{5,7},{7,5},{8,10},{10,8},{12,... | collective-permute-start | bytes 196616 | tf_op jit(solution)/shard_map/ppermute | solution.py:247
  31.7 1.8 %collective-permute-start.17 = (s32[1]{0:T(128)}, s32[1]{0:T(128)}, u32[]{:S(2)}, u32[]{:S(2)}) collective-permute-start(s32[1]{0:T(128)} %param.9), channel_id=1, source_target_pairs={{0,8},{8,0},{16,24},{24,16},{1,9},{9,1},{17,25},{25,17},{2,10},{10... | collective-permute-start | bytes 20 | tf_op jit(solution)/shard_map/ppermute | solution.py:247
  34.9 8.6 %collective-permute-start.6 = (bf16[64,512]{1,0:T(8,128)(2,1)S(1)}, bf16[64,512]{1,0:T(8,128)(2,1)S(1)}, u32[]{:S(2)}, u32[]{:S(2)}) collective-permute-start(bf16[64,512]{1,0:T(8,128)(2,1)S(1)} %fusion.2), channel_id=1, source_target_pairs={{0,4},{2,6},{4,0},{6,2},{1,5},{3,7},{5,1},{7,3},{8,12},{10,14},{12... | collective-permute-start | bytes 196616 | tf_op jit(solution)/shard_map/ppermute | solution.py:247
  37.3 6.7 %collective-permute-start.7 = (bf16[64,512]{1,0:T(8,128)(2,1)S(1)}, bf16[64,512]{1,0:T(8,128)(2,1)S(1)}, u32[]{:S(2)}, u32[]{:S(2)}) collective-permute-start(bf16[64,512]{1,0:T(8,128)(2,1)S(1)} %fusion.2), channel_id=1, source_target_pairs={{0,6},{2,4},{4,2},{6,0},{1,7},{3,5},{5,3},{7,1},{8,14},{10,12},{12... | collective-permute-start | bytes 196616 | tf_op jit(solution)/shard_map/ppermute | solution.py:247
  43.5 4.3 %collective-permute-start.8 = (bf16[64,512]{1,0:T(8,128)(2,1)S(1)}, bf16[64,512]{1,0:T(8,128)(2,1)S(1)}, u32[]{:S(2)}, u32[]{:S(2)}) collective-permute-start(bf16[64,512]{1,0:T(8,128)(2,1)S(1)} %fusion.2), channel_id=1, source_target_pairs={{0,1},{1,0},{2,3},{3,2},{4,5},{5,4},{6,7},{7,6},{8,9},{9,8},{10,11... | collective-permute-start | bytes 196616 | tf_op jit(solution)/shard_map/ppermute | solution.py:247
  44.0 5.0 %collective-permute-start.9 = (bf16[64,512]{1,0:T(8,128)(2,1)S(1)}, bf16[64,512]{1,0:T(8,128)(2,1)S(1)}, u32[]{:S(2)}, u32[]{:S(2)}) collective-permute-start(bf16[64,512]{1,0:T(8,128)(2,1)S(1)} %collective-permute-done.5), channel_id=1, source_target_pairs={{0,1},{1,0},{2,3},{3,2},{4,5},{5,4},{6,7},{7,6},{8,9},{9,8},{10,11... | collective-permute-start | bytes 196616 | tf_op jit(solution)/shard_map/ppermute | solution.py:247
  47.8 4.3 %collective-permute-start.10 = (bf16[64,512]{1,0:T(8,128)(2,1)S(1)}, bf16[64,512]{1,0:T(8,128)(2,1)S(1)}, u32[]{:S(2)}, u32[]{:S(2)}) collective-permute-start(bf16[64,512]{1,0:T(8,128)(2,1)S(1)} %collective-permute-done.6), channel_id=1, source_target_pairs={{0,1},{1,0},{2,3},{3,2},{4,5},{5,4},{6,7},{7,6},{8,9},{9,8},{10,11... | collective-permute-start | bytes 196616 | tf_op jit(solution)/shard_map/ppermute | solution.py:247
  49.0 4.3 %collective-permute-start.11 = (bf16[64,512]{1,0:T(8,128)(2,1)S(1)}, bf16[64,512]{1,0:T(8,128)(2,1)S(1)}, u32[]{:S(2)}, u32[]{:S(2)}) collective-permute-start(bf16[64,512]{1,0:T(8,128)(2,1)S(1)} %collective-permute-done.7), channel_id=1, source_target_pairs={{0,1},{1,0},{2,3},{3,2},{4,5},{5,4},{6,7},{7,6},{8,9},{9,8},{10,11... | collective-permute-start | bytes 196616 | tf_op jit(solution)/shard_map/ppermute | solution.py:247
  54.7 2.0 %collective-permute-start.12 = (bf16[256,512]{1,0:T(8,128)(2,1)S(1)}, bf16[256,512]{1,0:T(8,128)(2,1)S(1)}, u32[]{:S(2)}, u32[]{:S(2)}) collective-permute-start(bf16[256,512]{1,0:T(8,128)(2,1)S(1)} %pad_maximum_fusion.refs_1_), channel_id=1, source_target_pairs={{0,8},{8,0},{16,24},{24,16},{1,9},{9,1},{17,25},{25,17},{2,10},{10... | collective-permute-start | bytes 786440 | tf_op jit(solution)/shard_map/ppermute | solution.py:247
  55.7 9.2 %collective-permute-start.26 = (bf16[256,512]{1,0:T(8,128)(2,1)S(1)}, bf16[256,512]{1,0:T(8,128)(2,1)S(1)}, u32[]{:S(2)}, u32[]{:S(2)}) collective-permute-start(bf16[256,512]{1,0:T(8,128)(2,1)S(1)} %pad_maximum_fusion.refs_1_), channel_id=1, source_target_pairs={{0,16},{8,24},{16,0},{24,8},{1,17},{9,25},{17,1},{25,9},{2,18},{10... | collective-permute-start | bytes 786440 | tf_op jit(solution)/shard_map/ppermute | solution.py:247
  56.7 28.7 %collective-permute-start.34 = (bf16[224,2048]{1,0:T(8,128)(2,1)S(1)}, bf16[224,2048]{1,0:T(8,128)(2,1)S(1)}, u32[]{:S(2)}, u32[]{:S(2)}) collective-permute-start(bf16[224,2048]{1,0:T(8,128)(2,1)S(1)} %get-tuple-element.28), channel_id=1, source_target_pairs={{0,24},{8,16},{16,8},{24,0},{1,25},{9,17},{17,9},{25,1},{2,26},{10... | collective-permute-start | bytes 2752520 | tf_op jit(solution)/shard_map/ppermute | solution.py:247
  64.9 6.7 %collective-permute-start.27 = (bf16[256,512]{1,0:T(8,128)(2,1)S(1)}, bf16[256,512]{1,0:T(8,128)(2,1)S(1)}, u32[]{:S(2)}, u32[]{:S(2)}) collective-permute-start(bf16[256,512]{1,0:T(8,128)(2,1)S(1)} %collective-permute-done.26.refs_3_), channel_id=1, source_target_pairs={{0,1},{1,0},{2,3},{3,2},{4,5},{5,4},{6,7},{7,6},{8,9},{9,8},{10,11... | collective-permute-start | bytes 786440 | tf_op jit(solution)/shard_map/ppermute | solution.py:247
  71.6 32.6 %collective-permute-start.33 = (bf16[224,2048]{1,0:T(8,128)(2,1)S(1)}, bf16[224,2048]{1,0:T(8,128)(2,1)S(1)}, u32[]{:S(2)}, u32[]{:S(2)}) collective-permute-start(bf16[224,2048]{1,0:T(8,128)(2,1)S(1)} %own_slice.1), channel_id=1, source_target_pairs={{0,16},{8,24},{16,0},{24,8},{1,17},{9,25},{17,1},{25,9},{2,18},{10... | collective-permute-start | bytes 2752520 | tf_op jit(solution)/shard_map/ppermute | solution.py:247
  72.6 8.7 %collective-permute-start.28 = (bf16[256,512]{1,0:T(8,128)(2,1)S(1)}, bf16[256,512]{1,0:T(8,128)(2,1)S(1)}, u32[]{:S(2)}, u32[]{:S(2)}) collective-permute-start(bf16[256,512]{1,0:T(8,128)(2,1)S(1)} %collective-permute-done.26.refs_3_), channel_id=1, source_target_pairs={{0,8},{8,0},{16,24},{24,16},{1,9},{9,1},{17,25},{25,17},{2,10},{10... | collective-permute-start | bytes 786440 | tf_op jit(solution)/shard_map/ppermute | solution.py:247
  74.9 29.3 %collective-permute-start.29 = (bf16[256,512]{1,0:T(8,128)(2,1)S(1)}, bf16[256,512]{1,0:T(8,128)(2,1)S(1)}, u32[]{:S(2)}, u32[]{:S(2)}) collective-permute-start(bf16[256,512]{1,0:T(8,128)(2,1)S(1)} %collective-permute-done.27.refs_4_), channel_id=1, source_target_pairs={{0,8},{8,0},{16,24},{24,16},{1,9},{9,1},{17,25},{25,17},{2,10},{10... | collective-permute-start | bytes 786440 | tf_op jit(solution)/shard_map/ppermute | solution.py:247
  81.3 31.4 %collective-permute-start.24 = (bf16[96,2048]{1,0:T(8,128)(2,1)S(1)}, bf16[96,2048]{1,0:T(8,128)(2,1)S(1)}, u32[]{:S(2)}, u32[]{:S(2)}) collective-permute-start(bf16[96,2048]{1,0:T(8,128)(2,1)S(1)} %get-tuple-element.27), channel_id=1, source_target_pairs={{0,16},{8,24},{16,0},{24,8},{1,17},{9,25},{17,1},{25,9},{2,18},{10... | collective-permute-start | bytes 1179656 | tf_op jit(solution)/shard_map/ppermute | solution.py:247
  85.4 38.5 %collective-permute-start.22 = (bf16[128,2048]{1,0:T(8,128)(2,1)S(1)}, bf16[128,2048]{1,0:T(8,128)(2,1)S(1)}, u32[]{:S(2)}, u32[]{:S(2)}) collective-permute-start(bf16[128,2048]{1,0:T(8,128)(2,1)S(1)} %get-tuple-element.26), channel_id=1, source_target_pairs={{0,16},{8,24},{16,0},{24,8},{1,17},{9,25},{17,1},{25,9},{2,18},{10... | collective-permute-start | bytes 1572872 | tf_op jit(solution)/shard_map/ppermute | solution.py:247
  109.5 19.3 %collective-permute-start.35 = (bf16[128,2048]{1,0:T(8,128)(2,1)S(1)}, bf16[128,2048]{1,0:T(8,128)(2,1)S(1)}, u32[]{:S(2)}, u32[]{:S(2)}) collective-permute-start(bf16[128,2048]{1,0:T(8,128)(2,1)S(1)} %get-tuple-element.29.refs_0_), channel_id=1, source_target_pairs={{0,8},{8,0},{16,24},{24,16},{1,9},{9,1},{17,25},{25,17},{2,10},{10... | collective-permute-start | bytes 1572872 | tf_op jit(solution)/shard_map/ppermute | solution.py:247
  109.6 19.3 %collective-permute-start.36 = (bf16[96,2048]{1,0:T(8,128)(2,1)S(1)}, bf16[96,2048]{1,0:T(8,128)(2,1)S(1)}, u32[]{:S(2)}, u32[]{:S(2)}) collective-permute-start(bf16[96,2048]{1,0:T(8,128)(2,1)S(1)} %get-tuple-element.30.refs_2_), channel_id=1, source_target_pairs={{0,8},{8,0},{16,24},{24,16},{1,9},{9,1},{17,25},{25,17},{2,10},{10... | collective-permute-start | bytes 1179656 | tf_op jit(solution)/shard_map/ppermute | solution.py:247
  110.1 18.6 %collective-permute-start.20 = (bf16[64,2048]{1,0:T(8,128)(2,1)S(1)}, bf16[64,2048]{1,0:T(8,128)(2,1)S(1)}, u32[]{:S(2)}, u32[]{:S(2)}) collective-permute-start(bf16[64,2048]{1,0:T(8,128)(2,1)S(1)} %get-tuple-element.25), channel_id=1, source_target_pairs={{0,16},{8,24},{16,0},{24,8},{1,17},{9,25},{17,1},{25,9},{2,18},{10... | collective-permute-start | bytes 786440 | tf_op jit(solution)/shard_map/ppermute | solution.py:247
  112.8 17.4 %collective-permute-start.25 = (bf16[96,2048]{1,0:T(8,128)(2,1)S(1)}, bf16[96,2048]{1,0:T(8,128)(2,1)S(1)}, u32[]{:S(2)}, u32[]{:S(2)}) collective-permute-start(bf16[96,2048]{1,0:T(8,128)(2,1)S(1)} %add_convert_fusion.1.refs_2_), channel_id=1, source_target_pairs={{0,8},{8,0},{16,24},{24,16},{1,9},{9,1},{17,25},{25,17},{2,10},{10... | collective-permute-start | bytes 1179656 | tf_op jit(solution)/shard_map/ppermute | solution.py:247
  124.0 6.1 %collective-permute-start.23 = (bf16[128,2048]{1,0:T(8,128)(2,1)S(1)}, bf16[128,2048]{1,0:T(8,128)(2,1)S(1)}, u32[]{:S(2)}, u32[]{:S(2)}) collective-permute-start(bf16[128,2048]{1,0:T(8,128)(2,1)S(1)} %add_convert_fusion.refs_0_), channel_id=1, source_target_pairs={{0,8},{8,0},{16,24},{24,16},{1,9},{9,1},{17,25},{25,17},{2,10},{10... | collective-permute-start | bytes 1572872 | tf_op jit(solution)/shard_map/ppermute | solution.py:247
  128.8 2.8 %collective-permute-start.21 = (bf16[64,2048]{1,0:T(8,128)(2,1)S(1)}, bf16[64,2048]{1,0:T(8,128)(2,1)S(1)}, u32[]{:S(2)}, u32[]{:S(2)}) collective-permute-start(bf16[64,2048]{1,0:T(8,128)(2,1)S(1)} %add_convert_fusion.2.refs_4_), channel_id=1, source_target_pairs={{0,8},{8,0},{16,24},{24,16},{1,9},{9,1},{17,25},{25,17},{2,10},{10... | collective-permute-start | bytes 786440 | tf_op jit(solution)/shard_map/ppermute | solution.py:247
  (9 other events, 48.1 us)
